TPU v7x, 32 devices: a whole 2x2x4 slice. The times are simulated.
32 devices in a mesh: ctx: 8 (over z, y), wsh: 4 (over x, core).
Axes of the slice: x: 2, y: 2, z: 4, core: 2. Of those that a mesh axis runs over, the one named last changes fastest.
Arguments:
- tokens: bfloat16 [4, 1024, 768], P('wsh', 'ctx'), may hold values from -6 to 6
- teacher: bfloat16 [4, 1024, 768], P('wsh', 'ctx'), may hold values from -6 to 6
- doc_lengths: int32 [4, 8], P('wsh'), may hold values from 1 to 512, 1024 in all within a row
- valid_len: int32 [4], P('wsh'), may hold values from 512 to 1024
- q_weight: bfloat16 [768, 768], P('wsh'), may hold values from -0.21875 to 0.21875
- q_bias: bfloat16 [768], P('wsh'), may hold values from -3 to 3
- k_weight: bfloat16 [768, 768], P('wsh'), may hold values from -0.21875 to 0.21875
- v_weight: bfloat16 [768, 768], P('wsh'), may hold values from -0.21875 to 0.21875
- v_bias: bfloat16 [768], P('wsh'), may hold values from -0.29882812 to 0.29882812
- o_weight: bfloat16 [768, 768], P('wsh'), may hold values from -1.25 to 1.25
- o_bias: bfloat16 [768], P('wsh'), may hold values from -3 to 3
- ln1_gain: bfloat16 [768], P('wsh'), may hold values from 0.25 to 1.75
- ln1_bias: bfloat16 [768], P('wsh'), may hold values from -3 to 3
- in_weight: bfloat16 [768, 3072], P('wsh'), may hold values from -0.21875 to 0.21875
- in_bias: bfloat16 [3072], P('wsh'), may hold values from -3 to 3
- out_weight: bfloat16 [3072, 768], P('wsh'), may hold values from -0.109375 to 0.109375
- out_bias: bfloat16 [768], P('wsh'), may hold values from -3 to 3
- ln2_gain: bfloat16 [768], P('wsh'), may hold values from 0.25 to 1.75
- ln2_bias: bfloat16 [768], P('wsh'), may hold values from -3 to 3
Outputs:
- output: bfloat16 [4, 1024, 768], P('wsh', 'ctx')
- loss: float32 [], replicated
- input_grad: float32 [4, 1024, 768], P('wsh', 'ctx')
- q_weight_grad: float32 [768, 768], P('wsh')
- q_bias_grad: float32 [768], P('wsh')
- k_weight_grad: float32 [768, 768], P('wsh')
- v_weight_grad: float32 [768, 768], P('wsh')
- v_bias_grad: float32 [768], P('wsh')
- o_weight_grad: float32 [768, 768], P('wsh')
- o_bias_grad: float32 [768], P('wsh')
- ln1_gain_grad: float32 [768], P('wsh')
- ln1_bias_grad: float32 [768], P('wsh')
- in_weight_grad: float32 [768, 3072], P('wsh')
- in_bias_grad: float32 [3072], P('wsh')
- out_weight_grad: float32 [3072, 768], P('wsh')
- out_bias_grad: float32 [768], P('wsh')
- ln2_gain_grad: float32 [768], P('wsh')
- ln2_bias_grad: float32 [768], P('wsh')
Inputs may be any that keep to these rules, and one draw needn't show every extreme that they name: `doc_lengths`: row s lists, in order, the lengths of the documents that fill stream s; they sum to 1024 and the longest is exactly 512.
All inputs are finite; a program needn't handle non-finite values.
Results may differ from a plain program's by a relative error of at most 0.017.
Values may be sent and summed in bfloat16 or wider, within the bound.
A program may use at most 128 MiB of HBM per device.

v0:
```python
import math

import jax
import jax.numpy as jnp
from jax import lax
from jax.sharding import PartitionSpec as P

D = 768
H = 12
HD = 64


EPSILON = 1e-06
MASKED = -1e30


def shifted(block, axis, distance):
    devices = range(lax.axis_size(axis))
    route = [((i - distance) % len(devices), i) for i in devices]
    return lax.ppermute(block, axis, route)


def layer_norm(value, gain, shift):
    mean = jnp.mean(value, axis=-1, keepdims=True)
    centered = value - mean
    spread = jnp.mean(centered * centered, axis=-1, keepdims=True)
    return centered * lax.rsqrt(spread + EPSILON) * gain + shift


def activate(value):
    return jax.nn.gelu(value, approximate=True)


def matmul(left, right):
    return jnp.dot(left, right, preferred_element_type=jnp.float32)


def left_product(left, right):
    return lax.dot_general(
        left, right, (((0,), (0,)), ((), ())), preferred_element_type=jnp.float32
    )


def right_product(left, right):
    return lax.dot_general(
        left, right, (((1,), (1,)), ((), ())), preferred_element_type=jnp.float32
    )


def document_of(positions, starts):
    return jnp.sum((starts[None, :] <= positions[:, None]).astype(jnp.int32), axis=1) - 1


def permitted(own_doc, own_live, other_doc, other_live):
    return (own_doc[:, None] == other_doc[None, :]) & (own_live[:, None] == other_live[None, :])


def block_weights(queries, key_block, allowed, score_scale):
    scores = (
        jnp.einsum("qhd,khd->hqk", queries, key_block, preferred_element_type=jnp.float32)
        * score_scale
    )
    return jnp.exp(jnp.where(allowed[None], scores, MASKED))


def forward_visit(sums_state, queries, key_block, value_block, allowed, score_scale):
    row_total, weighted = sums_state
    weights = block_weights(queries, key_block, allowed, score_scale)
    row_total = row_total + jnp.sum(weights, axis=-1)
    weighted = weighted + jnp.einsum(
        "hqk,khd->qhd",
        weights.astype(jnp.bfloat16),
        value_block,
        preferred_element_type=jnp.float32,
    )
    return (row_total, weighted)


def backward_visit(
    queries, key_block, value_block, allowed, score_scale, weighted_grad, total_grad
):
    weights = block_weights(queries, key_block, allowed, score_scale)
    value_part = jnp.einsum(
        "hqk,qhd->khd",
        weights.astype(jnp.bfloat16),
        weighted_grad,
        preferred_element_type=jnp.float32,
    )
    weight_grad = (
        jnp.einsum("qhd,khd->hqk", weighted_grad, value_block, preferred_element_type=jnp.float32)
        + total_grad[:, :, None]
    )
    score_grad = (weights * weight_grad).astype(jnp.bfloat16)
    query_part = (
        jnp.einsum("hqk,khd->qhd", score_grad, key_block, preferred_element_type=jnp.float32)
        * score_scale
    )
    key_part = (
        jnp.einsum("hqk,qhd->khd", score_grad, queries, preferred_element_type=jnp.float32)
        * score_scale
    )
    return (query_part, key_part, value_part)


def body(
    tokens,
    teacher,
    doc_lengths,
    valid_len,
    q_weight,
    q_bias,
    k_weight,
    v_weight,
    v_bias,
    o_weight,
    o_bias,
    ln1_gain,
    ln1_bias,
    in_weight,
    in_bias,
    out_weight,
    out_bias,
    ln2_gain,
    ln2_bias,
):
    gathered = (
        lax.all_gather(q_weight, "wsh", axis=0, tiled=True),
        lax.all_gather(q_bias, "wsh", axis=0, tiled=True),
        lax.all_gather(k_weight, "wsh", axis=0, tiled=True),
        lax.all_gather(v_weight, "wsh", axis=0, tiled=True),
        lax.all_gather(v_bias, "wsh", axis=0, tiled=True),
        lax.all_gather(o_weight, "wsh", axis=0, tiled=True),
        lax.all_gather(o_bias, "wsh", axis=0, tiled=True),
        lax.all_gather(ln1_gain, "wsh", axis=0, tiled=True),
        lax.all_gather(ln1_bias, "wsh", axis=0, tiled=True),
        lax.all_gather(in_weight, "wsh", axis=0, tiled=True),
        lax.all_gather(in_bias, "wsh", axis=0, tiled=True),
        lax.all_gather(out_weight, "wsh", axis=0, tiled=True),
        lax.all_gather(out_bias, "wsh", axis=0, tiled=True),
        lax.all_gather(ln2_gain, "wsh", axis=0, tiled=True),
        lax.all_gather(ln2_bias, "wsh", axis=0, tiled=True),
    )
    (
        w_query,
        b_query,
        w_key,
        w_value,
        b_value,
        w_out,
        b_out,
        gain_one,
        shift_one,
        w_inner,
        b_inner,
        w_back,
        b_back,
        gain_two,
        shift_two,
    ) = gathered
    gain_first = gain_one.astype(jnp.float32)
    shift_first = shift_one.astype(jnp.float32)
    gain_second = gain_two.astype(jnp.float32)
    shift_second = shift_two.astype(jnp.float32)
    inputs = tokens[0]
    row_count = inputs.shape[0]
    cycle_size = lax.axis_size("ctx")
    stream_count = lax.axis_size("wsh")
    position = lax.axis_index("ctx")
    score_scale = 1.0 / math.sqrt(HD)
    offsets = jnp.arange(row_count, dtype=jnp.int32)
    lengths = doc_lengths[0]
    starts = jnp.cumsum(lengths) - lengths
    limit = valid_len[0]

    def key_mask(block_index):
        where_rows = jnp.mod(block_index, cycle_size) * row_count + offsets
        return (document_of(where_rows, starts), where_rows < limit)

    own_doc, own_live = key_mask(position)
    input_float = inputs.astype(jnp.float32)
    queries = (
        (matmul(inputs, w_query) + b_query.astype(jnp.float32))
        .astype(jnp.bfloat16)
        .reshape(row_count, H, HD)
    )
    key_rows = matmul(inputs, w_key).astype(jnp.bfloat16).reshape(row_count, H, HD)
    value_rows = (
        (matmul(inputs, w_value) + b_value.astype(jnp.float32))
        .astype(jnp.bfloat16)
        .reshape(row_count, H, HD)
    )

    def visit_forward(sums_state, key_block, value_block, block_index):
        other_doc, other_live = key_mask(block_index)
        allowed = permitted(own_doc, own_live, other_doc, other_live)
        return forward_visit(sums_state, queries, key_block, value_block, allowed, score_scale)

    empty_state = (
        jnp.zeros((H, row_count), jnp.float32),
        jnp.zeros((row_count, H, HD), jnp.float32),
    )
    first_state = visit_forward(empty_state, key_rows, value_rows, position)

    def advance(step_index, loop_state):
        key_block, value_block, running = loop_state
        key_block, value_block = shifted((key_block, value_block), "ctx", 1)
        running = visit_forward(running, key_block, value_block, position - step_index)
        return (key_block, value_block, running)

    row_total, weighted = lax.fori_loop(
        1, cycle_size, advance, (key_rows, value_rows, first_state)
    )[2]
    normed = weighted / jnp.transpose(row_total)[:, :, None]
    context = normed.astype(jnp.bfloat16).reshape(row_count, D)
    attn = matmul(context, w_out) + b_out.astype(jnp.float32)
    first_sum = input_float + attn
    settled = layer_norm(first_sum, gain_first, shift_first)
    settled_low = settled.astype(jnp.bfloat16)
    inner = matmul(settled_low, w_inner) + b_inner.astype(jnp.float32)
    activated = activate(inner).astype(jnp.bfloat16)
    branch = matmul(activated, w_back) + b_back.astype(jnp.float32)
    second_sum = settled + branch
    result = layer_norm(second_sum, gain_second, shift_second)
    target = teacher[0].astype(jnp.float32)
    diff = jnp.where(own_live[:, None], result - target, 0.0)
    error_sum, live_count = lax.psum(
        (jnp.sum(diff * diff), jnp.sum(own_live.astype(jnp.float32))), ("ctx", "wsh")
    )
    loss = error_sum / (live_count * D)
    upstream = diff * (row_count * cycle_size * stream_count / live_count)
    unused_second, second_back = jax.vjp(layer_norm, second_sum, gain_second, shift_second)
    d_second, gain_two_grad, shift_two_grad = second_back(upstream)
    branch_grad = d_second.astype(jnp.bfloat16)
    back_weight_grad = left_product(activated, branch_grad)
    back_bias_grad = jnp.sum(branch_grad, axis=0, dtype=jnp.float32)
    d_activated = right_product(branch_grad, w_back)
    unused_inner, gelu_back = jax.vjp(activate, inner)
    inner_grad = gelu_back(d_activated)[0].astype(jnp.bfloat16)
    inner_weight_grad = left_product(settled_low, inner_grad)
    inner_bias_grad = jnp.sum(inner_grad, axis=0, dtype=jnp.float32)
    d_settled = d_second + right_product(inner_grad, w_inner)
    unused_first, first_back = jax.vjp(layer_norm, first_sum, gain_first, shift_first)
    d_first, gain_one_grad, shift_one_grad = first_back(d_settled)
    attn_grad = d_first.astype(jnp.bfloat16)
    out_weight_grad_local = left_product(context, attn_grad)
    out_bias_grad_local = jnp.sum(attn_grad, axis=0, dtype=jnp.float32)
    context_low = lax.optimization_barrier(right_product(attn_grad, w_out).astype(jnp.bfloat16))
    context_grad = context_low.astype(jnp.float32).reshape(row_count, H, HD)
    weighted_grad = (context_grad / jnp.transpose(row_total)[:, :, None]).astype(jnp.bfloat16)
    total_grad = -jnp.transpose(jnp.sum(context_grad * weighted, axis=-1)) / (row_total * row_total)

    def visit_backward(key_block, value_block, block_index):
        other_doc, other_live = key_mask(block_index)
        allowed = permitted(own_doc, own_live, other_doc, other_live)
        return backward_visit(
            queries, key_block, value_block, allowed, score_scale, weighted_grad, total_grad
        )

    query_sum, key_sum, value_sum = visit_backward(key_rows, value_rows, position)

    def advance_back(step_index, loop_state):
        key_block, value_block, query_acc, key_acc, value_acc = loop_state
        key_block, value_block = shifted((key_block, value_block), "ctx", 1)
        key_acc, value_acc = (
            shifted(key_acc.astype(jnp.bfloat16), "ctx", 1).astype(key_acc.dtype),
            shifted(value_acc.astype(jnp.bfloat16), "ctx", 1).astype(value_acc.dtype),
        )
        query_part, key_part, value_part = visit_backward(
            key_block, value_block, position - step_index
        )
        return (
            key_block,
            value_block,
            query_acc + query_part,
            key_acc + key_part,
            value_acc + value_part,
        )

    loop_state = lax.fori_loop(
        1, cycle_size, advance_back, (key_rows, value_rows, query_sum, key_sum, value_sum)
    )
    query_total = loop_state[2]
    key_total, value_total = (
        shifted(loop_state[3].astype(jnp.bfloat16), "ctx", 1).astype(jnp.float32),
        shifted(loop_state[4].astype(jnp.bfloat16), "ctx", 1).astype(jnp.float32),
    )
    query_grad = query_total.astype(jnp.bfloat16).reshape(row_count, D)
    key_grad = key_total.astype(jnp.bfloat16).reshape(row_count, D)
    value_grad = value_total.astype(jnp.bfloat16).reshape(row_count, D)
    query_weight_grad = left_product(inputs, query_grad)
    query_bias_grad = jnp.sum(query_grad, axis=0, dtype=jnp.float32)
    key_weight_grad = left_product(inputs, key_grad)
    value_weight_grad = left_product(inputs, value_grad)
    value_bias_grad = jnp.sum(value_grad, axis=0, dtype=jnp.float32)
    input_grad = (
        d_first
        + right_product(query_grad, w_query)
        + right_product(key_grad, w_key)
        + right_product(value_grad, w_value)
    )
    reduced = (
        lax.psum_scatter(
            query_weight_grad.astype(jnp.bfloat16), "wsh", scatter_dimension=0, tiled=True
        ).astype(jnp.float32),
        lax.psum_scatter(
            query_bias_grad.astype(jnp.bfloat16), "wsh", scatter_dimension=0, tiled=True
        ).astype(jnp.float32),
        lax.psum_scatter(
            key_weight_grad.astype(jnp.bfloat16), "wsh", scatter_dimension=0, tiled=True
        ).astype(jnp.float32),
        lax.psum_scatter(
            value_weight_grad.astype(jnp.bfloat16), "wsh", scatter_dimension=0, tiled=True
        ).astype(jnp.float32),
        lax.psum_scatter(
            value_bias_grad.astype(jnp.bfloat16), "wsh", scatter_dimension=0, tiled=True
        ).astype(jnp.float32),
        lax.psum_scatter(
            out_weight_grad_local.astype(jnp.bfloat16), "wsh", scatter_dimension=0, tiled=True
        ).astype(jnp.float32),
        lax.psum_scatter(
            out_bias_grad_local.astype(jnp.bfloat16), "wsh", scatter_dimension=0, tiled=True
        ).astype(jnp.float32),
        lax.psum_scatter(
            gain_one_grad.astype(jnp.bfloat16), "wsh", scatter_dimension=0, tiled=True
        ).astype(jnp.float32),
        lax.psum_scatter(
            shift_one_grad.astype(jnp.bfloat16), "wsh", scatter_dimension=0, tiled=True
        ).astype(jnp.float32),
        lax.psum_scatter(
            inner_weight_grad.astype(jnp.bfloat16), "wsh", scatter_dimension=0, tiled=True
        ).astype(jnp.float32),
        lax.psum_scatter(
            inner_bias_grad.astype(jnp.bfloat16), "wsh", scatter_dimension=0, tiled=True
        ).astype(jnp.float32),
        lax.psum_scatter(
            back_weight_grad.astype(jnp.bfloat16), "wsh", scatter_dimension=0, tiled=True
        ).astype(jnp.float32),
        lax.psum_scatter(
            back_bias_grad.astype(jnp.bfloat16), "wsh", scatter_dimension=0, tiled=True
        ).astype(jnp.float32),
        lax.psum_scatter(
            gain_two_grad.astype(jnp.bfloat16), "wsh", scatter_dimension=0, tiled=True
        ).astype(jnp.float32),
        lax.psum_scatter(
            shift_two_grad.astype(jnp.bfloat16), "wsh", scatter_dimension=0, tiled=True
        ).astype(jnp.float32),
    )
    summed = lax.psum(
        (
            reduced[0],
            reduced[1],
            reduced[2],
            reduced[3],
            reduced[4],
            reduced[5],
            reduced[6],
            reduced[7],
            reduced[8],
            reduced[9],
            reduced[10],
            reduced[11],
            reduced[12],
            reduced[13],
            reduced[14],
        ),
        "ctx",
    )
    return (
        result.astype(jnp.bfloat16)[None],
        loss,
        input_grad[None],
        summed[0],
        summed[1],
        summed[2],
        summed[3],
        summed[4],
        summed[5],
        summed[6],
        summed[7],
        summed[8],
        summed[9],
        summed[10],
        summed[11],
        summed[12],
        summed[13],
        summed[14],
    )


def solution(mesh):
    in_specs = (
        P("wsh", "ctx", None),
        P("wsh", "ctx", None),
        P("wsh", None),
        P("wsh"),
        P("wsh", None),
        P("wsh"),
        P("wsh", None),
        P("wsh", None),
        P("wsh"),
        P("wsh", None),
        P("wsh"),
        P("wsh"),
        P("wsh"),
        P("wsh", None),
        P("wsh"),
        P("wsh", None),
        P("wsh"),
        P("wsh"),
        P("wsh"),
    )
    out_specs = (
        P("wsh", "ctx", None),
        P(),
        P("wsh", "ctx", None),
        P("wsh", None),
        P("wsh"),
        P("wsh", None),
        P("wsh", None),
        P("wsh"),
        P("wsh", None),
        P("wsh"),
        P("wsh"),
        P("wsh"),
        P("wsh", None),
        P("wsh"),
        P("wsh", None),
        P("wsh"),
        P("wsh"),
        P("wsh"),
    )
    return jax.shard_map(body, mesh=mesh, in_specs=in_specs, out_specs=out_specs, check_vma=False)
```

profile of v0, /device:TPU:0, one launch (start us, length us, event | category | flops | bytes accessed | tf_op | source)
XLA Modules:
  0.0 860.1 jit_solution(9805982596595255451)
XLA Ops:
  12.8 42.2 %psum.120 = f32[]{:T(128)} all-reduce(f32[]{:T(128)} %get-tuple-element.990), channel_id=1, replica_groups=mesh['ctx'=8,'wsh'=4] {'ctx','wsh'}, use_global_device_ids=true, to_apply=%region_14.15 | all-reduce | flops 1 | bytes 8 | tf_op jit(solution)/shard_map/psum | solution.py:226
  58.1 10.8 %all-reduce.19 = (bf16[768]{0:T(1024)(128)(2,1)S(1)}, bf16[768]{0:T(1024)(128)(2,1)S(1)}, bf16[768]{0:T(1024)(128)(2,1)S(1)}, bf16[768]{0:T(1024)(128)(2,1)S(1)}...) all-reduce(bf16[768]{0:T(1024)(128)(2,1)S(1)} %dynamic-update-slice, ...), channel_id=1, replica_groups=mesh['ctx'=8,'wsh'=4] {'wsh'}, use_global_device_ids=true, to_apply=%add | all-reduce | flops 6144 | bytes 24576
  69.0 5.3 all-gather
  86.5 84.8 %while.48 = (s32[]{:T(128)}, bf16[128,12,64]{0,2,1:T(8,128)(2,1)S(1)}, bf16[128,12,64]{0,2,1:T(8,128)(2,1)S(1)}, f32[12,128]{1,0:T(8,128)S(1)}, f32[128,12,64]{0...) while((s32[]{:T(128)}, ...), condition=%wide.region_6.7_spmd.clone.clone, body=%wide.region_3.6_spmd.clone.clone.sunk | while | flops 51269264 | bytes 4583834 | solution.py:210
  86.7 2.2 collective-permute-start
  90.6 6.6 collective-permute-done
  97.6 3.2 collective-permute-done.1
  103.2 8.5 collective-permute-done
  112.1 2.2 collective-permute-done.1
  115.6 9.2 %collective-permute-done = bf16[128,12,64]{0,2,1:T(8,128)(2,1)S(1)} collective-permute-done((bf16[128,12,64]{0,2,1:T(8,128)(2,1)S(1)}, bf16[128,12,64]{0,2,1:T(8,128)(2,1)S(1)}, u32[]{:S(2)}, u32[]{:S(2)}) %collective-permute-start) | collective-permute-done | bytes 196640 | tf_op jit(solution)/shard_map/while/body/eval_jaxpr/ppermute | solution.py:20
  125.3 1.7 collective-permute-done.1
  128.3 8.3 collective-permute-done
  137.0 1.7 collective-permute-done.1
  140.0 7.4 collective-permute-done
  147.8 1.7 collective-permute-done.1
  150.8 7.4 collective-permute-done
  158.6 1.7 collective-permute-done.1
  161.6 7.4 collective-permute-done
  169.4 1.7 collective-permute-done.1
  171.5 1.8 fusion.69
  173.5 3.2 convolution_add_fusion.1
  176.8 3.6 fusion.70
  183.4 2.6 fusion.60
  185.9 2.4 multiply_reduce_fusion.1
  196.4 136.7 %while.49 = (s32[]{:T(128)}, bf16[128,12,64]{0,2,1:T(8,128)(2,1)}, bf16[128,12,64]{0,2,1:T(8,128)(2,1)}, f32[128,12,64]{0,2,1:T(8,128)S(1)}, bf16[128,12,64]{0,2...) while((s32[]{:T(128)}, bf16[128,12,64]{0,2,1:T(8,128)(2,1)}, ...), condition=%wide.region_22.23_spmd.clone.clone, body=%wide.region_20.22_spmd.clone.clone.sunk | while | flops 127946384 | bytes 10463746 | solution.py:279
  198.7 7.0 collective-permute-done.2
  210.0 1.8 convert_add_fusion.4
  216.9 5.8 collective-permute-done.2
  227.1 1.8 convert_add_fusion.4
  229.0 2.3 collective-permute-done.5
  234.6 6.2 collective-permute-done.2
  246.3 1.8 convert_add_fusion.4
  248.1 2.3 collective-permute-done.5
  253.6 6.3 collective-permute-done.2
  264.0 2.5 collective-permute-done.4
  266.5 1.8 convert_add_fusion.4
  268.3 2.3 collective-permute-done.5
  274.0 6.0 collective-permute-done.2
  280.7 2.7 collective-permute-done.3
  285.3 2.5 collective-permute-done.4
  287.7 1.8 convert_add_fusion.4
  289.6 2.3 collective-permute-done.5
  295.5 6.1 collective-permute-done.2
  302.3 3.5 collective-permute-done.3
  307.6 2.5 collective-permute-done.4
  310.1 1.8 convert_add_fusion.4
  312.0 2.3 collective-permute-done.5
  317.8 5.9 collective-permute-done.2
  328.2 1.8 convert_add_fusion.4
  330.0 2.1 collective-permute-done.5
  335.9 2.4 convolution_convert_fusion.2
  338.5 8.6 collective-permute-done.6
  348.2 1.7 copy.107
  350.0 8.4 collective-permute-done.7
  362.1 3.6 convolution_convert_fusion.1
  366.7 3.8 convolution_convert_fusion
  372.6 37.3 %psum.119 = f32[]{:T(128)} all-reduce(f32[]{:T(128)} %get-tuple-element.892), channel_id=1, replica_groups=mesh['ctx'=8,'wsh'=4] {'ctx','wsh'}, use_global_device_ids=true, to_apply=%region_12.13 | all-reduce | flops 1 | bytes 8 | tf_op jit(solution)/shard_map/psum | solution.py:226
  411.3 1.9 convolution_add_fusion.4
  413.5 11.7 %all-reduce.18 = (bf16[768]{0:T(1024)(128)(2,1)S(1)}, bf16[768]{0:T(1024)(128)(2,1)S(1)}, bf16[768]{0:T(1024)(128)(2,1)S(1)}, bf16[768]{0:T(1024)(128)(2,1)S(1)}...) all-reduce(bf16[768]{0:T(1024)(128)(2,1)S(1)} %copy-done.32, ...), channel_id=3, replica_groups=mesh['ctx'=8,'wsh'=4] {'wsh'}, use_global_device_ids=true, to_apply=%region_26.27.clone | all-reduce | flops 9216 | bytes 36864
  431.6 13.9 %reduce-scatter.23.cloned.1.call-done = bf16[192,768]{1,0:T(8,128)(2,1)} async-done(((bf16[768,768]{1,0:T(8,128)(2,1)}), bf16[192,768]{1,0:T(8,128)(2,1)}) %reduce-scatter.23.cloned.1.call-update) | async-done | bytes 294928
  446.7 49.3 %reduce-scatter.15.cloned.1.call-done = bf16[192,3072]{1,0:T(8,128)(2,1)} async-done(((bf16[768,3072]{1,0:T(8,128)(2,1)}), bf16[192,3072]{1,0:T(8,128)(2,1)}) %reduce-scatter.15.cloned.1.call-update) | async-done | bytes 1179664 | tf_op jit(solution)/shard_map/reduce_scatter | solution.py:329
  495.9 50.4 %reduce-scatter.17.cloned.1.call-done = bf16[768,768]{1,0:T(8,128)(2,1)} async-done(((bf16[3072,768]{1,0:T(8,128)(2,1)}), bf16[768,768]{1,0:T(8,128)(2,1)}) %reduce-scatter.17.cloned.1.call-update) | async-done | bytes 1179664 | tf_op jit(solution)/shard_map/reduce_scatter | solution.py:335
  546.4 301.5 %all-reduce.21 = (f32[192,768]{0,1:T(8,128)}, f32[192]{0:T(256)}, f32[192,768]{0,1:T(8,128)S(1)}, f32[192,768]{0,1:T(8,128)S(1)}, f32[192]{0:T(256)}, /*index=5*...) all-reduce(bf16[192,768]{0,1:T(8,128)(2,1)S(1)} %copy.106, ...), channel_id=1, replica_groups=mesh['ctx'=8,'wsh'=4] {'ctx'}, use_global_device_ids=true, to_apply=%region_24.25 | all-reduce | flops 1771776 | bytes 10635264 | tf_op jit(solution)/shard_map/psum | solution.py:348
  847.8 2.2 copy.96
  (432 shorter events, 115.4 us)
Async XLA Ops:
  7.2 68.1 %all-gather.8.cloned.1.call-start = ((), (), s32[]{:S(2)}) async-start(), calls=%async_computation.6 | async-start | bytes 1474560 | tf_op jit(solution)/shard_map/all_gather | solution.py:129
  7.9 70.8 %all-gather.10.cloned.1.call-start = ((), (), s32[]{:S(2)}) async-start(), calls=%async_computation.7 | async-start | bytes 1474560 | tf_op jit(solution)/shard_map/all_gather | solution.py:130
  8.8 60.2 %copy-start.39 = (bf16[768]{0:T(1024)(128)(2,1)S(1)}, bf16[768]{0:T(1024)(128)(2,1)}, u32[]{:S(2)}) copy-start(bf16[768]{0:T(1024)(128)(2,1)} %param.37) | copy-start | bytes 4612
  8.8 66.5 %copy-start = (bf16[1,128,768]{2,1,0:T(8,128)(2,1)S(1)}, bf16[1,128,768]{2,1,0:T(8,128)(2,1)}, u32[]{:S(2)}) copy-start(bf16[1,128,768]{2,1,0:T(8,128)(2,1)} %param.23) | copy-start | bytes 589828
  8.8 73.2 %all-gather.12.cloned.1.call-start = ((), (), s32[]{:S(2)}) async-start(), calls=%async_computation.8 | async-start | bytes 1474560 | tf_op jit(solution)/shard_map/all_gather | solution.py:127
  9.5 161.9 %all-gather.14.cloned.1.call-start = ((), (), s32[]{:S(2)}) async-start(), calls=%async_computation.9 | async-start | bytes 1474560 | tf_op jit(solution)/shard_map/all_gather | solution.py:132
  10.1 163.4 %all-gather.16.cloned.1.call-start = ((), (), s32[]{:S(2)}) async-start(), calls=%async_computation.10 | async-start | bytes 5898240 | tf_op jit(solution)/shard_map/all_gather | solution.py:136
  10.7 166.1 %all-gather.18.cloned.1.call-start = ((), (), s32[]{:S(2)}) async-start(), calls=%async_computation.11 | async-start | bytes 5898240 | tf_op jit(solution)/shard_map/all_gather | solution.py:138
  11.3 417.9 %reduce-scatter.19.cloned.1.call-start = ((), (), s32[]{:S(2)}) async-start(), calls=%async_computation.15 | async-start | bytes 1474560
  86.7 10.5 %collective-permute-start = (bf16[128,12,64]{0,2,1:T(8,128)(2,1)S(1)}, bf16[128,12,64]{0,2,1:T(8,128)(2,1)S(1)}, u32[]{:S(2)}, u32[]{:S(2)}) collective-permute-start(bf16[128,12,64]{0,2,1:T(8,128)(2,1)S(1)} %get-tuple-element.1201), channel_id=1, source_target_pairs={{28,0},{0,4},{4,8},{8,12},{12,16},{16,20},{20,24},{24,28},{29,1},{... | collective-permute-start | bytes 589832 | tf_op jit(solution)/shard_map/while/body/eval_jaxpr/ppermute | solution.py:20
  88.9 11.8 %collective-permute-start.1 = (bf16[128,12,64]{0,2,1:T(8,128)(2,1)S(1)}, bf16[128,12,64]{0,2,1:T(8,128)(2,1)S(1)}, u32[]{:S(2)}, u32[]{:S(2)}) collective-permute-start(bf16[128,12,64]{0,2,1:T(8,128)(2,1)S(1)} %get-tuple-element.1202), channel_id=1, source_target_pairs={{28,0},{0,4},{4,8},{8,12},{12,16},{16,20},{20,24},{24,28},{29,1},{... | collective-permute-start | bytes 589832 | tf_op jit(solution)/shard_map/while/body/eval_jaxpr/ppermute | solution.py:20
  101.1 10.6 %collective-permute-start = (bf16[128,12,64]{0,2,1:T(8,128)(2,1)S(1)}, bf16[128,12,64]{0,2,1:T(8,128)(2,1)S(1)}, u32[]{:S(2)}, u32[]{:S(2)}) collective-permute-start(bf16[128,12,64]{0,2,1:T(8,128)(2,1)S(1)} %get-tuple-element.1201), channel_id=1, source_target_pairs={{28,0},{0,4},{4,8},{8,12},{12,16},{16,20},{20,24},{24,28},{29,1},{... | collective-permute-start | bytes 589832 | tf_op jit(solution)/shard_map/while/body/eval_jaxpr/ppermute | solution.py:20
  101.1 13.2 %collective-permute-start.1 = (bf16[128,12,64]{0,2,1:T(8,128)(2,1)S(1)}, bf16[128,12,64]{0,2,1:T(8,128)(2,1)S(1)}, u32[]{:S(2)}, u32[]{:S(2)}) collective-permute-start(bf16[128,12,64]{0,2,1:T(8,128)(2,1)S(1)} %get-tuple-element.1202), channel_id=1, source_target_pairs={{28,0},{0,4},{4,8},{8,12},{12,16},{16,20},{20,24},{24,28},{29,1},{... | collective-permute-start | bytes 589832 | tf_op jit(solution)/shard_map/while/body/eval_jaxpr/ppermute | solution.py:20
  114.6 10.2 %collective-permute-start = (bf16[128,12,64]{0,2,1:T(8,128)(2,1)S(1)}, bf16[128,12,64]{0,2,1:T(8,128)(2,1)S(1)}, u32[]{:S(2)}, u32[]{:S(2)}) collective-permute-start(bf16[128,12,64]{0,2,1:T(8,128)(2,1)S(1)} %get-tuple-element.1201), channel_id=1, source_target_pairs={{28,0},{0,4},{4,8},{8,12},{12,16},{16,20},{20,24},{24,28},{29,1},{... | collective-permute-start | bytes 589832 | tf_op jit(solution)/shard_map/while/body/eval_jaxpr/ppermute | solution.py:20
  114.7 12.3 %collective-permute-start.1 = (bf16[128,12,64]{0,2,1:T(8,128)(2,1)S(1)}, bf16[128,12,64]{0,2,1:T(8,128)(2,1)S(1)}, u32[]{:S(2)}, u32[]{:S(2)}) collective-permute-start(bf16[128,12,64]{0,2,1:T(8,128)(2,1)S(1)} %get-tuple-element.1202), channel_id=1, source_target_pairs={{28,0},{0,4},{4,8},{8,12},{12,16},{16,20},{20,24},{24,28},{29,1},{... | collective-permute-start | bytes 589832 | tf_op jit(solution)/shard_map/while/body/eval_jaxpr/ppermute | solution.py:20
  127.2 9.3 %collective-permute-start = (bf16[128,12,64]{0,2,1:T(8,128)(2,1)S(1)}, bf16[128,12,64]{0,2,1:T(8,128)(2,1)S(1)}, u32[]{:S(2)}, u32[]{:S(2)}) collective-permute-start(bf16[128,12,64]{0,2,1:T(8,128)(2,1)S(1)} %get-tuple-element.1201), channel_id=1, source_target_pairs={{28,0},{0,4},{4,8},{8,12},{12,16},{16,20},{20,24},{24,28},{29,1},{... | collective-permute-start | bytes 589832 | tf_op jit(solution)/shard_map/while/body/eval_jaxpr/ppermute | solution.py:20
  127.3 11.4 %collective-permute-start.1 = (bf16[128,12,64]{0,2,1:T(8,128)(2,1)S(1)}, bf16[128,12,64]{0,2,1:T(8,128)(2,1)S(1)}, u32[]{:S(2)}, u32[]{:S(2)}) collective-permute-start(bf16[128,12,64]{0,2,1:T(8,128)(2,1)S(1)} %get-tuple-element.1202), channel_id=1, source_target_pairs={{28,0},{0,4},{4,8},{8,12},{12,16},{16,20},{20,24},{24,28},{29,1},{... | collective-permute-start | bytes 589832 | tf_op jit(solution)/shard_map/while/body/eval_jaxpr/ppermute | solution.py:20
  138.9 8.4 collective-permute-start
  139.0 10.5 %collective-permute-start.1 = (bf16[128,12,64]{0,2,1:T(8,128)(2,1)S(1)}, bf16[128,12,64]{0,2,1:T(8,128)(2,1)S(1)}, u32[]{:S(2)}, u32[]{:S(2)}) collective-permute-start(bf16[128,12,64]{0,2,1:T(8,128)(2,1)S(1)} %get-tuple-element.1202), channel_id=1, source_target_pairs={{28,0},{0,4},{4,8},{8,12},{12,16},{16,20},{20,24},{24,28},{29,1},{... | collective-permute-start | bytes 589832 | tf_op jit(solution)/shard_map/while/body/eval_jaxpr/ppermute | solution.py:20
  149.7 8.4 collective-permute-start
  149.8 10.5 %collective-permute-start.1 = (bf16[128,12,64]{0,2,1:T(8,128)(2,1)S(1)}, bf16[128,12,64]{0,2,1:T(8,128)(2,1)S(1)}, u32[]{:S(2)}, u32[]{:S(2)}) collective-permute-start(bf16[128,12,64]{0,2,1:T(8,128)(2,1)S(1)} %get-tuple-element.1202), channel_id=1, source_target_pairs={{28,0},{0,4},{4,8},{8,12},{12,16},{16,20},{20,24},{24,28},{29,1},{... | collective-permute-start | bytes 589832 | tf_op jit(solution)/shard_map/while/body/eval_jaxpr/ppermute | solution.py:20
  160.6 8.4 collective-permute-start
  160.6 10.5 %collective-permute-start.1 = (bf16[128,12,64]{0,2,1:T(8,128)(2,1)S(1)}, bf16[128,12,64]{0,2,1:T(8,128)(2,1)S(1)}, u32[]{:S(2)}, u32[]{:S(2)}) collective-permute-start(bf16[128,12,64]{0,2,1:T(8,128)(2,1)S(1)} %get-tuple-element.1202), channel_id=1, source_target_pairs={{28,0},{0,4},{4,8},{8,12},{12,16},{16,20},{20,24},{24,28},{29,1},{... | collective-permute-start | bytes 589832 | tf_op jit(solution)/shard_map/while/body/eval_jaxpr/ppermute | solution.py:20
  196.4 9.3 %collective-permute-start.2 = (bf16[128,12,64]{0,2,1:T(8,128)(2,1)}, bf16[128,12,64]{0,2,1:T(8,128)(2,1)S(1)}, u32[]{:S(2)}, u32[]{:S(2)}) collective-permute-start(bf16[128,12,64]{0,2,1:T(8,128)(2,1)} %get-tuple-element.1252), channel_id=1, source_target_pairs={{28,0},{0,4},{4,8},{8,12},{12,16},{16,20},{20,24},{24,28},{29,1},{... | collective-permute-start | bytes 589832 | tf_op jit(solution)/shard_map/while/body/eval_jaxpr/ppermute | solution.py:20
  196.4 11.4 %collective-permute-start.3 = (bf16[128,12,64]{0,2,1:T(8,128)(2,1)}, bf16[128,12,64]{0,2,1:T(8,128)(2,1)S(1)}, u32[]{:S(2)}, u32[]{:S(2)}) collective-permute-start(bf16[128,12,64]{0,2,1:T(8,128)(2,1)} %get-tuple-element.1253), channel_id=1, source_target_pairs={{28,0},{0,4},{4,8},{8,12},{12,16},{16,20},{20,24},{24,28},{29,1},{... | collective-permute-start | bytes 589832 | tf_op jit(solution)/shard_map/while/body/eval_jaxpr/ppermute | solution.py:20
  196.4 13.6 %collective-permute-start.4 = (bf16[128,12,64]{0,2,1:T(8,128)(2,1)}, bf16[128,12,64]{0,2,1:T(8,128)(2,1)}, u32[]{:S(2)}, u32[]{:S(2)}) collective-permute-start(bf16[128,12,64]{0,2,1:T(8,128)(2,1)} %get-tuple-element.1255), channel_id=1, source_target_pairs={{28,0},{0,4},{4,8},{8,12},{12,16},{16,20},{20,24},{24,28},{29,1},{... | collective-permute-start | bytes 589832 | tf_op jit(solution)/shard_map/while/body/eval_jaxpr/ppermute | solution.py:20
  196.4 16.8 %collective-permute-start.5 = (bf16[128,12,64]{0,2,1:T(8,128)(2,1)}, bf16[128,12,64]{0,2,1:T(8,128)(2,1)S(1)}, u32[]{:S(2)}, u32[]{:S(2)}) collective-permute-start(bf16[128,12,64]{0,2,1:T(8,128)(2,1)} %get-tuple-element.1256), channel_id=1, source_target_pairs={{28,0},{0,4},{4,8},{8,12},{12,16},{16,20},{20,24},{24,28},{29,1},{... | collective-permute-start | bytes 589832 | tf_op jit(solution)/shard_map/while/body/eval_jaxpr/ppermute | solution.py:20
  214.1 8.6 collective-permute-start.2
  214.1 10.7 %collective-permute-start.3 = (bf16[128,12,64]{0,2,1:T(8,128)(2,1)}, bf16[128,12,64]{0,2,1:T(8,128)(2,1)S(1)}, u32[]{:S(2)}, u32[]{:S(2)}) collective-permute-start(bf16[128,12,64]{0,2,1:T(8,128)(2,1)} %get-tuple-element.1253), channel_id=1, source_target_pairs={{28,0},{0,4},{4,8},{8,12},{12,16},{16,20},{20,24},{24,28},{29,1},{... | collective-permute-start | bytes 589832 | tf_op jit(solution)/shard_map/while/body/eval_jaxpr/ppermute | solution.py:20
  214.1 13.0 %collective-permute-start.4 = (bf16[128,12,64]{0,2,1:T(8,128)(2,1)}, bf16[128,12,64]{0,2,1:T(8,128)(2,1)}, u32[]{:S(2)}, u32[]{:S(2)}) collective-permute-start(bf16[128,12,64]{0,2,1:T(8,128)(2,1)} %get-tuple-element.1255), channel_id=1, source_target_pairs={{28,0},{0,4},{4,8},{8,12},{12,16},{16,20},{20,24},{24,28},{29,1},{... | collective-permute-start | bytes 589832 | tf_op jit(solution)/shard_map/while/body/eval_jaxpr/ppermute | solution.py:20
  214.1 17.1 %collective-permute-start.5 = (bf16[128,12,64]{0,2,1:T(8,128)(2,1)}, bf16[128,12,64]{0,2,1:T(8,128)(2,1)S(1)}, u32[]{:S(2)}, u32[]{:S(2)}) collective-permute-start(bf16[128,12,64]{0,2,1:T(8,128)(2,1)} %get-tuple-element.1256), channel_id=1, source_target_pairs={{28,0},{0,4},{4,8},{8,12},{12,16},{16,20},{20,24},{24,28},{29,1},{... | collective-permute-start | bytes 589832 | tf_op jit(solution)/shard_map/while/body/eval_jaxpr/ppermute | solution.py:20
  232.2 8.6 collective-permute-start.2
  232.2 10.7 %collective-permute-start.3 = (bf16[128,12,64]{0,2,1:T(8,128)(2,1)}, bf16[128,12,64]{0,2,1:T(8,128)(2,1)S(1)}, u32[]{:S(2)}, u32[]{:S(2)}) collective-permute-start(bf16[128,12,64]{0,2,1:T(8,128)(2,1)} %get-tuple-element.1253), channel_id=1, source_target_pairs={{28,0},{0,4},{4,8},{8,12},{12,16},{16,20},{20,24},{24,28},{29,1},{... | collective-permute-start | bytes 589832 | tf_op jit(solution)/shard_map/while/body/eval_jaxpr/ppermute | solution.py:20
  232.2 14.1 %collective-permute-start.4 = (bf16[128,12,64]{0,2,1:T(8,128)(2,1)}, bf16[128,12,64]{0,2,1:T(8,128)(2,1)}, u32[]{:S(2)}, u32[]{:S(2)}) collective-permute-start(bf16[128,12,64]{0,2,1:T(8,128)(2,1)} %get-tuple-element.1255), channel_id=1, source_target_pairs={{28,0},{0,4},{4,8},{8,12},{12,16},{16,20},{20,24},{24,28},{29,1},{... | collective-permute-start | bytes 589832 | tf_op jit(solution)/shard_map/while/body/eval_jaxpr/ppermute | solution.py:20
  232.2 18.2 %collective-permute-start.5 = (bf16[128,12,64]{0,2,1:T(8,128)(2,1)}, bf16[128,12,64]{0,2,1:T(8,128)(2,1)S(1)}, u32[]{:S(2)}, u32[]{:S(2)}) collective-permute-start(bf16[128,12,64]{0,2,1:T(8,128)(2,1)} %get-tuple-element.1256), channel_id=1, source_target_pairs={{28,0},{0,4},{4,8},{8,12},{12,16},{16,20},{20,24},{24,28},{29,1},{... | collective-permute-start | bytes 589832 | tf_op jit(solution)/shard_map/while/body/eval_jaxpr/ppermute | solution.py:20
  251.3 8.6 collective-permute-start.2
  251.3 10.9 %collective-permute-start.3 = (bf16[128,12,64]{0,2,1:T(8,128)(2,1)}, bf16[128,12,64]{0,2,1:T(8,128)(2,1)S(1)}, u32[]{:S(2)}, u32[]{:S(2)}) collective-permute-start(bf16[128,12,64]{0,2,1:T(8,128)(2,1)} %get-tuple-element.1253), channel_id=1, source_target_pairs={{28,0},{0,4},{4,8},{8,12},{12,16},{16,20},{20,24},{24,28},{29,1},{... | collective-permute-start | bytes 589832 | tf_op jit(solution)/shard_map/while/body/eval_jaxpr/ppermute | solution.py:20
  251.3 15.2 %collective-permute-start.4 = (bf16[128,12,64]{0,2,1:T(8,128)(2,1)}, bf16[128,12,64]{0,2,1:T(8,128)(2,1)}, u32[]{:S(2)}, u32[]{:S(2)}) collective-permute-start(bf16[128,12,64]{0,2,1:T(8,128)(2,1)} %get-tuple-element.1255), channel_id=1, source_target_pairs={{28,0},{0,4},{4,8},{8,12},{12,16},{16,20},{20,24},{24,28},{29,1},{... | collective-permute-start | bytes 589832 | tf_op jit(solution)/shard_map/while/body/eval_jaxpr/ppermute | solution.py:20
  251.3 19.3 %collective-permute-start.5 = (bf16[128,12,64]{0,2,1:T(8,128)(2,1)}, bf16[128,12,64]{0,2,1:T(8,128)(2,1)S(1)}, u32[]{:S(2)}, u32[]{:S(2)}) collective-permute-start(bf16[128,12,64]{0,2,1:T(8,128)(2,1)} %get-tuple-element.1256), channel_id=1, source_target_pairs={{28,0},{0,4},{4,8},{8,12},{12,16},{16,20},{20,24},{24,28},{29,1},{... | collective-permute-start | bytes 589832 | tf_op jit(solution)/shard_map/while/body/eval_jaxpr/ppermute | solution.py:20
  271.5 8.6 collective-permute-start.2
  271.5 11.9 %collective-permute-start.3 = (bf16[128,12,64]{0,2,1:T(8,128)(2,1)}, bf16[128,12,64]{0,2,1:T(8,128)(2,1)S(1)}, u32[]{:S(2)}, u32[]{:S(2)}) collective-permute-start(bf16[128,12,64]{0,2,1:T(8,128)(2,1)} %get-tuple-element.1253), channel_id=1, source_target_pairs={{28,0},{0,4},{4,8},{8,12},{12,16},{16,20},{20,24},{24,28},{29,1},{... | collective-permute-start | bytes 589832 | tf_op jit(solution)/shard_map/while/body/eval_jaxpr/ppermute | solution.py:20
  271.5 16.3 %collective-permute-start.4 = (bf16[128,12,64]{0,2,1:T(8,128)(2,1)}, bf16[128,12,64]{0,2,1:T(8,128)(2,1)}, u32[]{:S(2)}, u32[]{:S(2)}) collective-permute-start(bf16[128,12,64]{0,2,1:T(8,128)(2,1)} %get-tuple-element.1255), channel_id=1, source_target_pairs={{28,0},{0,4},{4,8},{8,12},{12,16},{16,20},{20,24},{24,28},{29,1},{... | collective-permute-start | bytes 589832 | tf_op jit(solution)/shard_map/while/body/eval_jaxpr/ppermute | solution.py:20
  271.5 20.4 %collective-permute-start.5 = (bf16[128,12,64]{0,2,1:T(8,128)(2,1)}, bf16[128,12,64]{0,2,1:T(8,128)(2,1)S(1)}, u32[]{:S(2)}, u32[]{:S(2)}) collective-permute-start(bf16[128,12,64]{0,2,1:T(8,128)(2,1)} %get-tuple-element.1256), channel_id=1, source_target_pairs={{28,0},{0,4},{4,8},{8,12},{12,16},{16,20},{20,24},{24,28},{29,1},{... | collective-permute-start | bytes 589832 | tf_op jit(solution)/shard_map/while/body/eval_jaxpr/ppermute | solution.py:20
  292.8 8.8 %collective-permute-start.2 = (bf16[128,12,64]{0,2,1:T(8,128)(2,1)}, bf16[128,12,64]{0,2,1:T(8,128)(2,1)S(1)}, u32[]{:S(2)}, u32[]{:S(2)}) collective-permute-start(bf16[128,12,64]{0,2,1:T(8,128)(2,1)} %get-tuple-element.1252), channel_id=1, source_target_pairs={{28,0},{0,4},{4,8},{8,12},{12,16},{16,20},{20,24},{24,28},{29,1},{... | collective-permute-start | bytes 589832 | tf_op jit(solution)/shard_map/while/body/eval_jaxpr/ppermute | solution.py:20
  292.8 13.0 %collective-permute-start.3 = (bf16[128,12,64]{0,2,1:T(8,128)(2,1)}, bf16[128,12,64]{0,2,1:T(8,128)(2,1)S(1)}, u32[]{:S(2)}, u32[]{:S(2)}) collective-permute-start(bf16[128,12,64]{0,2,1:T(8,128)(2,1)} %get-tuple-element.1253), channel_id=1, source_target_pairs={{28,0},{0,4},{4,8},{8,12},{12,16},{16,20},{20,24},{24,28},{29,1},{... | collective-permute-start | bytes 589832 | tf_op jit(solution)/shard_map/while/body/eval_jaxpr/ppermute | solution.py:20
  292.8 17.3 %collective-permute-start.4 = (bf16[128,12,64]{0,2,1:T(8,128)(2,1)}, bf16[128,12,64]{0,2,1:T(8,128)(2,1)}, u32[]{:S(2)}, u32[]{:S(2)}) collective-permute-start(bf16[128,12,64]{0,2,1:T(8,128)(2,1)} %get-tuple-element.1255), channel_id=1, source_target_pairs={{28,0},{0,4},{4,8},{8,12},{12,16},{16,20},{20,24},{24,28},{29,1},{... | collective-permute-start | bytes 589832 | tf_op jit(solution)/shard_map/while/body/eval_jaxpr/ppermute | solution.py:20
  292.8 21.4 %collective-permute-start.5 = (bf16[128,12,64]{0,2,1:T(8,128)(2,1)}, bf16[128,12,64]{0,2,1:T(8,128)(2,1)S(1)}, u32[]{:S(2)}, u32[]{:S(2)}) collective-permute-start(bf16[128,12,64]{0,2,1:T(8,128)(2,1)} %get-tuple-element.1256), channel_id=1, source_target_pairs={{28,0},{0,4},{4,8},{8,12},{12,16},{16,20},{20,24},{24,28},{29,1},{... | collective-permute-start | bytes 589832 | tf_op jit(solution)/shard_map/while/body/eval_jaxpr/ppermute | solution.py:20
  315.1 8.6 collective-permute-start.2
  315.1 10.7 %collective-permute-start.3 = (bf16[128,12,64]{0,2,1:T(8,128)(2,1)}, bf16[128,12,64]{0,2,1:T(8,128)(2,1)S(1)}, u32[]{:S(2)}, u32[]{:S(2)}) collective-permute-start(bf16[128,12,64]{0,2,1:T(8,128)(2,1)} %get-tuple-element.1253), channel_id=1, source_target_pairs={{28,0},{0,4},{4,8},{8,12},{12,16},{16,20},{20,24},{24,28},{29,1},{... | collective-permute-start | bytes 589832 | tf_op jit(solution)/shard_map/while/body/eval_jaxpr/ppermute | solution.py:20
  315.1 13.0 %collective-permute-start.4 = (bf16[128,12,64]{0,2,1:T(8,128)(2,1)}, bf16[128,12,64]{0,2,1:T(8,128)(2,1)}, u32[]{:S(2)}, u32[]{:S(2)}) collective-permute-start(bf16[128,12,64]{0,2,1:T(8,128)(2,1)} %get-tuple-element.1255), channel_id=1, source_target_pairs={{28,0},{0,4},{4,8},{8,12},{12,16},{16,20},{20,24},{24,28},{29,1},{... | collective-permute-start | bytes 589832 | tf_op jit(solution)/shard_map/while/body/eval_jaxpr/ppermute | solution.py:20
  315.2 17.0 %collective-permute-start.5 = (bf16[128,12,64]{0,2,1:T(8,128)(2,1)}, bf16[128,12,64]{0,2,1:T(8,128)(2,1)S(1)}, u32[]{:S(2)}, u32[]{:S(2)}) collective-permute-start(bf16[128,12,64]{0,2,1:T(8,128)(2,1)} %get-tuple-element.1256), channel_id=1, source_target_pairs={{28,0},{0,4},{4,8},{8,12},{12,16},{16,20},{20,24},{24,28},{29,1},{... | collective-permute-start | bytes 589832 | tf_op jit(solution)/shard_map/while/body/eval_jaxpr/ppermute | solution.py:20
  335.9 94.5 %reduce-scatter.13.cloned.1.call-start = ((), (), s32[]{:S(2)}) async-start(), calls=%async_computation.12 | async-start | bytes 1474560 | tf_op jit(solution)/shard_map/reduce_scatter | solution.py:317
  338.3 92.1 %reduce-scatter.21.cloned.1.call-start = ((), (), s32[]{:S(2)}) async-start(), calls=%async_computation.16 | async-start | bytes 1474560
  338.4 8.6 %collective-permute-start.6 = (bf16[128,12,64]{0,2,1:T(8,128)(2,1)}, bf16[128,12,64]{0,2,1:T(8,128)(2,1)S(1)}, u32[]{:S(2)}, u32[]{:S(2)}) collective-permute-start(bf16[128,12,64]{0,2,1:T(8,128)(2,1)} %get-tuple-element.666), channel_id=1, source_target_pairs={{28,0},{0,4},{4,8},{8,12},{12,16},{16,20},{20,24},{24,28},{29,1},{... | collective-permute-start | bytes 589832 | tf_op jit(solution)/shard_map/ppermute | solution.py:20
  349.9 95.7 %reduce-scatter.23.cloned.1.call-start = ((), (), s32[]{:S(2)}) async-start(), calls=%async_computation.17 | async-start | bytes 1474560
  349.9 8.4 collective-permute-start.7
  361.0 134.9 %reduce-scatter.15.cloned.1.call-start = ((), (), s32[]{:S(2)}) async-start(), calls=%async_computation.13 | async-start | bytes 5898240 | tf_op jit(solution)/shard_map/reduce_scatter | solution.py:329
  365.8 180.6 %reduce-scatter.17.cloned.1.call-start = ((), (), s32[]{:S(2)}) async-start(), calls=%async_computation.14 | async-start | bytes 5898240 | tf_op jit(solution)/shard_map/reduce_scatter | solution.py:335
  429.1 117.2 %copy-start.33 = (f32[192]{0:T(256)S(1)}, f32[192]{0:T(256)}, u32[]{:S(2)}) copy-start(f32[192]{0:T(256)} %get-tuple-element.1015) | copy-start | bytes 2308
  429.1 117.2 %copy-start.34 = (f32[192]{0:T(256)S(1)}, f32[192]{0:T(256)}, u32[]{:S(2)}) copy-start(f32[192]{0:T(256)} %get-tuple-element.1012) | copy-start | bytes 2308
  429.1 117.2 %copy-start.35 = (f32[192]{0:T(256)S(1)}, f32[192]{0:T(256)}, u32[]{:S(2)}) copy-start(f32[192]{0:T(256)} %get-tuple-element.1013) | copy-start | bytes 2308
  429.1 117.2 %copy-start.36 = (f32[192]{0:T(256)S(1)}, f32[192]{0:T(256)}, u32[]{:S(2)}) copy-start(f32[192]{0:T(256)} %get-tuple-element.1010) | copy-start | bytes 2308
  429.1 117.2 %copy-start.37 = (f32[192]{0:T(256)S(1)}, f32[192]{0:T(256)}, u32[]{:S(2)}) copy-start(f32[192]{0:T(256)} %get-tuple-element.1011) | copy-start | bytes 2308
  430.4 116.0 %copy-start.22 = (bf16[192,768]{1,0:T(8,128)(2,1)S(1)}, bf16[192,768]{1,0:T(8,128)(2,1)}, u32[]{:S(2)}) copy-start(bf16[192,768]{1,0:T(8,128)(2,1)} %reduce-scatter.13.cloned.1.call-done) | copy-start | bytes 884740
  (46 other events, 866.9 us)
Sparse Core Ops, SparseCore 0:
  9.6 20.5 all-gather.7
  31.8 17.3 all-gather.9
  50.7 17.6 all-gather.11
  69.9 17.4 all-gather.13
  88.8 37.4 all-gather.15
  127.7 37.4 all-gather.17
  336.0 23.4 reduce-scatter.18
  362.2 25.8 reduce-scatter.12
  391.3 25.6 reduce-scatter.20
  419.6 25.9 reduce-scatter.22
  448.1 47.8 reduce-scatter.14
  498.5 47.7 reduce-scatter.16
where the time goes:
time: 862 us; the launch traced here: 860 us
  blocking collectives  409 us (47%)
  waiting for transfers between devices  285 us (33%)
  matrix products  73.1 us (8%)
  local copies, waits for them, and re-layouts  34.6 us (4%)
  other arithmetic  28.7 us (3%)
  between operations  21 us (2%)
    psum x1, blocking collectives, body(): lax.psum((reduced[0], reduced[1], reduced[2], reduced[3], reduced[4], red...  301 us
    ppermute x44, waiting for transfers between devices, shifted(): return lax.ppermute(block, axis, route)  168 us
    psum x2, blocking collectives, body(): lax.psum((jnp.sum(diff * diff), jnp.sum(own_live.astype(jnp.float32))), (...  79.4 us
    reduce_scatter x1, waiting for transfers between devices, body(): lax.psum_scatter(back_weight_grad.astype(jnp.bfloat16), 'wsh', scatter_di...  50.4 us
    reduce_scatter x1, waiting for transfers between devices, body(): lax.psum_scatter(inner_weight_grad.astype(jnp.bfloat16), 'wsh', scatter_d...  49.3 us
    unnamed x2, blocking collectives  22.5 us
    unnamed x137, local copies, waits for them, and re-layouts  22.2 us
    unnamed x15, waiting for transfers between devices  17.7 us
  transfers between devices with their start and end apart: 56, of which 47 were waited for; matrix products, arithmetic and copies ran while one was open for 12% of the time, Pallas kernels for 0%

commit v1 on v0

--- a/solution.py
+++ b/solution.py
@@ -1,8 +1,11 @@
 import math
+import types
 
 import jax
 import jax.numpy as jnp
 from jax import lax
+from jax.experimental import pallas as pl
+from jax.experimental.pallas import tpu as pltpu
 from jax.sharding import PartitionSpec as P
 
 D = 768
@@ -387,6 +390,854 @@
     )
 
 
+BF = jnp.bfloat16
+F32 = jnp.float32
+FF = 3072
+ROWS = 128
+HEADS = 3
+HW = HEADS * HD
+GROUP = 4
+CTX = 8
+MESH = pl.DeviceIdType.MESH
+
+Q, K, V, O, IN, OUT = range(6)
+WEIGHT_SHAPES = [(192, 768), (192, 768), (192, 768), (192, 768), (192, 3072), (768, 768)]
+PART_SHAPES = [(384, 384), (384, 384), (384, 384), (384, 384), (384, 1536), (768, 768)]
+
+(
+    SMALL,
+    WEIGHT_X,
+    WEIGHT_Y,
+    WEIGHT_CORE,
+    WEIGHT_CORE_X,
+    WEIGHT_CORE_Y,
+    KEY_VALUE,
+    QUERY,
+    CONTEXT,
+    CONTEXT_GRAD,
+    KEY_VALUE_GRAD,
+    QUERY_GRAD,
+    X_ALL,
+    SETTLED_ALL,
+    CONTEXT_ALL,
+    ATTN_GRAD_ALL,
+    INNER_GRAD_ALL,
+    ACTIVATED_ALL,
+    BRANCH_GRAD_ALL,
+    PROJECTED_GRAD_ALL,
+    PAIR,
+    LINE,
+    BACK,
+    GIVE,
+    OWN,
+    VECTORS_W,
+    VECTORS_Z,
+    VECTORS_Y,
+    TOKENS,
+    TEACHER,
+    OUTPUT,
+    INPUT_GRAD,
+    LOAD,
+) = range(33)
+
+
+def fused_fits(mesh):
+    return mesh.shape["ctx"] == CTX and mesh.shape["wsh"] == GROUP
+
+
+def tn(left, right):
+    return lax.dot_general(
+        left, right, (((0,), (0,)), ((), ())), preferred_element_type=jnp.float32
+    )
+
+
+def norm_parts(value):
+    mean = jnp.mean(value, axis=-1, keepdims=True)
+    centered = value - mean
+    spread = jnp.mean(centered * centered, axis=-1, keepdims=True)
+    inverse = lax.rsqrt(spread + EPSILON)
+    return centered * inverse, inverse
+
+
+def norm_back(upstream_gained, normal, inverse):
+    return (
+        upstream_gained
+        - jnp.mean(upstream_gained, axis=-1, keepdims=True)
+        - normal * jnp.mean(upstream_gained * normal, axis=-1, keepdims=True)
+    ) * inverse
+
+
+GELU_C = math.sqrt(2.0 / math.pi)
+
+
+class Numbers:
+    def __init__(self):
+        self.count = 0
+        self.table = {}
+
+    def take(self, key, size=1):
+        if key not in self.table:
+            self.table[key] = self.count
+            self.count += size
+        return self.table[key]
+
+
+def scratch_table():
+    s = types.SimpleNamespace()
+    s.full = [pltpu.VMEM((GROUP, rows, cols), BF) for rows, cols in WEIGHT_SHAPES]
+    s.x = pltpu.VMEM((ROWS, D), BF)
+    s.teacher = pltpu.VMEM((ROWS, D), BF)
+    s.small = pltpu.VMEM((GROUP, 16, D), F32)
+    s.kv_send = pltpu.VMEM((4, 2 * HW, ROWS), BF)
+    s.kv = pltpu.VMEM((CTX, 2 * HW, ROWS), BF)
+    s.q_send = pltpu.VMEM((4, HW, ROWS), BF)
+    s.q = pltpu.VMEM((4, HW, ROWS), BF)
+    s.weights = pltpu.VMEM((CTX, HEADS, ROWS, 4 * ROWS), F32)
+    s.mix = pltpu.VMEM((HEADS, HD, 4 * ROWS), F32)
+    s.total = pltpu.VMEM((HEADS, 8, 4 * ROWS), F32)
+    s.ctx_send = pltpu.VMEM((4, HW, ROWS), BF)
+    s.ctx = pltpu.VMEM((4, HW, ROWS), BF)
+    s.inner = pltpu.VMEM((4, ROWS, D), F32)
+    s.act = pltpu.VMEM((4, ROWS, D), BF)
+    s.first = pltpu.VMEM((ROWS, D), F32)
+    s.keep = pltpu.VMEM((ROWS, D), F32)
+    s.x_half = pltpu.VMEM((2, ROWS, 384), BF)
+    s.set_half = pltpu.VMEM((2, ROWS, 384), BF)
+    s.ag_half = pltpu.VMEM((2, ROWS, 384), BF)
+    s.ig_half = pltpu.VMEM((2, ROWS, 1536), BF)
+    s.bg = pltpu.VMEM((ROWS, D), BF)
+    s.x_all = pltpu.VMEM((GROUP, ROWS, 384), BF)
+    s.set_all = pltpu.VMEM((GROUP, ROWS, 384), BF)
+    s.ctx_all = pltpu.VMEM((GROUP, 2, HW, ROWS), BF)
+    s.ag_all = pltpu.VMEM((GROUP, ROWS, 384), BF)
+    s.ig_all = pltpu.VMEM((GROUP, ROWS, 1536), BF)
+    s.act_all = pltpu.VMEM((GROUP, ROWS, D), BF)
+    s.bg_all = pltpu.VMEM((GROUP, ROWS, D), BF)
+    s.projected_half = [pltpu.VMEM((2, ROWS, 384), BF) for name in (Q, K, V)]
+    s.projected_all = [pltpu.VMEM((GROUP, ROWS, 384), BF) for name in (Q, K, V)]
+    s.cg_send = pltpu.VMEM((4, HW, ROWS), BF)
+    s.cg = pltpu.VMEM((4, HW, ROWS), BF)
+    s.dkv_send = pltpu.VMEM((CTX, 2 * HW, ROWS), BF)
+    s.dkv = pltpu.VMEM((CTX, 2 * HW, ROWS), BF)
+    s.dq_send = pltpu.VMEM((4, HW, ROWS), BF)
+    s.dq = pltpu.VMEM((4, HW, ROWS), BF)
+    s.part = [pltpu.VMEM((rows, cols), BF) for rows, cols in PART_SHAPES]
+    s.pair = [pltpu.VMEM((rows // 2, cols), BF) for rows, cols in PART_SHAPES]
+    s.sum = [pltpu.VMEM((4, rows // 8, cols), BF) for rows, cols in PART_SHAPES]
+    s.line = [pltpu.VMEM((3, rows // 8, cols), BF) for rows, cols in PART_SHAPES]
+    s.done = [pltpu.VMEM((4, rows // 8, cols), BF) for rows, cols in PART_SHAPES]
+    s.wg = pltpu.VMEM((HEADS, HD, 4 * ROWS), BF)
+    s.smalls = pltpu.VMEM((GROUP, 16, HW), F32)
+    s.sg = pltpu.VMEM((16, D), F32)
+    s.sg_w = pltpu.VMEM((GROUP, 16, D), F32)
+    s.sg_z = pltpu.VMEM((4, 16, D), F32)
+    s.sg_y = pltpu.VMEM((2, 16, D), F32)
+    s.out_low = pltpu.VMEM((ROWS, D), BF)
+    return vars(s)
+
+
+LOCAL_SEMS = 32
+REMOTE_SEMS = 160
+
+
+def is_memory(item):
+    return not isinstance(item, (dict, list))
+
+
+def scratch_shapes():
+    return jax.tree.flatten(scratch_table(), is_leaf=is_memory)
+
+
+def fused_kernel(*refs):
+    (tokens, teacher), own_shards = refs[:2], refs[2:8]
+    small_in, lengths, valid = refs[8:11]
+    output, input_grad_out = refs[11:13]
+    grad_out, smalls_out = refs[13:19], refs[19]
+    flat, shape = scratch_shapes()
+    S = types.SimpleNamespace(**jax.tree.unflatten(shape, refs[20 : 20 + len(flat)]))
+    send_sems, recv_sems, local_sems = refs[20 + len(flat) :]
+
+    c = lax.axis_index("ctx")
+    w = lax.axis_index("wsh")
+    a, b = c // 2, c % 2
+    x, core = w // 2, w % 2
+
+    numbers = Numbers()
+    locals_ = Numbers()
+    started = []
+
+    def bit_xor(value, j):
+        out = value
+        bit = 1
+        while bit <= j:
+            if j & bit:
+                has = (value // bit) % 2
+                out = out + bit * (1 - 2 * has)
+            bit *= 2
+        return out
+
+    def remote(key, src, dst, c_to, w_to, offset=0, size=1):
+        number = numbers.take(key, size) + offset
+        copy = pltpu.make_async_remote_copy(
+            src_ref=src,
+            dst_ref=dst,
+            send_sem=send_sems.at[number],
+            recv_sem=recv_sems.at[number],
+            device_id={"ctx": c_to, "wsh": w_to},
+            device_id_type=MESH,
+        )
+        copy.start()
+        started.append(copy)
+        return copy
+
+    def arrived(key, landing, offset=0):
+        number = numbers.take(key) + offset
+        pltpu.make_async_copy(landing, landing, recv_sems.at[number]).wait()
+
+    def local(key, src, dst):
+        copy = pltpu.make_async_copy(src, dst, local_sems.at[locals_.take(key)])
+        copy.start()
+        return copy
+
+    peers = [(c, bit_xor(w, j)) for j in (1, 2, 3)]
+    peers += [(bit_xor(c, j), w) for j in range(1, CTX)]
+    peers += [(bit_xor(c, 1), bit_xor(w, 1))]
+
+    loads = {
+        TOKENS: local(TOKENS, tokens.at[0], S.x),
+        TEACHER: local(TEACHER, teacher.at[0], S.teacher),
+        SMALL: local(SMALL, small_in, S.small.at[w]),
+    }
+    for name in range(6):
+        loads[(LOAD, name)] = local((LOAD, name), own_shards[name], S.full[name].at[w])
+
+    barrier = pltpu.get_barrier_semaphore()
+    for c_to, w_to in peers:
+        pl.semaphore_signal(
+            barrier, inc=1, device_id={"ctx": c_to, "wsh": w_to}, device_id_type=MESH
+        )
+    pl.semaphore_wait(barrier, len(peers))
+
+    for j in (1, 2, 3):
+        remote((SMALL, j), small_in, S.small.at[w], c, bit_xor(w, j))
+
+    def half_of(name, which):
+        rows = WEIGHT_SHAPES[name][0] // 2
+        return pl.ds(pl.multiple_of(which * rows, rows), rows)
+
+    order = (K, V, Q, O, IN, OUT)
+    for name in order:
+        full = S.full[name]
+        own = half_of(name, b)
+        remote((WEIGHT_X, name), own_shards[name].at[own], full.at[w, own], c, bit_xor(w, 2))
+        remote((WEIGHT_CORE, name), own_shards[name], full.at[w], c, bit_xor(w, 1))
+
+    def pump_x(name):
+        slot = S.full[name].at[bit_xor(w, 2), half_of(name, b)]
+        arrived((WEIGHT_X, name), slot)
+        remote((WEIGHT_Y, name), slot, slot, bit_xor(c, 1), w)
+        remote((WEIGHT_CORE_X, name), slot, slot, c, bit_xor(w, 1))
+
+    def pump_y(name):
+        slot = S.full[name].at[bit_xor(w, 2), half_of(name, 1 - b)]
+        arrived((WEIGHT_Y, name), slot)
+        remote((WEIGHT_CORE_Y, name), slot, slot, c, bit_xor(w, 1))
+
+    def weight_ready(name):
+        full = S.full[name]
+        loads[(LOAD, name)].wait()
+        arrived((WEIGHT_CORE, name), full.at[bit_xor(w, 1)])
+        arrived((WEIGHT_CORE_X, name), full.at[bit_xor(w, 3), half_of(name, b)])
+        arrived((WEIGHT_CORE_Y, name), full.at[bit_xor(w, 3), half_of(name, 1 - b)])
+
+    def square(name):
+        return S.full[name][...].reshape(D, D)
+
+    starts, running = [], 0
+    for i in range(lengths.shape[1]):
+        starts.append(running)
+        running = running + lengths[0, i]
+    limit = valid[0]
+
+    def code_of(position):
+        code = jnp.zeros(position.shape, jnp.int32)
+        for start in starts:
+            code = code + (start <= position).astype(jnp.int32)
+        return 2 * code + (position < limit).astype(jnp.int32)
+
+    lane = lax.broadcasted_iota(jnp.int32, (1, 4 * ROWS), 1)
+    query_code = code_of((2 * (lane // ROWS) + b) * ROWS + lane % ROWS)
+
+    def key_code(block):
+        return code_of(block * ROWS + lax.broadcasted_iota(jnp.int32, (ROWS, 1), 0))
+
+    own_live = c * ROWS + lax.broadcasted_iota(jnp.int32, (ROWS, 1), 0) < limit
+
+    loads[TOKENS].wait()
+    x_low = S.x[...]
+    for i in range(2):
+        S.x_half[i] = x_low[:, 384 * i : 384 * (i + 1)]
+
+    loads[SMALL].wait()
+    for j in (1, 2, 3):
+        arrived((SMALL, j), S.small.at[bit_xor(w, j)])
+    small = (S.small[0] + S.small[1]) + (S.small[2] + S.small[3])
+
+    def vector(row):
+        return small[row : row + 1, :]
+
+    def project(name, bias):
+        value = matmul(x_low, square(name))
+        if bias is not None:
+            value = value + vector(bias)
+        return value.T.astype(BF)
+
+    pump_x(K)
+    pump_x(V)
+    pump_y(K)
+    weight_ready(K)
+    turned = project(K, None)
+    for i in range(4):
+        S.kv_send[i, 0:HW, :] = turned[HW * i : HW * (i + 1), :]
+    pump_x(Q)
+    pump_y(V)
+    weight_ready(V)
+    turned = project(V, 1)
+    for i in range(4):
+        S.kv_send[i, HW : 2 * HW, :] = turned[HW * i : HW * (i + 1), :]
+    for j in range(1, CTX):
+        to = bit_xor(c, j)
+        remote((KEY_VALUE, j), S.kv_send.at[to // 2], S.kv.at[c], to, w)
+    S.kv[c] = S.kv_send[a]
+    pump_x(O)
+    pump_y(Q)
+    weight_ready(Q)
+    turned = project(Q, 0)
+    for i in range(4):
+        S.q_send[i] = turned[HW * i : HW * (i + 1), :]
+    for j in (1, 2, 3):
+        remote((QUERY, j), S.q_send.at[bit_xor(a, j)], S.q.at[a], bit_xor(c, 2 * j), w)
+    S.q[a] = S.q_send[a]
+
+    def to_group(key, source_of, everywhere):
+        for j in (1, 2, 3):
+            to = bit_xor(w, j)
+            remote((*key, j), source_of(to), everywhere.at[w], c, to)
+
+    def from_group(key, everywhere):
+        for j in (1, 2, 3):
+            arrived((*key, j), everywhere.at[bit_xor(w, j)])
+
+    to_group((X_ALL,), lambda to: S.x_half.at[to // 2], S.x_all)
+    S.x_all[w] = S.x_half[x]
+
+    pump_x(IN)
+    pump_y(O)
+
+    for j in (1, 2, 3):
+        arrived((QUERY, j), S.q.at[bit_xor(a, j)])
+    for j in range(1, CTX):
+        arrived((KEY_VALUE, j), S.kv.at[bit_xor(c, j)])
+
+    score_scale = 1.0 / math.sqrt(HD)
+
+    def wide(ref, h):
+        return jnp.concatenate(
+            [ref[i, HD * h : HD * (h + 1), :] for i in range(4)], axis=1
+        )
+
+    S.mix[...] = jnp.zeros(S.mix.shape, F32)
+    S.total[...] = jnp.zeros(S.total.shape, F32)
+
+    @pl.loop(0, CTX)
+    def attend_block(block):
+        allowed = key_code(block) == query_code
+        for h in range(HEADS):
+            key_t = S.kv[block, HD * h : HD * (h + 1), :]
+            value_t = S.kv[block, HW + HD * h : HW + HD * (h + 1), :]
+            scores = tn(key_t, wide(S.q, h)) * score_scale
+            weights = jnp.exp(jnp.where(allowed, scores, MASKED))
+            S.weights[block, h] = weights
+            S.total[h, 0:1, :] += jnp.sum(weights, axis=0, keepdims=True)
+            S.mix[h] += matmul(value_t, weights.astype(BF))
+
+    for h in range(HEADS):
+        context_t = (S.mix[h] / S.total[h, 0:1, :]).astype(BF)
+        for i in range(4):
+            S.ctx_send[i, HD * h : HD * (h + 1), :] = context_t[:, ROWS * i : ROWS * (i + 1)]
+    for j in (1, 2, 3):
+        to = bit_xor(a, j)
+        remote((CONTEXT, j), S.ctx_send.at[to], S.ctx.at[a], bit_xor(c, 2 * j), w)
+    S.ctx[a] = S.ctx_send[a]
+    pump_x(OUT)
+    pump_y(IN)
+    weight_ready(O)
+    for j in (1, 2, 3):
+        arrived((CONTEXT, j), S.ctx.at[bit_xor(a, j)])
+
+    to_group((CONTEXT_ALL,), lambda to: S.ctx.at[pl.ds(2 * (to // 2), 2)], S.ctx_all)
+    S.ctx_all[w] = S.ctx[pl.ds(2 * x, 2)]
+    attn = tn(S.ctx[...].reshape(D, ROWS), square(O)) + vector(2)
+    first_sum = x_low.astype(F32) + attn
+    normal_one, inverse_one = norm_parts(first_sum)
+    settled = normal_one * vector(3) + vector(4)
+    settled_low = settled.astype(BF)
+    S.first[...] = normal_one
+    S.keep[...] = settled
+    for i in range(2):
+        S.set_half[i] = settled_low[:, 384 * i : 384 * (i + 1)]
+    to_group((SETTLED_ALL,), lambda to: S.set_half.at[to // 2], S.set_all)
+    S.set_all[w] = S.set_half[x]
+    pump_y(OUT)
+    weight_ready(IN)
+    for t in range(4):
+        w_part = S.full[IN][:, :, D * t : D * (t + 1)].reshape(D, D)
+        inner = matmul(settled_low, w_part) + vector(8 + t)
+        S.inner[t] = inner
+        S.act[t] = (
+            0.5 * inner * (1.0 + jnp.tanh(GELU_C * (inner + 0.044715 * inner * inner * inner)))
+        ).astype(BF)
+    to_group((ACTIVATED_ALL,), lambda to: S.act.at[to], S.act_all)
+    S.act_all[w] = S.act[w]
+    weight_ready(OUT)
+    branch = vector(5)
+    for t in range(4):
+        branch = branch + matmul(S.act[t], S.full[OUT][t])
+    normal_two, inverse_two = norm_parts(S.keep[...] + branch)
+    result = normal_two * vector(6) + vector(7)
+    S.out_low[...] = result.astype(BF)
+    finishing = [local(OUTPUT, S.out_low, output)]
+    loads[TEACHER].wait()
+    diff = jnp.where(own_live, result - S.teacher[...].astype(F32), 0.0)
+    count = vector(12)
+    upstream = diff * ((ROWS * CTX * GROUP) / count)
+    S.sg[...] = jnp.zeros((16, D), F32)
+
+    def note(row, value):
+        S.sg[row : row + 1, :] = jnp.sum(value.astype(F32), axis=0, keepdims=True)
+
+    note(12, diff * diff)
+    S.sg[13:14, :] = count * (1.0 / (CTX * GROUP))
+    note(6, upstream * normal_two)
+    note(7, upstream)
+
+    d_second = norm_back(upstream * vector(6), normal_two, inverse_two)
+    branch_grad = d_second.astype(BF)
+    S.bg[...] = branch_grad
+    to_group((BRANCH_GRAD_ALL,), lambda to: S.bg, S.bg_all)
+    S.bg_all[w] = branch_grad
+    note(5, branch_grad)
+    d_settled = d_second
+    for t in range(4):
+        d_act = right_product(branch_grad, S.full[OUT][t])
+        inner = S.inner[t]
+        squared = inner * inner
+        bend = jnp.tanh(GELU_C * (inner + 0.044715 * squared * inner))
+        slope = 0.5 * (1.0 + bend) + 0.5 * inner * (1.0 - bend * bend) * (
+            GELU_C * (1.0 + 3 * 0.044715 * squared)
+        )
+        inner_grad = (d_act * slope).astype(BF)
+        S.ig_half[t // 2, :, D * (t % 2) : D * (t % 2 + 1)] = inner_grad
+        note(8 + t, inner_grad)
+        w_part = S.full[IN][:, :, D * t : D * (t + 1)].reshape(D, D)
+        d_settled = d_settled + right_product(inner_grad, w_part)
+    to_group((INNER_GRAD_ALL,), lambda to: S.ig_half.at[to % 2], S.ig_all)
+    S.ig_all[w] = S.ig_half[core]
+    normal_one = S.first[...]
+    note(3, d_settled * normal_one)
+    note(4, d_settled)
+    d_first = norm_back(d_settled * vector(3), normal_one, inverse_one)
+    S.keep[...] = d_first
+    attn_grad = d_first.astype(BF)
+    note(2, attn_grad)
+    context_grad = right_product(attn_grad, square(O)).T.astype(BF)
+    for i in range(4):
+        S.cg_send[i] = context_grad[HW * i : HW * (i + 1), :]
+    for j in (1, 2, 3):
+        to = bit_xor(a, j)
+        remote((CONTEXT_GRAD, j), S.cg_send.at[to], S.cg.at[a], bit_xor(c, 2 * j), w)
+    S.cg[a] = S.cg_send[a]
+    for i in range(2):
+        S.ag_half[i] = attn_grad[:, 384 * i : 384 * (i + 1)]
+    to_group((ATTN_GRAD_ALL,), lambda to: S.ag_half.at[to % 2], S.ag_all)
+    S.ag_all[w] = S.ag_half[core]
+
+    def reduce_pair(name):
+        half = PART_SHAPES[name][0] // 2
+        there = pl.ds(pl.multiple_of((1 - b) * half, half), half)
+        remote((PAIR, name), S.part[name].at[there], S.pair[name], bit_xor(c, 1), w)
+
+    def reduce_line(name):
+        rows, cols = PART_SHAPES[name]
+        half = rows // 2
+        arrived((PAIR, name), S.pair[name])
+        here = pl.ds(pl.multiple_of(b * half, half), half)
+        both = S.part[name][here, :].astype(F32) + S.pair[name][...].astype(F32)
+        S.sum[name][...] = both.astype(BF).reshape(4, rows // 8, cols)
+        for j in (1, 2, 3):
+            remote(
+                (LINE, name, j),
+                S.sum[name].at[bit_xor(a, j)],
+                S.line[name].at[j - 1],
+                bit_xor(c, 2 * j),
+                w,
+            )
+
+    def spread_line(name):
+        for j in (1, 2, 3):
+            arrived((LINE, name, j), S.line[name].at[j - 1])
+        total = S.sum[name][a].astype(F32)
+        for j in range(3):
+            total = total + S.line[name][j].astype(F32)
+        done = S.done[name]
+        done[a] = total.astype(BF)
+        for j in (1, 2, 3):
+            remote((BACK, name, j), done.at[a], done.at[a], bit_xor(c, 2 * j), w)
+
+    def spread_pair(name):
+        done, out = S.done[name], grad_out[name]
+        for j in (1, 2, 3):
+            arrived((BACK, name, j), done.at[bit_xor(a, j)])
+        if name == OUT:
+            remote((GIVE, name), done, out.at[b], bit_xor(c, 1), w)
+            finishing.append(local((GIVE, name), done, out.at[b]))
+            return
+        remote((GIVE, name), done, out.at[core], bit_xor(c, 1), 2 * x + b, core, 2)
+
+        @pl.when(core == b)
+        def keep_own():
+            local((OWN, name), done, out.at[core])
+
+        @pl.when(core != b)
+        def give_core():
+            remote((OWN, name), done, out.at[core], c, bit_xor(w, 1))
+            started.pop()
+
+    def settle(name):
+        done, out = S.done[name], grad_out[name]
+        if name == OUT:
+            arrived((GIVE, name), out.at[1 - b])
+            return
+
+        @pl.when(core == b)
+        def from_chip():
+            pltpu.make_async_copy(
+                done, out.at[core], local_sems.at[locals_.take((OWN, name))]
+            ).wait()
+            arrived((OWN, name), out.at[1 - core])
+
+        @pl.when(core != b)
+        def from_partner():
+            arrived((GIVE, name), out.at[0], 0)
+            arrived((GIVE, name), out.at[1], 1)
+            sent = numbers.take((OWN, name))
+            pltpu.make_async_copy(done, done, send_sems.at[sent]).wait()
+
+    from_group((ACTIVATED_ALL,), S.act_all)
+    from_group((BRANCH_GRAD_ALL,), S.bg_all)
+    S.part[OUT][...] = tn(
+        S.act_all[...].reshape(GROUP * ROWS, D), S.bg_all[...].reshape(GROUP * ROWS, D)
+    ).astype(BF)
+    reduce_pair(OUT)
+
+    for j in (1, 2, 3):
+        arrived((CONTEXT_GRAD, j), S.cg.at[bit_xor(a, j)])
+    for h in range(HEADS):
+        grad = wide(S.cg, h).astype(F32)
+        row_total = S.total[h, 0:1, :]
+        S.wg[h] = (grad / row_total).astype(BF)
+        S.total[h, 1:2, :] = -jnp.sum(grad * S.mix[h], axis=0, keepdims=True) / (
+            row_total * row_total
+        )
+    S.mix[...] = jnp.zeros(S.mix.shape, F32)
+
+    @pl.loop(0, CTX)
+    def attend_back(block):
+        for h in range(HEADS):
+            key_rows = slice(HD * h, HD * (h + 1))
+            value_rows = slice(HW + HD * h, HW + HD * (h + 1))
+            key_t = S.kv[block, key_rows, :]
+            value_t = S.kv[block, value_rows, :]
+            weights = S.weights[block, h]
+            grad = S.wg[h]
+            weight_grad = tn(value_t, grad) + S.total[h, 1:2, :]
+            score_grad = (weights * weight_grad).astype(BF)
+            S.mix[h] += matmul(key_t, score_grad)
+            S.dkv_send[block, key_rows, :] = (
+                right_product(wide(S.q, h), score_grad) * score_scale
+            ).astype(BF)
+            S.dkv_send[block, value_rows, :] = right_product(grad, weights.astype(BF)).astype(BF)
+
+    for j in range(1, CTX):
+        to = bit_xor(c, j)
+        remote((KEY_VALUE_GRAD, j), S.dkv_send.at[to], S.dkv.at[c], to, w)
+    S.dkv[c] = S.dkv_send[c]
+    for h in range(HEADS):
+        query_t = (S.mix[h] * score_scale).astype(BF)
+        for i in range(4):
+            S.dq_send[i, HD * h : HD * (h + 1), :] = query_t[:, ROWS * i : ROWS * (i + 1)]
+    for j in (1, 2, 3):
+        to = bit_xor(a, j)
+        remote((QUERY_GRAD, j), S.dq_send.at[to], S.dq.at[a], bit_xor(c, 2 * j), w)
+    S.dq[a] = S.dq_send[a]
+
+    from_group((SETTLED_ALL,), S.set_all)
+    from_group((INNER_GRAD_ALL,), S.ig_all)
+    S.part[IN][...] = tn(
+        S.set_all[...].reshape(GROUP * ROWS, 384), S.ig_all[...].reshape(GROUP * ROWS, 1536)
+    ).astype(BF)
+    reduce_pair(IN)
+    reduce_line(OUT)
+    from_group((CONTEXT_ALL,), S.ctx_all)
+    from_group((ATTN_GRAD_ALL,), S.ag_all)
+    context_all = jnp.concatenate(
+        [S.ctx_all[i].reshape(384, ROWS) for i in range(GROUP)], axis=1
+    )
+    S.part[O][...] = matmul(context_all, S.ag_all[...].reshape(GROUP * ROWS, 384)).astype(BF)
+    reduce_pair(O)
+    reduce_line(IN)
+    from_group((X_ALL,), S.x_all)
+
+    for j in range(1, CTX):
+        arrived((KEY_VALUE_GRAD, j), S.dkv.at[bit_xor(c, j)])
+    for j in (1, 2, 3):
+        arrived((QUERY_GRAD, j), S.dq.at[bit_xor(a, j)])
+
+    def summed(first_row):
+        parts = []
+        for i in range(4):
+            rows = slice(first_row, first_row + HW)
+            both = S.dkv[2 * i, rows, :].astype(F32) + S.dkv[2 * i + 1, rows, :].astype(F32)
+            parts.append(both)
+        return jnp.concatenate(parts, axis=0).T.astype(BF)
+
+    grads = {
+        V: summed(HW),
+        K: summed(0),
+        Q: S.dq[...].reshape(D, ROWS).T,
+    }
+    note(1, grads[V])
+    note(0, grads[Q])
+    for name in (V, K, Q):
+        for i in range(2):
+            S.projected_half[name][i] = grads[name][:, 384 * i : 384 * (i + 1)]
+        half = S.projected_half[name]
+        to_group((PROJECTED_GRAD_ALL, name), lambda to: half.at[to % 2], S.projected_all[name])
+        S.projected_all[name][w] = half[core]
+    for j in (1, 2, 3):
+        remote((VECTORS_W, j), S.sg, S.sg_w.at[w], c, bit_xor(w, j))
+    S.sg_w[w] = S.sg[...]
+
+    input_grad = S.keep[...]
+    for name in (Q, K, V):
+        input_grad = input_grad + right_product(grads[name], square(name))
+    S.first[...] = input_grad
+    finishing.append(local(INPUT_GRAD, S.first, input_grad_out))
+
+    x_all = S.x_all[...].reshape(GROUP * ROWS, 384)
+    spread_line(OUT)
+    for name in (V, K, Q):
+        from_group((PROJECTED_GRAD_ALL, name), S.projected_all[name])
+        S.part[name][...] = tn(
+            x_all, S.projected_all[name][...].reshape(GROUP * ROWS, 384)
+        ).astype(BF)
+        reduce_pair(name)
+    reduce_line(O)
+    spread_line(IN)
+    for j in (1, 2, 3):
+        arrived((VECTORS_W, j), S.sg_w.at[bit_xor(w, j)])
+    S.sg_z[a] = (S.sg_w[0] + S.sg_w[1]) + (S.sg_w[2] + S.sg_w[3])
+    for j in (1, 2, 3):
+        remote((VECTORS_Z, j), S.sg_z.at[a], S.sg_z.at[a], bit_xor(c, 2 * j), w)
+    spread_pair(OUT)
+    reduce_line(V)
+    spread_line(O)
+    reduce_line(K)
+    spread_pair(IN)
+    reduce_line(Q)
+    for j in (1, 2, 3):
+        arrived((VECTORS_Z, j), S.sg_z.at[bit_xor(a, j)])
+    S.sg_y[b] = (S.sg_z[0] + S.sg_z[1]) + (S.sg_z[2] + S.sg_z[3])
+    remote(VECTORS_Y, S.sg_y.at[b], S.sg_y.at[b], bit_xor(c, 1), w)
+    spread_line(V)
+    spread_pair(O)
+    spread_line(K)
+    spread_line(Q)
+    spread_pair(V)
+    spread_pair(K)
+    arrived(VECTORS_Y, S.sg_y.at[1 - b])
+    everything = S.sg_y[0] + S.sg_y[1]
+    for i in range(4):
+        S.smalls[i] = everything[:, HW * i : HW * (i + 1)]
+    finishing.append(local(VECTORS_Y, S.smalls, smalls_out))
+    spread_pair(Q)
+
+    for name in range(6):
+        settle(name)
+    for copy in finishing:
+        copy.wait()
+    for copy in started:
+        copy.wait_send()
+
+
+def finish_kernel(*refs):
+    (g_q, g_k, g_v, g_o, g_in, g_out, smalls, output, input_grad) = refs[:9]
+    (r_q, r_k, r_v, r_o, r_in, r_out, vectors, inner_bias, loss, r_output, r_input) = refs[9:]
+    step = pl.program_id(0)
+    for source, result in ((g_q, r_q), (g_k, r_k), (g_v, r_v), (g_o, r_o), (g_in, r_in)):
+        width = source.shape[3]
+        for i in range(2):
+            result[:, width * i : width * (i + 1)] = source[i, 0].astype(F32)
+    r_out[...] = g_out[0].reshape(HW, D).astype(F32)
+    r_output[0] = output[...]
+    r_input[0] = input_grad[...]
+
+    @pl.when(step == 0)
+    def once():
+        w = lax.axis_index("wsh")
+        vectors[...] = smalls[w, 0:8, :]
+        for i in range(4):
+            inner_bias[0:1, HW * i : HW * (i + 1)] = smalls[i, pl.ds(8 + w, 1), :]
+        error = jnp.sum(smalls[:, 12:13, :])
+        count = jnp.max(smalls[0, 13:14, :])
+        loss[0, 0] = error / (count * D)
+
+
+def fused_body(tokens, teacher, doc_lengths, valid_len, *weights):
+    (
+        q_weight,
+        q_bias,
+        k_weight,
+        v_weight,
+        v_bias,
+        o_weight,
+        o_bias,
+        ln1_gain,
+        ln1_bias,
+        in_weight,
+        in_bias,
+        out_weight,
+        out_bias,
+        ln2_gain,
+        ln2_bias,
+    ) = weights
+    w = lax.axis_index("wsh")
+    own = (jnp.arange(GROUP) == w).astype(F32)
+    rows = jnp.stack(
+        [q_bias, v_bias, o_bias, ln1_gain, ln1_bias, out_bias, ln2_gain, ln2_bias]
+    ).astype(F32)
+    rows = (rows[:, None, :] * own[None, :, None]).reshape(8, D)
+    inner_rows = in_bias.astype(F32)[None, :] * own[:, None]
+    valid_row = jnp.broadcast_to(valid_len.astype(F32)[:, None], (1, D))
+    small = jnp.concatenate([rows, inner_rows, valid_row, jnp.zeros((3, D), F32)], axis=0)
+
+    hbm = pl.BlockSpec(memory_space=pl.ANY)
+    smem = pl.BlockSpec(memory_space=pltpu.SMEM)
+    low = lambda *shape: jax.ShapeDtypeStruct(shape, BF)
+    full = lambda *shape: jax.ShapeDtypeStruct(shape, F32)
+    output, input_grad, g_q, g_k, g_v, g_o, g_in, g_out, smalls = pl.pallas_call(
+        fused_kernel,
+        out_shape=(
+            low(ROWS, D),
+            full(ROWS, D),
+            low(2, 4, 48, 384),
+            low(2, 4, 48, 384),
+            low(2, 4, 48, 384),
+            low(2, 4, 48, 384),
+            low(2, 4, 48, 1536),
+            low(2, 4, 96, D),
+            full(GROUP, 16, HW),
+        ),
+        in_specs=[hbm] * 9 + [smem] * 2,
+        out_specs=[hbm] * 9,
+        scratch_shapes=scratch_shapes()[0]
+        + [
+            pltpu.SemaphoreType.DMA((REMOTE_SEMS,)),
+            pltpu.SemaphoreType.DMA((REMOTE_SEMS,)),
+            pltpu.SemaphoreType.DMA((LOCAL_SEMS,)),
+        ],
+        compiler_params=pltpu.CompilerParams(
+            collective_id=0, has_side_effects=True, vmem_limit_bytes=67043328
+        ),
+        name="layer",
+    )(
+        tokens,
+        teacher,
+        q_weight,
+        k_weight,
+        v_weight,
+        o_weight,
+        in_weight,
+        out_weight,
+        small,
+        doc_lengths,
+        valid_len,
+    )
+
+    steps = 4
+    square_in = pl.BlockSpec((2, 1, HW // steps, 384), lambda i: (0, i, 0, 0))
+    square_out = pl.BlockSpec((HW // steps, D), lambda i: (i, 0))
+    whole = lambda *shape: pl.BlockSpec(shape, lambda i: (0,) * len(shape))
+    results = pl.pallas_call(
+        finish_kernel,
+        grid=(steps,),
+        out_shape=(
+            full(HW, D),
+            full(HW, D),
+            full(HW, D),
+            full(HW, D),
+            full(HW, FF),
+            full(D, D),
+            full(8, HW),
+            full(1, D),
+            full(1, 1),
+            low(1, ROWS, D),
+            full(1, ROWS, D),
+        ),
+        in_specs=[square_in] * 4
+        + [
+            pl.BlockSpec((2, 1, HW // steps, 1536), lambda i: (0, i, 0, 0)),
+            pl.BlockSpec((1, 2, 96, D), lambda i: (i // 2, i % 2, 0, 0)),
+            whole(GROUP, 16, HW),
+            pl.BlockSpec((ROWS // steps, D), lambda i: (i, 0)),
+            pl.BlockSpec((ROWS // steps, D), lambda i: (i, 0)),
+        ],
+        out_specs=[square_out] * 4
+        + [
+            pl.BlockSpec((HW // steps, FF), lambda i: (i, 0)),
+            pl.BlockSpec((D // steps, D), lambda i: (i, 0)),
+            whole(8, HW),
+            whole(1, D),
+            pl.BlockSpec(memory_space=pltpu.SMEM),
+            pl.BlockSpec((1, ROWS // steps, D), lambda i: (0, i, 0)),
+            pl.BlockSpec((1, ROWS // steps, D), lambda i: (0, i, 0)),
+        ],
+        compiler_params=pltpu.CompilerParams(dimension_semantics=("arbitrary",)),
+        name="finish",
+    )(g_q, g_k, g_v, g_o, g_in, g_out, smalls, output, input_grad)
+    r_q, r_k, r_v, r_o, r_in, r_out, vectors, inner_bias, loss, r_output, r_input = results
+    return (
+        r_output,
+        loss[0, 0],
+        r_input,
+        r_q,
+        vectors[0],
+        r_k,
+        r_v,
+        vectors[1],
+        r_o,
+        vectors[2],
+        vectors[3],
+        vectors[4],
+        r_in,
+        inner_bias[0],
+        r_out,
+        vectors[5],
+        vectors[6],
+        vectors[7],
+    )
+
+
 def solution(mesh):
     in_specs = (
         P("wsh", "ctx", None),
@@ -429,4 +1280,5 @@
         P("wsh"),
         P("wsh"),
     )
-    return jax.shard_map(body, mesh=mesh, in_specs=in_specs, out_specs=out_specs, check_vma=False)
+    program = fused_body if fused_fits(mesh) else body
+    return jax.shard_map(program, mesh=mesh, in_specs=in_specs, out_specs=out_specs, check_vma=False)

time: 862 us -> 230 us (0.27)
  the two profiles are of different devices: /device:TPU:0 before, /device:TPU:17 now
where the time goes in v1:
time: 230 us; the launch traced here: 229 us
  Pallas kernels  218 us (95%)
  local copies, waits for them, and re-layouts  7.27 us (3%)
  other arithmetic  2.74 us (1%)
    pallas_call x1, Pallas kernels, fused_body(): pl.pallas_call(fused_kernel, out_shape=(low(ROWS, D), full(ROWS, D), low(...  212 us
    pallas_call x1, Pallas kernels, fused_body(): pl.pallas_call(finish_kernel, grid=(steps,), out_shape=(full(HW, D), full...  5.98 us
    another operation x9, local copies, waits for them, and re-layouts, fused_body(): jnp.stack([q_bias, v_bias, o_bias, ln1_gain, ln1_bias, out_bias, ln2_gain...  5.29 us

profile of v1, /device:TPU:17, one launch (start us, length us, event | category | flops | bytes accessed | tf_op | source)
XLA Modules:
  0.0 229.3 jit_solution(16185227902342111281)
XLA Ops:
  1.3 0.1 pad.2.clone
  1.4 0.1 pad.3.clone
  1.5 0.7 stack.27
  2.1 0.7 stack.28
  2.8 0.7 stack.29
  3.4 0.7 stack.30
  4.1 0.7 stack.31
  4.8 0.7 stack.32
  5.4 0.7 stack.33
  6.1 0.7 stack.34
  6.8 0.7 convert_element_type.26
  7.5 0.1 mul.35
  7.5 0.1 mul.36
  7.6 0.1 broadcast_multiply_fusion.1
  7.7 0.1 mul.34
  7.8 0.7 maximum_maximum_fusion.refs_8_
  8.5 211.9 %layer.1 = (bf16[128,768]{1,0:T(8,128)(2,1)}, f32[128,768]{1,0:T(8,128)}, bf16[2,4,48,384]{3,2,1,0:T(8,128)(2,1)}, bf16[2,4,48,384]{3,2,1,0:T(8,128)(2,1)}, bf16...) custom-call(bf16[1,128,768]{2,1,0:T(8,128)(2,1)} %refs_0_.1, ...), custom_call_target="tpu_custom_call" | custom-call | tf_op jit(solution)/shard_map/layer/pallas_call | solution.py:1138
  220.4 6.0 %finish.1 = (f32[192,768]{1,0:T(8,128)}, f32[192,768]{1,0:T(8,128)}, f32[192,768]{1,0:T(8,128)}, f32[192,768]{1,0:T(8,128)}, f32[192,3072]{1,0:T(8,128)}, /*inde...) custom-call(bf16[2,4,48,384]{3,2,1,0:T(8,128)(2,1)} %get-tuple-eleme, ...), custom_call_target="tpu_custom_call" | custom-call | tf_op jit(solution)/shard_map/finish/pallas_call | solution.py:1181
  226.4 1.3 reduce
  227.7 1.6 fusion
  (5 shorter events, 0.0 us)

commit v2 on v1

--- a/solution.py
+++ b/solution.py
@@ -400,36 +400,42 @@
 CTX = 8
 MESH = pl.DeviceIdType.MESH
 
-Q, K, V, O, IN, OUT = range(6)
-WEIGHT_SHAPES = [(192, 768), (192, 768), (192, 768), (192, 768), (192, 3072), (768, 768)]
-PART_SHAPES = [(384, 384), (384, 384), (384, 384), (384, 384), (384, 1536), (768, 768)]
+Q, K, V, O, IN, OUT, PART_Q, PART_K, PART_V = range(9)
+SLICE = 256
+WEIGHT_SHAPES = [(192, 768)] * 4 + [(192, 3072), (768, 768)] + [(192, SLICE)] * 3
+SECOND_WAY = {Q: 2, K: 2, V: 2, O: 1, IN: 1, OUT: 2, PART_Q: 1, PART_K: 1, PART_V: 1}
+PART_SHAPES = {O: (384, 384), IN: (384, 1536), OUT: (768, 768)}
+HALVING = {O: (1, 2, 4), IN: (1, 2, 4), OUT: (1, 2, 4)}
+HEAD_COLS = 640
 
 (
     SMALL,
     WEIGHT_X,
-    WEIGHT_Y,
+    WEIGHT_SECOND,
     WEIGHT_CORE,
     WEIGHT_CORE_X,
-    WEIGHT_CORE_Y,
-    KEY_VALUE,
-    QUERY,
+    WEIGHT_CORE_SECOND,
+    X_LINE,
+    X_PAIR,
     CONTEXT,
     CONTEXT_GRAD,
     KEY_VALUE_GRAD,
     QUERY_GRAD,
-    X_ALL,
     SETTLED_ALL,
     CONTEXT_ALL,
     ATTN_GRAD_ALL,
     INNER_GRAD_ALL,
     ACTIVATED_ALL,
     BRANCH_GRAD_ALL,
-    PROJECTED_GRAD_ALL,
-    PAIR,
-    LINE,
-    BACK,
+    REDUCE,
+    SPREAD,
     GIVE,
     OWN,
+    HEADS_CORE,
+    HEADS_X,
+    HEADS_Y,
+    HEADS_LINE,
+    HEADS_PAIR,
     VECTORS_W,
     VECTORS_Z,
     VECTORS_Y,
@@ -438,7 +444,7 @@
     OUTPUT,
     INPUT_GRAD,
     LOAD,
-) = range(33)
+) = range(35)
 
 
 def fused_fits(mesh):
@@ -485,13 +491,15 @@
 def scratch_table():
     s = types.SimpleNamespace()
     s.full = [pltpu.VMEM((GROUP, rows, cols), BF) for rows, cols in WEIGHT_SHAPES]
+    s.turned_weight = pltpu.VMEM((3 * SLICE, D), BF)
     s.x = pltpu.VMEM((ROWS, D), BF)
+    s.xt = pltpu.VMEM((CTX, D, ROWS), BF)
     s.teacher = pltpu.VMEM((ROWS, D), BF)
-    s.small = pltpu.VMEM((GROUP, 16, D), F32)
-    s.kv_send = pltpu.VMEM((4, 2 * HW, ROWS), BF)
-    s.kv = pltpu.VMEM((CTX, 2 * HW, ROWS), BF)
-    s.q_send = pltpu.VMEM((4, HW, ROWS), BF)
-    s.q = pltpu.VMEM((4, HW, ROWS), BF)
+    s.small = pltpu.VMEM((GROUP, 16, D), BF)
+    s.vectors = pltpu.VMEM((16, D), F32)
+    s.kt = pltpu.VMEM((CTX, SLICE, ROWS), BF)
+    s.vt = pltpu.VMEM((CTX, SLICE, ROWS), BF)
+    s.qt = pltpu.VMEM((4, SLICE, ROWS), BF)
     s.weights = pltpu.VMEM((CTX, HEADS, ROWS, 4 * ROWS), F32)
     s.mix = pltpu.VMEM((HEADS, HD, 4 * ROWS), F32)
     s.total = pltpu.VMEM((HEADS, 8, 4 * ROWS), F32)
@@ -501,34 +509,41 @@
     s.act = pltpu.VMEM((4, ROWS, D), BF)
     s.first = pltpu.VMEM((ROWS, D), F32)
     s.keep = pltpu.VMEM((ROWS, D), F32)
-    s.x_half = pltpu.VMEM((2, ROWS, 384), BF)
     s.set_half = pltpu.VMEM((2, ROWS, 384), BF)
     s.ag_half = pltpu.VMEM((2, ROWS, 384), BF)
     s.ig_half = pltpu.VMEM((2, ROWS, 1536), BF)
     s.bg = pltpu.VMEM((ROWS, D), BF)
-    s.x_all = pltpu.VMEM((GROUP, ROWS, 384), BF)
     s.set_all = pltpu.VMEM((GROUP, ROWS, 384), BF)
     s.ctx_all = pltpu.VMEM((GROUP, 2, HW, ROWS), BF)
     s.ag_all = pltpu.VMEM((GROUP, ROWS, 384), BF)
     s.ig_all = pltpu.VMEM((GROUP, ROWS, 1536), BF)
     s.act_all = pltpu.VMEM((GROUP, ROWS, D), BF)
     s.bg_all = pltpu.VMEM((GROUP, ROWS, D), BF)
-    s.projected_half = [pltpu.VMEM((2, ROWS, 384), BF) for name in (Q, K, V)]
-    s.projected_all = [pltpu.VMEM((GROUP, ROWS, 384), BF) for name in (Q, K, V)]
     s.cg_send = pltpu.VMEM((4, HW, ROWS), BF)
     s.cg = pltpu.VMEM((4, HW, ROWS), BF)
+    s.wg = pltpu.VMEM((HEADS, HD, 4 * ROWS), BF)
     s.dkv_send = pltpu.VMEM((CTX, 2 * HW, ROWS), BF)
     s.dkv = pltpu.VMEM((CTX, 2 * HW, ROWS), BF)
     s.dq_send = pltpu.VMEM((4, HW, ROWS), BF)
     s.dq = pltpu.VMEM((4, HW, ROWS), BF)
-    s.part = [pltpu.VMEM((rows, cols), BF) for rows, cols in PART_SHAPES]
-    s.pair = [pltpu.VMEM((rows // 2, cols), BF) for rows, cols in PART_SHAPES]
-    s.sum = [pltpu.VMEM((4, rows // 8, cols), BF) for rows, cols in PART_SHAPES]
-    s.line = [pltpu.VMEM((3, rows // 8, cols), BF) for rows, cols in PART_SHAPES]
-    s.done = [pltpu.VMEM((4, rows // 8, cols), BF) for rows, cols in PART_SHAPES]
-    s.wg = pltpu.VMEM((HEADS, HD, 4 * ROWS), BF)
+    s.heads = pltpu.VMEM((2, 2, HW, HEAD_COLS), BF)
+    s.heads_core = pltpu.VMEM((2, HW, HEAD_COLS), BF)
+    s.heads_sum = pltpu.VMEM((2, HW, HEAD_COLS), BF)
+    s.heads_x = pltpu.VMEM((HW, HEAD_COLS), BF)
+    s.heads_row = pltpu.VMEM((2, HW // 2, HEAD_COLS), BF)
+    s.heads_y = pltpu.VMEM((HW // 2, HEAD_COLS), BF)
+    s.heads_done = pltpu.VMEM((4, HW // 2, HEAD_COLS), BF)
+    s.part = {k: pltpu.VMEM((2, r // 2, n), BF) for k, (r, n) in PART_SHAPES.items()}
+    s.got = {
+        k: [pltpu.VMEM((r >> i, n), BF) for i in (1, 2, 3)] for k, (r, n) in PART_SHAPES.items()
+    }
+    s.sum = {
+        k: [pltpu.VMEM((2, r >> i, n), BF) for i in (2, 3)] for k, (r, n) in PART_SHAPES.items()
+    }
+    s.done = {k: pltpu.VMEM((2, 2, 2, r // 8, n), BF) for k, (r, n) in PART_SHAPES.items()}
     s.smalls = pltpu.VMEM((GROUP, 16, HW), F32)
     s.sg = pltpu.VMEM((16, D), F32)
+    s.sg_rows = pltpu.VMEM((16, D), F32)
     s.sg_w = pltpu.VMEM((GROUP, 16, D), F32)
     s.sg_z = pltpu.VMEM((4, 16, D), F32)
     s.sg_y = pltpu.VMEM((2, 16, D), F32)
@@ -537,7 +552,7 @@
 
 
 LOCAL_SEMS = 32
-REMOTE_SEMS = 160
+REMOTE_SEMS = 192
 
 
 def is_memory(item):
@@ -549,13 +564,15 @@
 
 
 def fused_kernel(*refs):
-    (tokens, teacher), own_shards = refs[:2], refs[2:8]
-    small_in, lengths, valid = refs[8:11]
-    output, input_grad_out = refs[11:13]
-    grad_out, smalls_out = refs[13:19], refs[19]
+    (tokens, teacher), shards = refs[:2], refs[2:8]
+    lengths, valid = refs[8:10]
+    biases = refs[10:19]
+    output, input_grad_out = refs[19:21]
+    grad_out, heads_out, smalls_out, rows_out = refs[21:24], refs[24], refs[25], refs[26]
+    grad_out = dict(zip((O, IN, OUT), grad_out))
     flat, shape = scratch_shapes()
-    S = types.SimpleNamespace(**jax.tree.unflatten(shape, refs[20 : 20 + len(flat)]))
-    send_sems, recv_sems, local_sems = refs[20 + len(flat) :]
+    S = types.SimpleNamespace(**jax.tree.unflatten(shape, refs[27 : 27 + len(flat)]))
+    send_sems, recv_sems, local_sems = refs[27 + len(flat) :]
 
     c = lax.axis_index("ctx")
     w = lax.axis_index("wsh")
@@ -603,52 +620,87 @@
     peers += [(bit_xor(c, j), w) for j in range(1, CTX)]
     peers += [(bit_xor(c, 1), bit_xor(w, 1))]
 
-    loads = {
-        TOKENS: local(TOKENS, tokens.at[0], S.x),
-        TEACHER: local(TEACHER, teacher.at[0], S.teacher),
-        SMALL: local(SMALL, small_in, S.small.at[w]),
-    }
-    for name in range(6):
-        loads[(LOAD, name)] = local((LOAD, name), own_shards[name], S.full[name].at[w])
+    def bit(value, mask):
+        return (value // mask) % 2
+
+    first_col = pl.multiple_of((3 * a) // 2 * 128, 128)
+    first_row = pl.multiple_of(a % 2 * 64, 64)
+
+    def shard(name):
+        if name < PART_Q:
+            return shards[name]
+        return shards[name - PART_Q].at[:, pl.ds(first_col, SLICE)]
+
+    loads = {TOKENS: local(TOKENS, tokens.at[0], S.x)}
+    for name in (PART_K, PART_V, PART_Q, O, IN, OUT, K, V, Q):
+        loads[name] = local((LOAD, name), shard(name), S.full[name].at[w])
+    loads[TEACHER] = local(TEACHER, teacher.at[0], S.teacher)
 
     barrier = pltpu.get_barrier_semaphore()
     for c_to, w_to in peers:
         pl.semaphore_signal(
             barrier, inc=1, device_id={"ctx": c_to, "wsh": w_to}, device_id_type=MESH
         )
+    loads[TOKENS].wait()
+    x_low = S.x[...]
+    S.xt[c] = x_low.T
+    bias_rows = [row[...].astype(F32).reshape(1, HW) for row in biases[:8]]
+    tall = jnp.concatenate(bias_rows, axis=0)
+    valid_high = (valid[0] // 64).astype(F32)
+    valid_low = (valid[0] % 64).astype(F32)
+    wide_rows = [biases[8][...].astype(F32).reshape(1, D)]
+    wide_rows += [jnp.full((1, D), 64.0, F32) * valid_high, jnp.full((1, D), 1.0, F32) * valid_low]
+    wide_rows += [jnp.zeros((5, D), F32)]
+    S.small[w, :, 0:HW] = jnp.concatenate(
+        [tall, jnp.concatenate(wide_rows, axis=0)[:, 0:HW]], axis=0
+    ).astype(BF)
+    S.small[w, 8:16, HW:D] = jnp.concatenate(wide_rows, axis=0)[:, HW:D].astype(BF)
+
     pl.semaphore_wait(barrier, len(peers))
-
-    for j in (1, 2, 3):
-        remote((SMALL, j), small_in, S.small.at[w], c, bit_xor(w, j))
 
     def half_of(name, which):
         rows = WEIGHT_SHAPES[name][0] // 2
         return pl.ds(pl.multiple_of(which * rows, rows), rows)
 
-    order = (K, V, Q, O, IN, OUT)
-    for name in order:
-        full = S.full[name]
-        own = half_of(name, b)
-        remote((WEIGHT_X, name), own_shards[name].at[own], full.at[w, own], c, bit_xor(w, 2))
-        remote((WEIGHT_CORE, name), own_shards[name], full.at[w], c, bit_xor(w, 1))
+    def mine(name):
+        return bit(c, SECOND_WAY[name])
+
+    def send_weight(name):
+        full, own = S.full[name], half_of(name, mine(name))
+        if name < PART_Q:
+            half = shard(name).at[own]
+        else:
+            half = shards[name - PART_Q].at[own, pl.ds(first_col, SLICE)]
+        remote((WEIGHT_X, name), half, full.at[w, own], c, bit_xor(w, 2))
+        remote((WEIGHT_CORE, name), shard(name), full.at[w], c, bit_xor(w, 1))
+
+    for name in (PART_K, PART_V, PART_Q):
+        send_weight(name)
+    for j in (1, 2, 3):
+        remote((SMALL, j), S.small.at[w], S.small.at[w], c, bit_xor(w, j))
+    remote((X_PAIR,), S.xt.at[c], S.xt.at[c], bit_xor(c, 1), w, 0, 4)
+    for j in (1, 2, 3):
+        remote((X_LINE, j), S.xt.at[c], S.xt.at[c], bit_xor(c, 2 * j), w)
+    for name in (O, IN, OUT, K, V, Q):
+        send_weight(name)
 
     def pump_x(name):
-        slot = S.full[name].at[bit_xor(w, 2), half_of(name, b)]
+        slot = S.full[name].at[bit_xor(w, 2), half_of(name, mine(name))]
         arrived((WEIGHT_X, name), slot)
-        remote((WEIGHT_Y, name), slot, slot, bit_xor(c, 1), w)
+        remote((WEIGHT_SECOND, name), slot, slot, bit_xor(c, SECOND_WAY[name]), w)
         remote((WEIGHT_CORE_X, name), slot, slot, c, bit_xor(w, 1))
 
-    def pump_y(name):
-        slot = S.full[name].at[bit_xor(w, 2), half_of(name, 1 - b)]
-        arrived((WEIGHT_Y, name), slot)
-        remote((WEIGHT_CORE_Y, name), slot, slot, c, bit_xor(w, 1))
+    def pump_second(name):
+        slot = S.full[name].at[bit_xor(w, 2), half_of(name, 1 - mine(name))]
+        arrived((WEIGHT_SECOND, name), slot)
+        remote((WEIGHT_CORE_SECOND, name), slot, slot, c, bit_xor(w, 1))
 
     def weight_ready(name):
         full = S.full[name]
-        loads[(LOAD, name)].wait()
+        loads[name].wait()
         arrived((WEIGHT_CORE, name), full.at[bit_xor(w, 1)])
-        arrived((WEIGHT_CORE_X, name), full.at[bit_xor(w, 3), half_of(name, b)])
-        arrived((WEIGHT_CORE_Y, name), full.at[bit_xor(w, 3), half_of(name, 1 - b)])
+        arrived((WEIGHT_CORE_X, name), full.at[bit_xor(w, 3), half_of(name, mine(name))])
+        arrived((WEIGHT_CORE_SECOND, name), full.at[bit_xor(w, 3), half_of(name, 1 - mine(name))])
 
     def square(name):
         return S.full[name][...].reshape(D, D)
@@ -673,51 +725,66 @@
 
     own_live = c * ROWS + lax.broadcasted_iota(jnp.int32, (ROWS, 1), 0) < limit
 
-    loads[TOKENS].wait()
-    x_low = S.x[...]
-    for i in range(2):
-        S.x_half[i] = x_low[:, 384 * i : 384 * (i + 1)]
-
-    loads[SMALL].wait()
+    def block_on(j, pair):
+        if isinstance(j, int):
+            return 2 * bit_xor(a, j) + pair
+        low = (a % 2 + j % 2) % 2
+        high = (a // 2 + j // 2) % 2
+        return 2 * (2 * high + low) + pair
+
+    def pass_on(j):
+        block = S.xt.at[block_on(j, b)]
+        arrived((X_LINE, j), block)
+        remote((X_PAIR,), block, block, bit_xor(c, 1), w, j, 4)
+
+    pump_x(PART_K)
+    pump_x(PART_V)
+    pump_x(PART_Q)
     for j in (1, 2, 3):
         arrived((SMALL, j), S.small.at[bit_xor(w, j)])
-    small = (S.small[0] + S.small[1]) + (S.small[2] + S.small[3])
+    S.vectors[0:8, :] = jnp.concatenate(
+        [S.small[i, 0:8, 0:HW].astype(F32) for i in range(GROUP)], axis=1
+    )
+    small = [S.small[i, 8:16, :].astype(F32) for i in range(GROUP)]
+    S.vectors[8:16, :] = jnp.concatenate(
+        [part[0:1] for part in small]
+        + [sum(part[1:2] + part[2:3] for part in small), jnp.zeros((3, D), F32)],
+        axis=0,
+    )
 
     def vector(row):
-        return small[row : row + 1, :]
-
-    def project(name, bias):
-        value = matmul(x_low, square(name))
-        if bias is not None:
-            value = value + vector(bias)
-        return value.T.astype(BF)
-
-    pump_x(K)
-    pump_x(V)
-    pump_y(K)
-    weight_ready(K)
-    turned = project(K, None)
-    for i in range(4):
-        S.kv_send[i, 0:HW, :] = turned[HW * i : HW * (i + 1), :]
-    pump_x(Q)
-    pump_y(V)
-    weight_ready(V)
-    turned = project(V, 1)
-    for i in range(4):
-        S.kv_send[i, HW : 2 * HW, :] = turned[HW * i : HW * (i + 1), :]
-    for j in range(1, CTX):
-        to = bit_xor(c, j)
-        remote((KEY_VALUE, j), S.kv_send.at[to // 2], S.kv.at[c], to, w)
-    S.kv[c] = S.kv_send[a]
+        return S.vectors[row : row + 1, :]
+
+    def tall_bias(row):
+        return jnp.broadcast_to(S.vectors[row : row + 1, pl.ds(first_col, SLICE)], (8, SLICE)).T[
+            :, 0:1
+        ]
+
+    pass_on(1)
+    pump_second(PART_K)
+    pump_second(PART_V)
+    pump_second(PART_Q)
+    pass_on(2)
+    for i, name in enumerate((PART_Q, PART_K, PART_V)):
+        weight_ready(name)
+        S.turned_weight[SLICE * i : SLICE * (i + 1), :] = S.full[name][...].reshape(D, SLICE).T
+    query_bias, value_bias = tall_bias(0), tall_bias(1)
+
+    def project(block):
+        both = matmul(S.turned_weight[SLICE : 3 * SLICE, :], S.xt[block])
+        S.kt[block] = both[0:SLICE].astype(BF)
+        S.vt[block] = (both[SLICE : 2 * SLICE] + value_bias).astype(BF)
+
+    def project_queries(j):
+        block = block_on(j, b)
+        queries = matmul(S.turned_weight[0:SLICE, :], S.xt[block]) + query_bias
+        S.qt[block // 2] = queries.astype(BF)
+
+    for j in (0, 1, 2):
+        project_queries(j)
     pump_x(O)
-    pump_y(Q)
-    weight_ready(Q)
-    turned = project(Q, 0)
-    for i in range(4):
-        S.q_send[i] = turned[HW * i : HW * (i + 1), :]
-    for j in (1, 2, 3):
-        remote((QUERY, j), S.q_send.at[bit_xor(a, j)], S.q.at[a], bit_xor(c, 2 * j), w)
-    S.q[a] = S.q_send[a]
+    pass_on(3)
+    project_queries(3)
 
     def to_group(key, source_of, everywhere):
         for j in (1, 2, 3):
@@ -728,38 +795,44 @@
         for j in (1, 2, 3):
             arrived((*key, j), everywhere.at[bit_xor(w, j)])
 
-    to_group((X_ALL,), lambda to: S.x_half.at[to // 2], S.x_all)
-    S.x_all[w] = S.x_half[x]
-
-    pump_x(IN)
-    pump_y(O)
-
-    for j in (1, 2, 3):
-        arrived((QUERY, j), S.q.at[bit_xor(a, j)])
-    for j in range(1, CTX):
-        arrived((KEY_VALUE, j), S.kv.at[bit_xor(c, j)])
-
     score_scale = 1.0 / math.sqrt(HD)
 
+    def head(ref, block, h):
+        return ref[block, pl.ds(first_row + HD * h, HD), :]
+
+    def wide_queries(h):
+        return jnp.concatenate([head(S.qt, i, h) for i in range(4)], axis=1)
+
     def wide(ref, h):
-        return jnp.concatenate(
-            [ref[i, HD * h : HD * (h + 1), :] for i in range(4)], axis=1
-        )
+        return jnp.concatenate([ref[i, HD * h : HD * (h + 1), :] for i in range(4)], axis=1)
 
     S.mix[...] = jnp.zeros(S.mix.shape, F32)
     S.total[...] = jnp.zeros(S.total.shape, F32)
 
-    @pl.loop(0, CTX)
     def attend_block(block):
+        project(block)
         allowed = key_code(block) == query_code
         for h in range(HEADS):
-            key_t = S.kv[block, HD * h : HD * (h + 1), :]
-            value_t = S.kv[block, HW + HD * h : HW + HD * (h + 1), :]
-            scores = tn(key_t, wide(S.q, h)) * score_scale
+            scores = tn(head(S.kt, block, h), wide_queries(h)) * score_scale
             weights = jnp.exp(jnp.where(allowed, scores, MASKED))
             S.weights[block, h] = weights
             S.total[h, 0:1, :] += jnp.sum(weights, axis=0, keepdims=True)
-            S.mix[h] += matmul(value_t, weights.astype(BF))
+            S.mix[h] += matmul(head(S.vt, block, h), weights.astype(BF))
+
+    @pl.loop(0, 4)
+    def attend_line(j):
+        attend_block(block_on(j, b))
+
+    pump_second(O)
+    pump_x(IN)
+    pair_base = numbers.take((X_PAIR,), 4)
+
+    @pl.loop(0, 4)
+    def attend_pair(j):
+        block = block_on(j, 1 - b)
+        landing = S.xt.at[block]
+        pltpu.make_async_copy(landing, landing, recv_sems.at[pair_base + j]).wait()
+        attend_block(block)
 
     for h in range(HEADS):
         context_t = (S.mix[h] / S.total[h, 0:1, :]).astype(BF)
@@ -769,8 +842,8 @@
         to = bit_xor(a, j)
         remote((CONTEXT, j), S.ctx_send.at[to], S.ctx.at[a], bit_xor(c, 2 * j), w)
     S.ctx[a] = S.ctx_send[a]
+    pump_second(IN)
     pump_x(OUT)
-    pump_y(IN)
     weight_ready(O)
     for j in (1, 2, 3):
         arrived((CONTEXT, j), S.ctx.at[bit_xor(a, j)])
@@ -788,8 +861,8 @@
         S.set_half[i] = settled_low[:, 384 * i : 384 * (i + 1)]
     to_group((SETTLED_ALL,), lambda to: S.set_half.at[to // 2], S.set_all)
     S.set_all[w] = S.set_half[x]
-    pump_y(OUT)
     weight_ready(IN)
+    pump_second(OUT)
     for t in range(4):
         w_part = S.full[IN][:, :, D * t : D * (t + 1)].reshape(D, D)
         inner = matmul(settled_low, w_part) + vector(8 + t)
@@ -824,6 +897,8 @@
     d_second = norm_back(upstream * vector(6), normal_two, inverse_two)
     branch_grad = d_second.astype(BF)
     S.bg[...] = branch_grad
+    for name in (K, V, Q):
+        pump_x(name)
     to_group((BRANCH_GRAD_ALL,), lambda to: S.bg, S.bg_all)
     S.bg_all[w] = branch_grad
     note(5, branch_grad)
@@ -841,6 +916,8 @@
         note(8 + t, inner_grad)
         w_part = S.full[IN][:, :, D * t : D * (t + 1)].reshape(D, D)
         d_settled = d_settled + right_product(inner_grad, w_part)
+    for name in (K, V, Q):
+        pump_second(name)
     to_group((INNER_GRAD_ALL,), lambda to: S.ig_half.at[to % 2], S.ig_all)
     S.ig_all[w] = S.ig_half[core]
     normal_one = S.first[...]
@@ -862,71 +939,71 @@
     to_group((ATTN_GRAD_ALL,), lambda to: S.ag_half.at[to % 2], S.ag_all)
     S.ag_all[w] = S.ag_half[core]
 
-    def reduce_pair(name):
-        half = PART_SHAPES[name][0] // 2
-        there = pl.ds(pl.multiple_of((1 - b) * half, half), half)
-        remote((PAIR, name), S.part[name].at[there], S.pair[name], bit_xor(c, 1), w)
-
-    def reduce_line(name):
-        rows, cols = PART_SHAPES[name]
-        half = rows // 2
-        arrived((PAIR, name), S.pair[name])
-        here = pl.ds(pl.multiple_of(b * half, half), half)
-        both = S.part[name][here, :].astype(F32) + S.pair[name][...].astype(F32)
-        S.sum[name][...] = both.astype(BF).reshape(4, rows // 8, cols)
-        for j in (1, 2, 3):
-            remote(
-                (LINE, name, j),
-                S.sum[name].at[bit_xor(a, j)],
-                S.line[name].at[j - 1],
-                bit_xor(c, 2 * j),
-                w,
-            )
-
-    def spread_line(name):
-        for j in (1, 2, 3):
-            arrived((LINE, name, j), S.line[name].at[j - 1])
-        total = S.sum[name][a].astype(F32)
-        for j in range(3):
-            total = total + S.line[name][j].astype(F32)
-        done = S.done[name]
-        done[a] = total.astype(BF)
-        for j in (1, 2, 3):
-            remote((BACK, name, j), done.at[a], done.at[a], bit_xor(c, 2 * j), w)
-
-    def spread_pair(name):
-        done, out = S.done[name], grad_out[name]
-        for j in (1, 2, 3):
-            arrived((BACK, name, j), done.at[bit_xor(a, j)])
+    def reduce_send(name, stage):
+        mask = HALVING[name][stage]
+        source = S.part[name] if stage == 0 else S.sum[name][stage - 1]
+        there = source.at[1 - bit(c, mask)]
+        remote((REDUCE, name, stage), there, S.got[name][stage], bit_xor(c, mask), w)
+
+    def slot(name):
+        return [bit(c, mask) for mask in HALVING[name]]
+
+    def reduce_add(name, stage):
+        source = S.part[name] if stage == 0 else S.sum[name][stage - 1]
+        got = S.got[name][stage]
+        arrived((REDUCE, name, stage), got)
+        total = source[bit(c, HALVING[name][stage])].astype(F32) + got[...].astype(F32)
+        if stage == 2:
+            i, j, k = slot(name)
+            S.done[name][i, j, k] = total.astype(BF)
+        else:
+            rows, cols = PART_SHAPES[name]
+            S.sum[name][stage][...] = total.astype(BF).reshape(2, rows >> (stage + 2), cols)
+
+    def spread_send(name, stage):
+        i, j, k = slot(name)
+        part = S.done[name].at[i, j, k] if stage == 2 else S.done[name].at[i, j]
+        remote((SPREAD, name, stage), part, part, bit_xor(c, HALVING[name][stage]), w)
+
+    def spread_wait(name, stage):
+        i, j, k = slot(name)
+        part = S.done[name].at[i, j, 1 - k] if stage == 2 else S.done[name].at[i, 1 - j]
+        arrived((SPREAD, name, stage), part)
+
+    def give(name):
+        mask = HALVING[name][0]
+        half = bit(c, mask)
+        done, out = S.done[name].at[half], grad_out[name]
         if name == OUT:
-            remote((GIVE, name), done, out.at[b], bit_xor(c, 1), w)
-            finishing.append(local((GIVE, name), done, out.at[b]))
+            remote((GIVE, name), done, out.at[half], bit_xor(c, mask), w)
+            finishing.append(local((GIVE, name), done, out.at[half]))
             return
-        remote((GIVE, name), done, out.at[core], bit_xor(c, 1), 2 * x + b, core, 2)
-
-        @pl.when(core == b)
+        remote((GIVE, name), done, out.at[core], bit_xor(c, mask), 2 * x + half, core, 2)
+
+        @pl.when(core == half)
         def keep_own():
             local((OWN, name), done, out.at[core])
 
-        @pl.when(core != b)
+        @pl.when(core != half)
         def give_core():
             remote((OWN, name), done, out.at[core], c, bit_xor(w, 1))
             started.pop()
 
     def settle(name):
-        done, out = S.done[name], grad_out[name]
+        half = bit(c, HALVING[name][0])
+        done, out = S.done[name].at[half], grad_out[name]
         if name == OUT:
-            arrived((GIVE, name), out.at[1 - b])
+            arrived((GIVE, name), out.at[1 - half])
             return
 
-        @pl.when(core == b)
+        @pl.when(core == half)
         def from_chip():
             pltpu.make_async_copy(
                 done, out.at[core], local_sems.at[locals_.take((OWN, name))]
             ).wait()
             arrived((OWN, name), out.at[1 - core])
 
-        @pl.when(core != b)
+        @pl.when(core != half)
         def from_partner():
             arrived((GIVE, name), out.at[0], 0)
             arrived((GIVE, name), out.at[1], 1)
@@ -935,10 +1012,12 @@
 
     from_group((ACTIVATED_ALL,), S.act_all)
     from_group((BRANCH_GRAD_ALL,), S.bg_all)
-    S.part[OUT][...] = tn(
-        S.act_all[...].reshape(GROUP * ROWS, D), S.bg_all[...].reshape(GROUP * ROWS, D)
-    ).astype(BF)
-    reduce_pair(OUT)
+    S.part[OUT][...] = (
+        tn(S.act_all[...].reshape(GROUP * ROWS, D), S.bg_all[...].reshape(GROUP * ROWS, D))
+        .astype(BF)
+        .reshape(2, D // 2, D)
+    )
+    reduce_send(OUT, 0)
 
     for j in (1, 2, 3):
         arrived((CONTEXT_GRAD, j), S.cg.at[bit_xor(a, j)])
@@ -956,15 +1035,13 @@
         for h in range(HEADS):
             key_rows = slice(HD * h, HD * (h + 1))
             value_rows = slice(HW + HD * h, HW + HD * (h + 1))
-            key_t = S.kv[block, key_rows, :]
-            value_t = S.kv[block, value_rows, :]
             weights = S.weights[block, h]
             grad = S.wg[h]
-            weight_grad = tn(value_t, grad) + S.total[h, 1:2, :]
+            weight_grad = tn(head(S.vt, block, h), grad) + S.total[h, 1:2, :]
             score_grad = (weights * weight_grad).astype(BF)
-            S.mix[h] += matmul(key_t, score_grad)
+            S.mix[h] += matmul(head(S.kt, block, h), score_grad)
             S.dkv_send[block, key_rows, :] = (
-                right_product(wide(S.q, h), score_grad) * score_scale
+                right_product(wide_queries(h), score_grad) * score_scale
             ).astype(BF)
             S.dkv_send[block, value_rows, :] = right_product(grad, weights.astype(BF)).astype(BF)
 
@@ -981,98 +1058,136 @@
         remote((QUERY_GRAD, j), S.dq_send.at[to], S.dq.at[a], bit_xor(c, 2 * j), w)
     S.dq[a] = S.dq_send[a]
 
+    def lanes(ref, pair):
+        return jnp.concatenate([ref[2 * i + pair] for i in range(4)], axis=1)
+
+    own_grads = jnp.concatenate(
+        [
+            lanes(S.dkv_send, b),
+            jnp.concatenate([S.dq_send[i] for i in range(4)], axis=1),
+            jnp.zeros((HEAD_COLS - 3 * HW, 4 * ROWS), BF),
+        ],
+        axis=0,
+    )
+    other = right_product(lanes(S.xt, 1 - b), lanes(S.dkv_send, 1 - b))
+    heads = right_product(lanes(S.xt, b), own_grads)
+    heads = jnp.concatenate([heads[:, : 2 * HW] + other, heads[:, 2 * HW :]], axis=1).astype(BF)
+    S.heads[...] = heads.reshape(2, 2, HW, HEAD_COLS)
+    for i in range(2):
+        remote((HEADS_CORE, i), S.heads.at[i, 1 - core], S.heads_core.at[i], c, bit_xor(w, 1))
+
     from_group((SETTLED_ALL,), S.set_all)
     from_group((INNER_GRAD_ALL,), S.ig_all)
-    S.part[IN][...] = tn(
-        S.set_all[...].reshape(GROUP * ROWS, 384), S.ig_all[...].reshape(GROUP * ROWS, 1536)
-    ).astype(BF)
-    reduce_pair(IN)
-    reduce_line(OUT)
+    S.part[IN][...] = (
+        tn(S.set_all[...].reshape(GROUP * ROWS, 384), S.ig_all[...].reshape(GROUP * ROWS, 1536))
+        .astype(BF)
+        .reshape(2, HW, 1536)
+    )
+    reduce_send(IN, 0)
+    for i in range(2):
+        arrived((HEADS_CORE, i), S.heads_core.at[i])
+        S.heads_sum[i] = (S.heads[i, core].astype(F32) + S.heads_core[i].astype(F32)).astype(BF)
+    remote((HEADS_X,), S.heads_sum.at[1 - x], S.heads_x, c, bit_xor(w, 2))
+    reduce_add(OUT, 0)
+    reduce_send(OUT, 1)
     from_group((CONTEXT_ALL,), S.ctx_all)
     from_group((ATTN_GRAD_ALL,), S.ag_all)
     context_all = jnp.concatenate(
         [S.ctx_all[i].reshape(384, ROWS) for i in range(GROUP)], axis=1
     )
-    S.part[O][...] = matmul(context_all, S.ag_all[...].reshape(GROUP * ROWS, 384)).astype(BF)
-    reduce_pair(O)
-    reduce_line(IN)
-    from_group((X_ALL,), S.x_all)
-
+    S.part[O][...] = (
+        matmul(context_all, S.ag_all[...].reshape(GROUP * ROWS, 384)).astype(BF).reshape(2, HW, 384)
+    )
+    reduce_send(O, 0)
+    arrived((HEADS_X,), S.heads_x)
+    S.heads_row[...] = (
+        (S.heads_sum[x].astype(F32) + S.heads_x[...].astype(F32))
+        .astype(BF)
+        .reshape(2, HW // 2, HEAD_COLS)
+    )
+    remote((HEADS_Y,), S.heads_row.at[1 - b], S.heads_y, bit_xor(c, 1), w)
+    reduce_add(OUT, 1)
+    reduce_send(OUT, 2)
+    reduce_add(IN, 0)
+    reduce_send(IN, 1)
+    reduce_add(OUT, 2)
+    spread_send(OUT, 2)
+    arrived((HEADS_Y,), S.heads_y)
+    S.heads_done[a] = (S.heads_row[b].astype(F32) + S.heads_y[...].astype(F32)).astype(BF)
+    for j in (1, 2, 3):
+        remote((HEADS_LINE, j), S.heads_done.at[a], S.heads_done.at[a], bit_xor(c, 2 * j), w)
+
+    for name in (K, V, Q):
+        weight_ready(name)
     for j in range(1, CTX):
         arrived((KEY_VALUE_GRAD, j), S.dkv.at[bit_xor(c, j)])
     for j in (1, 2, 3):
         arrived((QUERY_GRAD, j), S.dq.at[bit_xor(a, j)])
 
-    def summed(first_row):
+    def summed(first):
         parts = []
         for i in range(4):
-            rows = slice(first_row, first_row + HW)
+            rows = slice(first, first + HW)
             both = S.dkv[2 * i, rows, :].astype(F32) + S.dkv[2 * i + 1, rows, :].astype(F32)
             parts.append(both)
         return jnp.concatenate(parts, axis=0).T.astype(BF)
 
-    grads = {
-        V: summed(HW),
-        K: summed(0),
-        Q: S.dq[...].reshape(D, ROWS).T,
-    }
+    grads = {V: summed(HW), K: summed(0), Q: S.dq[...].reshape(D, ROWS).T}
     note(1, grads[V])
     note(0, grads[Q])
-    for name in (V, K, Q):
-        for i in range(2):
-            S.projected_half[name][i] = grads[name][:, 384 * i : 384 * (i + 1)]
-        half = S.projected_half[name]
-        to_group((PROJECTED_GRAD_ALL, name), lambda to: half.at[to % 2], S.projected_all[name])
-        S.projected_all[name][w] = half[core]
     for j in (1, 2, 3):
         remote((VECTORS_W, j), S.sg, S.sg_w.at[w], c, bit_xor(w, j))
     S.sg_w[w] = S.sg[...]
-
     input_grad = S.keep[...]
     for name in (Q, K, V):
         input_grad = input_grad + right_product(grads[name], square(name))
     S.first[...] = input_grad
     finishing.append(local(INPUT_GRAD, S.first, input_grad_out))
 
-    x_all = S.x_all[...].reshape(GROUP * ROWS, 384)
-    spread_line(OUT)
-    for name in (V, K, Q):
-        from_group((PROJECTED_GRAD_ALL, name), S.projected_all[name])
-        S.part[name][...] = tn(
-            x_all, S.projected_all[name][...].reshape(GROUP * ROWS, 384)
-        ).astype(BF)
-        reduce_pair(name)
-    reduce_line(O)
-    spread_line(IN)
+    reduce_add(IN, 1)
+    reduce_send(IN, 2)
+    spread_wait(OUT, 2)
+    spread_send(OUT, 1)
+    reduce_add(O, 0)
+    reduce_send(O, 1)
+    reduce_add(IN, 2)
+    spread_send(IN, 2)
     for j in (1, 2, 3):
         arrived((VECTORS_W, j), S.sg_w.at[bit_xor(w, j)])
     S.sg_z[a] = (S.sg_w[0] + S.sg_w[1]) + (S.sg_w[2] + S.sg_w[3])
     for j in (1, 2, 3):
         remote((VECTORS_Z, j), S.sg_z.at[a], S.sg_z.at[a], bit_xor(c, 2 * j), w)
-    spread_pair(OUT)
-    reduce_line(V)
-    spread_line(O)
-    reduce_line(K)
-    spread_pair(IN)
-    reduce_line(Q)
+    reduce_add(O, 1)
+    reduce_send(O, 2)
+    spread_wait(OUT, 1)
+    give(OUT)
+    spread_wait(IN, 2)
+    spread_send(IN, 1)
+    for j in (1, 2, 3):
+        arrived((HEADS_LINE, j), S.heads_done.at[bit_xor(a, j)])
+    remote((HEADS_PAIR,), S.heads_done, heads_out.at[b], bit_xor(c, 1), w)
+    finishing.append(local((HEADS_PAIR,), S.heads_done, heads_out.at[b]))
+    reduce_add(O, 2)
+    spread_send(O, 2)
     for j in (1, 2, 3):
         arrived((VECTORS_Z, j), S.sg_z.at[bit_xor(a, j)])
     S.sg_y[b] = (S.sg_z[0] + S.sg_z[1]) + (S.sg_z[2] + S.sg_z[3])
     remote(VECTORS_Y, S.sg_y.at[b], S.sg_y.at[b], bit_xor(c, 1), w)
-    spread_line(V)
-    spread_pair(O)
-    spread_line(K)
-    spread_line(Q)
-    spread_pair(V)
-    spread_pair(K)
+    spread_wait(IN, 1)
+    give(IN)
+    spread_wait(O, 2)
+    spread_send(O, 1)
     arrived(VECTORS_Y, S.sg_y.at[1 - b])
     everything = S.sg_y[0] + S.sg_y[1]
+    S.sg_rows[...] = everything
     for i in range(4):
         S.smalls[i] = everything[:, HW * i : HW * (i + 1)]
     finishing.append(local(VECTORS_Y, S.smalls, smalls_out))
-    spread_pair(Q)
-
-    for name in range(6):
+    finishing.append(local(VECTORS_Z, S.sg_rows, rows_out))
+    spread_wait(O, 1)
+    give(O)
+    arrived((HEADS_PAIR,), heads_out.at[1 - b])
+    for name in (OUT, IN, O):
         settle(name)
     for copy in finishing:
         copy.wait()
@@ -1081,26 +1196,34 @@
 
 
 def finish_kernel(*refs):
-    (g_q, g_k, g_v, g_o, g_in, g_out, smalls, output, input_grad) = refs[:9]
-    (r_q, r_k, r_v, r_o, r_in, r_out, vectors, inner_bias, loss, r_output, r_input) = refs[9:]
+    g_o, g_in, g_out, heads, smalls, rows, output, input_grad = refs[:8]
+    r_q, r_k, r_v, r_o, r_in, r_out = refs[8:14]
+    vectors, inner_bias, loss, r_output, r_input = refs[14:22], refs[22], refs[23], refs[24], refs[25]
     step = pl.program_id(0)
-    for source, result in ((g_q, r_q), (g_k, r_k), (g_v, r_v), (g_o, r_o), (g_in, r_in)):
-        width = source.shape[3]
+    for source, result in ((g_o, r_o), (g_in, r_in)):
+        width = source.shape[-1]
+        rest = result.shape[0]
         for i in range(2):
-            result[:, width * i : width * (i + 1)] = source[i, 0].astype(F32)
-    r_out[...] = g_out[0].reshape(HW, D).astype(F32)
+            result[:, width * i : width * (i + 1)] = (
+                source[i].reshape(rest, width).astype(F32)
+            )
+    r_out[...] = g_out[...].reshape(D // 2, D).astype(F32)
+    for i, result in ((0, r_k), (1, r_v), (2, r_q)):
+        result[...] = jnp.concatenate(
+            [heads[0, j, :, HW * i : HW * (i + 1)].astype(F32) for j in range(4)], axis=1
+        )
     r_output[0] = output[...]
     r_input[0] = input_grad[...]
 
     @pl.when(step == 0)
     def once():
         w = lax.axis_index("wsh")
-        vectors[...] = smalls[w, 0:8, :]
-        for i in range(4):
-            inner_bias[0:1, HW * i : HW * (i + 1)] = smalls[i, pl.ds(8 + w, 1), :]
-        error = jnp.sum(smalls[:, 12:13, :])
-        count = jnp.max(smalls[0, 13:14, :])
-        loss[0, 0] = error / (count * D)
+        for i in range(8):
+            vectors[i][...] = smalls[w, i, :]
+        inner_bias[...] = rows[8 + w, :]
+        error = jnp.sum(rows[12:13, :])
+        count = jnp.max(rows[13:14, :])
+        loss[0] = error / (count * D)
 
 
 def fused_body(tokens, teacher, doc_lengths, valid_len, *weights):
@@ -1121,35 +1244,25 @@
         ln2_gain,
         ln2_bias,
     ) = weights
-    w = lax.axis_index("wsh")
-    own = (jnp.arange(GROUP) == w).astype(F32)
-    rows = jnp.stack(
-        [q_bias, v_bias, o_bias, ln1_gain, ln1_bias, out_bias, ln2_gain, ln2_bias]
-    ).astype(F32)
-    rows = (rows[:, None, :] * own[None, :, None]).reshape(8, D)
-    inner_rows = in_bias.astype(F32)[None, :] * own[:, None]
-    valid_row = jnp.broadcast_to(valid_len.astype(F32)[:, None], (1, D))
-    small = jnp.concatenate([rows, inner_rows, valid_row, jnp.zeros((3, D), F32)], axis=0)
-
     hbm = pl.BlockSpec(memory_space=pl.ANY)
     smem = pl.BlockSpec(memory_space=pltpu.SMEM)
+    vmem = pl.BlockSpec(memory_space=pltpu.VMEM)
     low = lambda *shape: jax.ShapeDtypeStruct(shape, BF)
     full = lambda *shape: jax.ShapeDtypeStruct(shape, F32)
-    output, input_grad, g_q, g_k, g_v, g_o, g_in, g_out, smalls = pl.pallas_call(
+    output, input_grad, g_o, g_in, g_out, heads, smalls, rows = pl.pallas_call(
         fused_kernel,
         out_shape=(
             low(ROWS, D),
             full(ROWS, D),
-            low(2, 4, 48, 384),
-            low(2, 4, 48, 384),
-            low(2, 4, 48, 384),
-            low(2, 4, 48, 384),
-            low(2, 4, 48, 1536),
-            low(2, 4, 96, D),
+            low(2, 2, 2, 48, 384),
+            low(2, 2, 2, 48, 1536),
+            low(2, 2, 2, 96, D),
+            low(2, 4, HW // 2, HEAD_COLS),
             full(GROUP, 16, HW),
+            full(16, D),
         ),
-        in_specs=[hbm] * 9 + [smem] * 2,
-        out_specs=[hbm] * 9,
+        in_specs=[hbm] * 8 + [smem] * 2 + [vmem] * 9,
+        out_specs=[hbm] * 8,
         scratch_shapes=scratch_shapes()[0]
         + [
             pltpu.SemaphoreType.DMA((REMOTE_SEMS,)),
@@ -1169,56 +1282,60 @@
         o_weight,
         in_weight,
         out_weight,
-        small,
         doc_lengths,
         valid_len,
-    )
-
-    steps = 4
-    square_in = pl.BlockSpec((2, 1, HW // steps, 384), lambda i: (0, i, 0, 0))
+        q_bias,
+        v_bias,
+        o_bias,
+        ln1_gain,
+        ln1_bias,
+        out_bias,
+        ln2_gain,
+        ln2_bias,
+        in_bias,
+    )
+
+    steps = 2
     square_out = pl.BlockSpec((HW // steps, D), lambda i: (i, 0))
     whole = lambda *shape: pl.BlockSpec(shape, lambda i: (0,) * len(shape))
+    by_row = pl.BlockSpec((ROWS // steps, D), lambda i: (i, 0))
     results = pl.pallas_call(
         finish_kernel,
         grid=(steps,),
-        out_shape=(
-            full(HW, D),
-            full(HW, D),
-            full(HW, D),
-            full(HW, D),
-            full(HW, FF),
-            full(D, D),
-            full(8, HW),
-            full(1, D),
-            full(1, 1),
-            low(1, ROWS, D),
-            full(1, ROWS, D),
-        ),
-        in_specs=[square_in] * 4
-        + [
-            pl.BlockSpec((2, 1, HW // steps, 1536), lambda i: (0, i, 0, 0)),
-            pl.BlockSpec((1, 2, 96, D), lambda i: (i // 2, i % 2, 0, 0)),
+        out_shape=(full(HW, D),) * 4
+        + (full(HW, FF), full(D, D))
+        + (full(HW),) * 8
+        + (full(D), full(1), low(1, ROWS, D), full(1, ROWS, D)),
+        in_specs=[
+            pl.BlockSpec((2, 1, 2, 48, 384), lambda i: (0, i, 0, 0, 0)),
+            pl.BlockSpec((2, 1, 2, 48, 1536), lambda i: (0, i, 0, 0, 0)),
+            pl.BlockSpec((1, 2, 2, 96, D), lambda i: (i, 0, 0, 0, 0)),
+            pl.BlockSpec((1, 4, HW // 2, HEAD_COLS), lambda i: (i, 0, 0, 0)),
             whole(GROUP, 16, HW),
-            pl.BlockSpec((ROWS // steps, D), lambda i: (i, 0)),
-            pl.BlockSpec((ROWS // steps, D), lambda i: (i, 0)),
+            whole(16, D),
+            by_row,
+            by_row,
         ],
         out_specs=[square_out] * 4
         + [
             pl.BlockSpec((HW // steps, FF), lambda i: (i, 0)),
             pl.BlockSpec((D // steps, D), lambda i: (i, 0)),
-            whole(8, HW),
-            whole(1, D),
+        ]
+        + [whole(HW)] * 8
+        + [
+            whole(D),
             pl.BlockSpec(memory_space=pltpu.SMEM),
             pl.BlockSpec((1, ROWS // steps, D), lambda i: (0, i, 0)),
             pl.BlockSpec((1, ROWS // steps, D), lambda i: (0, i, 0)),
         ],
         compiler_params=pltpu.CompilerParams(dimension_semantics=("arbitrary",)),
         name="finish",
-    )(g_q, g_k, g_v, g_o, g_in, g_out, smalls, output, input_grad)
-    r_q, r_k, r_v, r_o, r_in, r_out, vectors, inner_bias, loss, r_output, r_input = results
+    )(g_o, g_in, g_out, heads, smalls, rows, output, input_grad)
+    r_q, r_k, r_v, r_o, r_in, r_out = results[:6]
+    vectors, inner_bias, loss, r_output, r_input = results[6:14], *results[14:]
     return (
         r_output,
-        loss[0, 0],
+        loss.reshape(()),
         r_input,
         r_q,
         vectors[0],
@@ -1230,7 +1347,7 @@
         vectors[3],
         vectors[4],
         r_in,
-        inner_bias[0],
+        inner_bias,
         r_out,
         vectors[5],
         vectors[6],

time: 230 us -> 199 us (0.87)
  the two profiles are of different devices: /device:TPU:17 before, /device:TPU:0 now
where the time goes in v2:
time: 199 us; the launch traced here: 196 us
  Pallas kernels  194 us (97%)
    pallas_call x1, Pallas kernels, fused_body(): pl.pallas_call(fused_kernel, out_shape=(low(ROWS, D), full(ROWS, D), low(...  189 us
    pallas_call x1, Pallas kernels, fused_body(): pl.pallas_call(finish_kernel, grid=(steps,), out_shape=(full(HW, D),) * 4...  5.15 us

profile of v2, /device:TPU:0, one launch (start us, length us, event | category | flops | bytes accessed | tf_op | source)
XLA Modules:
  0.0 195.7 jit_solution(11186060524185198866)
XLA Ops:
  1.3 189.1 %layer.1 = (bf16[128,768]{1,0:T(8,128)(2,1)}, f32[128,768]{1,0:T(8,128)}, bf16[2,2,2,48,384]{4,3,2,1,0:T(8,128)(2,1)}, bf16[2,2,2,48,1536]{4,3,2,1,0:T(8,128)(2,...) custom-call(bf16[1,128,768]{2,1,0:T(8,128)(2,1)} %refs_0_.1, ...), custom_call_target="tpu_custom_call" | custom-call | tf_op jit(solution)/shard_map/layer/pallas_call | solution.py:1252
  190.4 5.1 %finish.1 = (f32[192,768]{1,0:T(8,128)}, f32[192,768]{1,0:T(8,128)}, f32[192,768]{1,0:T(8,128)}, f32[192,768]{1,0:T(8,128)}, f32[192,3072]{1,0:T(8,128)}, /*inde...) custom-call(bf16[2,2,2,48,384]{4,3,2,1,0:T(8,128)(2,1)} %get-tuple-e, ...), custom_call_target="tpu_custom_call" | custom-call | tf_op jit(solution)/shard_map/finish/pallas_call | solution.py:1302

commit v3 on v2

--- a/solution.py
+++ b/solution.py
@@ -403,9 +403,10 @@
 Q, K, V, O, IN, OUT, PART_Q, PART_K, PART_V = range(9)
 SLICE = 256
 WEIGHT_SHAPES = [(192, 768)] * 4 + [(192, 3072), (768, 768)] + [(192, SLICE)] * 3
-SECOND_WAY = {Q: 2, K: 2, V: 2, O: 1, IN: 1, OUT: 2, PART_Q: 1, PART_K: 1, PART_V: 1}
-PART_SHAPES = {O: (384, 384), IN: (384, 1536), OUT: (768, 768)}
-HALVING = {O: (1, 2, 4), IN: (1, 2, 4), OUT: (1, 2, 4)}
+SECOND_WAY = {O: 1, IN: 1, OUT: 2, PART_Q: 1, PART_K: 1, PART_V: 1}
+LOT_O, LOT_IN, LOT_OUT = (0,), (1, 2), (3, 4, 5, 6)
+LOTS = [(96, 384)] + [(4, 48, 384)] * 2 + [(48, D)] * 4
+PIECES = {IN: (1, 4), OUT: (4, 1)}
 HEAD_COLS = 640
 
 (
@@ -416,21 +417,21 @@
     WEIGHT_CORE_X,
     WEIGHT_CORE_SECOND,
     X_LINE,
-    X_PAIR,
+    X_EDGE,
+    KEY_VALUE,
     CONTEXT,
     CONTEXT_GRAD,
     KEY_VALUE_GRAD,
-    QUERY_GRAD,
+    INPUT_PARTS,
     SETTLED_ALL,
     CONTEXT_ALL,
     ATTN_GRAD_ALL,
-    INNER_GRAD_ALL,
-    ACTIVATED_ALL,
     BRANCH_GRAD_ALL,
     REDUCE,
     SPREAD,
     GIVE,
     OWN,
+    GROUP_X,
     HEADS_CORE,
     HEADS_X,
     HEADS_Y,
@@ -490,16 +491,18 @@
 
 def scratch_table():
     s = types.SimpleNamespace()
-    s.full = [pltpu.VMEM((GROUP, rows, cols), BF) for rows, cols in WEIGHT_SHAPES]
-    s.turned_weight = pltpu.VMEM((3 * SLICE, D), BF)
+    s.full = {k: pltpu.VMEM((GROUP, *WEIGHT_SHAPES[k]), BF) for k in SECOND_WAY}
+    s.turned = pltpu.VMEM((SLICE, D), BF)
+    s.head_weight = pltpu.VMEM((3 * HW, D), BF)
+    s.tall_bias = pltpu.VMEM((SLICE, ROWS), F32)
+    s.head_bias = pltpu.VMEM((3 * HW, ROWS), F32)
     s.x = pltpu.VMEM((ROWS, D), BF)
     s.xt = pltpu.VMEM((CTX, D, ROWS), BF)
     s.teacher = pltpu.VMEM((ROWS, D), BF)
     s.small = pltpu.VMEM((GROUP, 16, D), BF)
     s.vectors = pltpu.VMEM((16, D), F32)
-    s.kt = pltpu.VMEM((CTX, SLICE, ROWS), BF)
-    s.vt = pltpu.VMEM((CTX, SLICE, ROWS), BF)
-    s.qt = pltpu.VMEM((4, SLICE, ROWS), BF)
+    s.kv = pltpu.VMEM((CTX, 2 * HW, ROWS), BF)
+    s.q = pltpu.VMEM((4, HW, ROWS), BF)
     s.weights = pltpu.VMEM((CTX, HEADS, ROWS, 4 * ROWS), F32)
     s.mix = pltpu.VMEM((HEADS, HD, 4 * ROWS), F32)
     s.total = pltpu.VMEM((HEADS, 8, 4 * ROWS), F32)
@@ -509,23 +512,24 @@
     s.act = pltpu.VMEM((4, ROWS, D), BF)
     s.first = pltpu.VMEM((ROWS, D), F32)
     s.keep = pltpu.VMEM((ROWS, D), F32)
-    s.set_half = pltpu.VMEM((2, ROWS, 384), BF)
+    s.set_low = pltpu.VMEM((ROWS, D), BF)
     s.ag_half = pltpu.VMEM((2, ROWS, 384), BF)
-    s.ig_half = pltpu.VMEM((2, ROWS, 1536), BF)
     s.bg = pltpu.VMEM((ROWS, D), BF)
-    s.set_all = pltpu.VMEM((GROUP, ROWS, 384), BF)
+    s.set_all = pltpu.VMEM((GROUP, ROWS, D), BF)
     s.ctx_all = pltpu.VMEM((GROUP, 2, HW, ROWS), BF)
     s.ag_all = pltpu.VMEM((GROUP, ROWS, 384), BF)
-    s.ig_all = pltpu.VMEM((GROUP, ROWS, 1536), BF)
-    s.act_all = pltpu.VMEM((GROUP, ROWS, D), BF)
+    s.inner_all = pltpu.VMEM((GROUP * ROWS, D), F32)
+    s.act_all = pltpu.VMEM((GROUP * ROWS, D), BF)
     s.bg_all = pltpu.VMEM((GROUP, ROWS, D), BF)
     s.cg_send = pltpu.VMEM((4, HW, ROWS), BF)
     s.cg = pltpu.VMEM((4, HW, ROWS), BF)
     s.wg = pltpu.VMEM((HEADS, HD, 4 * ROWS), BF)
-    s.dkv_send = pltpu.VMEM((CTX, 2 * HW, ROWS), BF)
-    s.dkv = pltpu.VMEM((CTX, 2 * HW, ROWS), BF)
-    s.dq_send = pltpu.VMEM((4, HW, ROWS), BF)
-    s.dq = pltpu.VMEM((4, HW, ROWS), BF)
+    s.dkv = pltpu.VMEM((2, 4, 2 * HW, ROWS), BF)
+    s.dkv_pair = pltpu.VMEM((4, 2 * HW, ROWS), BF)
+    s.grads = pltpu.VMEM((HEAD_COLS, 4 * ROWS), BF)
+    s.dx_send = pltpu.VMEM((4, ROWS, D), BF)
+    s.dx = pltpu.VMEM((4, ROWS, D), BF)
+    s.column = pltpu.VMEM((D, ROWS), F32)
     s.heads = pltpu.VMEM((2, 2, HW, HEAD_COLS), BF)
     s.heads_core = pltpu.VMEM((2, HW, HEAD_COLS), BF)
     s.heads_sum = pltpu.VMEM((2, HW, HEAD_COLS), BF)
@@ -533,14 +537,14 @@
     s.heads_row = pltpu.VMEM((2, HW // 2, HEAD_COLS), BF)
     s.heads_y = pltpu.VMEM((HW // 2, HEAD_COLS), BF)
     s.heads_done = pltpu.VMEM((4, HW // 2, HEAD_COLS), BF)
-    s.part = {k: pltpu.VMEM((2, r // 2, n), BF) for k, (r, n) in PART_SHAPES.items()}
-    s.got = {
-        k: [pltpu.VMEM((r >> i, n), BF) for i in (1, 2, 3)] for k, (r, n) in PART_SHAPES.items()
-    }
-    s.sum = {
-        k: [pltpu.VMEM((2, r >> i, n), BF) for i in (2, 3)] for k, (r, n) in PART_SHAPES.items()
-    }
-    s.done = {k: pltpu.VMEM((2, 2, 2, r // 8, n), BF) for k, (r, n) in PART_SHAPES.items()}
+    s.part = [pltpu.VMEM((2, 2, *shape), BF) for shape in LOTS]
+    s.got = [
+        [pltpu.VMEM((2, *shape), BF), pltpu.VMEM((2, *shape), BF), pltpu.VMEM(shape, BF)]
+        for shape in LOTS
+    ]
+    s.sum = [[pltpu.VMEM((2, *shape), BF), pltpu.VMEM((2, *shape), BF)] for shape in LOTS]
+    s.own = {lot: pltpu.VMEM(LOTS[lot], BF) for lot in LOT_IN}
+    s.done = [pltpu.VMEM((2, 2, *shape), BF) for shape in LOTS]
     s.smalls = pltpu.VMEM((GROUP, 16, HW), F32)
     s.sg = pltpu.VMEM((16, D), F32)
     s.sg_rows = pltpu.VMEM((16, D), F32)
@@ -552,7 +556,7 @@
 
 
 LOCAL_SEMS = 32
-REMOTE_SEMS = 192
+REMOTE_SEMS = 240
 
 
 def is_memory(item):
@@ -568,11 +572,11 @@
     lengths, valid = refs[8:10]
     biases = refs[10:19]
     output, input_grad_out = refs[19:21]
-    grad_out, heads_out, smalls_out, rows_out = refs[21:24], refs[24], refs[25], refs[26]
-    grad_out = dict(zip((O, IN, OUT), grad_out))
+    grad_o, *grad_in, grad_out = refs[21:25]
+    heads_out, smalls_out, rows_out = refs[25:28]
     flat, shape = scratch_shapes()
-    S = types.SimpleNamespace(**jax.tree.unflatten(shape, refs[27 : 27 + len(flat)]))
-    send_sems, recv_sems, local_sems = refs[27 + len(flat) :]
+    S = types.SimpleNamespace(**jax.tree.unflatten(shape, refs[28 : 28 + len(flat)]))
+    send_sems, recv_sems, local_sems = refs[28 + len(flat) :]
 
     c = lax.axis_index("ctx")
     w = lax.axis_index("wsh")
@@ -593,8 +597,20 @@
             bit *= 2
         return out
 
-    def remote(key, src, dst, c_to, w_to, offset=0, size=1):
+    at_end = a * (3 - a) == 0
+    roles, sent_by_role = [None], []
+
+    def only(end):
+        def run(action):
+            roles.append(end)
+            pl.when(at_end if end else jnp.logical_not(at_end))(action)
+            roles.pop()
+
+        return run
+
+    def remote(key, src, dst, c_bits, w_bits, offset=0, size=1, to=None, like=None):
         number = numbers.take(key, size) + offset
+        c_to, w_to = bit_xor(c, c_bits), bit_xor(w, w_bits) if to is None else to
         copy = pltpu.make_async_remote_copy(
             src_ref=src,
             dst_ref=dst,
@@ -604,8 +620,10 @@
             device_id_type=MESH,
         )
         copy.start()
-        started.append(copy)
-        return copy
+        if roles[-1] is None:
+            started.append(copy)
+        else:
+            sent_by_role.append((roles[-1], like, number))
 
     def arrived(key, landing, offset=0):
         number = numbers.take(key) + offset
@@ -632,7 +650,7 @@
         return shards[name - PART_Q].at[:, pl.ds(first_col, SLICE)]
 
     loads = {TOKENS: local(TOKENS, tokens.at[0], S.x)}
-    for name in (PART_K, PART_V, PART_Q, O, IN, OUT, K, V, Q):
+    for name in (PART_K, PART_V, PART_Q, O, IN, OUT):
         loads[name] = local((LOAD, name), shard(name), S.full[name].at[w])
     loads[TEACHER] = local(TEACHER, teacher.at[0], S.teacher)
 
@@ -658,49 +676,70 @@
 
     pl.semaphore_wait(barrier, len(peers))
 
-    def half_of(name, which):
-        rows = WEIGHT_SHAPES[name][0] // 2
-        return pl.ds(pl.multiple_of(which * rows, rows), rows)
-
     def mine(name):
         return bit(c, SECOND_WAY[name])
 
-    def send_weight(name):
-        full, own = S.full[name], half_of(name, mine(name))
-        if name < PART_Q:
-            half = shard(name).at[own]
-        else:
-            half = shards[name - PART_Q].at[own, pl.ds(first_col, SLICE)]
-        remote((WEIGHT_X, name), half, full.at[w, own], c, bit_xor(w, 2))
-        remote((WEIGHT_CORE, name), shard(name), full.at[w], c, bit_xor(w, 1))
+    def pieces(name):
+        tall, across = PIECES.get(name, (1, 1))
+        return range(tall * across)
+
+    def piece(name, which, number):
+        rows, cols = WEIGHT_SHAPES[name]
+        tall, across = PIECES.get(name, (1, 1))
+        high, broad = rows // 2 // tall, cols // across
+        row = which * (rows // 2) + number // across * high
+        return pl.ds(pl.multiple_of(row, 16), high), slice(
+            number % across * broad, (number % across + 1) * broad
+        )
+
+    def send_core(name):
+        remote((WEIGHT_CORE, name), shard(name), S.full[name].at[w], 0, 1)
+
+    def send_x(name):
+        for i in pieces(name):
+            rows, cols = piece(name, mine(name), i)
+            if name < PART_Q:
+                source = shards[name].at[rows, cols]
+            else:
+                source = shards[name - PART_Q].at[rows, pl.ds(first_col, SLICE)]
+            remote((WEIGHT_X, name, i), source, S.full[name].at[w, rows, cols], 0, 2)
 
     for name in (PART_K, PART_V, PART_Q):
-        send_weight(name)
+        send_x(name)
+        send_core(name)
     for j in (1, 2, 3):
-        remote((SMALL, j), S.small.at[w], S.small.at[w], c, bit_xor(w, j))
-    remote((X_PAIR,), S.xt.at[c], S.xt.at[c], bit_xor(c, 1), w, 0, 4)
-    for j in (1, 2, 3):
-        remote((X_LINE, j), S.xt.at[c], S.xt.at[c], bit_xor(c, 2 * j), w)
-    for name in (O, IN, OUT, K, V, Q):
-        send_weight(name)
-
-    def pump_x(name):
-        slot = S.full[name].at[bit_xor(w, 2), half_of(name, mine(name))]
-        arrived((WEIGHT_X, name), slot)
-        remote((WEIGHT_SECOND, name), slot, slot, bit_xor(c, SECOND_WAY[name]), w)
-        remote((WEIGHT_CORE_X, name), slot, slot, c, bit_xor(w, 1))
-
-    def pump_second(name):
-        slot = S.full[name].at[bit_xor(w, 2), half_of(name, 1 - mine(name))]
-        arrived((WEIGHT_SECOND, name), slot)
-        remote((WEIGHT_CORE_SECOND, name), slot, slot, c, bit_xor(w, 1))
-
-    def weight_ready(name):
+        remote((SMALL, j), S.small.at[w], S.small.at[w], 0, j)
+    remote((X_LINE, 1), S.xt.at[c], S.xt.at[c], 2, 0)
+
+    @only(False)
+    def x_to_middle():
+        remote((X_LINE, 3), S.xt.at[c], S.xt.at[c], 6, 0, like=lambda: S.xt.at[0])
+
+    for name in (O, IN, OUT):
+        send_x(name)
+        send_core(name)
+
+    def pump_x(name, number=0):
+        slot = S.full[name].at[bit_xor(w, 2), *piece(name, mine(name), number)]
+        arrived((WEIGHT_X, name, number), slot)
+        remote((WEIGHT_SECOND, name, number), slot, slot, SECOND_WAY[name], 0)
+        remote((WEIGHT_CORE_X, name, number), slot, slot, 0, 1)
+
+    def pump_second(name, number=0):
+        slot = S.full[name].at[bit_xor(w, 2), *piece(name, 1 - mine(name), number)]
+        arrived((WEIGHT_SECOND, name, number), slot)
+        remote((WEIGHT_CORE_SECOND, name, number), slot, slot, 0, 1)
+
+    def weight_ready(name, numbers_=(0,), first=True):
         full = S.full[name]
-        loads[name].wait()
-        arrived((WEIGHT_CORE, name), full.at[bit_xor(w, 1)])
-        arrived((WEIGHT_CORE_X, name), full.at[bit_xor(w, 3), half_of(name, mine(name))])
-        arrived((WEIGHT_CORE_SECOND, name), full.at[bit_xor(w, 3), half_of(name, 1 - mine(name))])
+        if first:
+            loads[name].wait()
+            arrived((WEIGHT_CORE, name), full.at[bit_xor(w, 1)])
+        for i in numbers_:
+            near = full.at[bit_xor(w, 3), *piece(name, mine(name), i)]
+            far = full.at[bit_xor(w, 3), *piece(name, 1 - mine(name), i)]
+            arrived((WEIGHT_CORE_X, name, i), near)
+            arrived((WEIGHT_CORE_SECOND, name, i), far)
 
     def square(name):
         return S.full[name][...].reshape(D, D)
@@ -726,16 +765,12 @@
     own_live = c * ROWS + lax.broadcasted_iota(jnp.int32, (ROWS, 1), 0) < limit
 
     def block_on(j, pair):
-        if isinstance(j, int):
-            return 2 * bit_xor(a, j) + pair
-        low = (a % 2 + j % 2) % 2
-        high = (a // 2 + j // 2) % 2
-        return 2 * (2 * high + low) + pair
-
-    def pass_on(j):
+        return 2 * bit_xor(a, j) + pair
+
+    def pass_x(key, j, onward, bits):
         block = S.xt.at[block_on(j, b)]
-        arrived((X_LINE, j), block)
-        remote((X_PAIR,), block, block, bit_xor(c, 1), w, j, 4)
+        arrived((key, j), block)
+        remote(onward, block, block, bits, 0, like=lambda: S.xt.at[0])
 
     pump_x(PART_K)
     pump_x(PART_V)
@@ -755,53 +790,82 @@
     def vector(row):
         return S.vectors[row : row + 1, :]
 
-    def tall_bias(row):
-        return jnp.broadcast_to(S.vectors[row : row + 1, pl.ds(first_col, SLICE)], (8, SLICE)).T[
-            :, 0:1
-        ]
-
-    pass_on(1)
+    arrived((X_LINE, 1), S.xt.at[block_on(1, b)])
+
+    @only(False)
+    def pass_near_end():
+        block = S.xt.at[block_on(1, b)]
+        remote((X_LINE, 2), block, block, 6, 0, like=lambda: S.xt.at[0])
+        pass_x(X_LINE, 3, (X_EDGE, 2), 2)
+
     pump_second(PART_K)
     pump_second(PART_V)
     pump_second(PART_Q)
-    pass_on(2)
-    for i, name in enumerate((PART_Q, PART_K, PART_V)):
+    for i, (name, bias) in enumerate(((PART_K, None), (PART_V, 1), (PART_Q, 0))):
+        rows = slice(HW * i, HW * (i + 1))
         weight_ready(name)
-        S.turned_weight[SLICE * i : SLICE * (i + 1), :] = S.full[name][...].reshape(D, SLICE).T
-    query_bias, value_bias = tall_bias(0), tall_bias(1)
-
-    def project(block):
-        both = matmul(S.turned_weight[SLICE : 3 * SLICE, :], S.xt[block])
-        S.kt[block] = both[0:SLICE].astype(BF)
-        S.vt[block] = (both[SLICE : 2 * SLICE] + value_bias).astype(BF)
-
-    def project_queries(j):
+        S.turned[...] = S.full[name][...].reshape(D, SLICE).T
+        S.head_weight[rows, :] = S.turned[pl.ds(first_row, HW), :]
+        if bias is None:
+            S.head_bias[rows, :] = jnp.zeros((HW, ROWS), F32)
+        else:
+            row = S.vectors[bias : bias + 1, pl.ds(first_col, SLICE)]
+            S.tall_bias[...] = jnp.broadcast_to(row, (ROWS, SLICE)).T
+            S.head_bias[rows, :] = S.tall_bias[pl.ds(first_row, HW), :]
+
+    def project(j):
         block = block_on(j, b)
-        queries = matmul(S.turned_weight[0:SLICE, :], S.xt[block]) + query_bias
-        S.qt[block // 2] = queries.astype(BF)
-
-    for j in (0, 1, 2):
-        project_queries(j)
+        out = matmul(S.head_weight[...], S.xt[block]) + S.head_bias[...]
+        S.kv[block] = out[0 : 2 * HW].astype(BF)
+        S.q[block // 2] = out[2 * HW :].astype(BF)
+        remote((KEY_VALUE, j), S.kv.at[block], S.kv.at[block], 1, 0)
+
+    project(0)
+    project(1)
     pump_x(O)
-    pass_on(3)
-    project_queries(3)
+    pump_x(IN, 0)
+
+    @only(False)
+    def pass_far_end():
+        pass_x(X_LINE, 2, (X_EDGE, 3), 2)
+
+    @only(True)
+    def from_middle():
+        arrived((X_EDGE, 2), S.xt.at[block_on(2, b)])
+
+    project(2)
+    pump_x(IN, 1)
+
+    @only(True)
+    def from_far_end():
+        arrived((X_EDGE, 3), S.xt.at[block_on(3, b)])
+
+    project(3)
+    pump_x(IN, 2)
 
     def to_group(key, source_of, everywhere):
         for j in (1, 2, 3):
             to = bit_xor(w, j)
-            remote((*key, j), source_of(to), everywhere.at[w], c, to)
+            remote((*key, j), source_of(to), everywhere.at[w], 0, j)
 
     def from_group(key, everywhere):
         for j in (1, 2, 3):
             arrived((*key, j), everywhere.at[bit_xor(w, j)])
 
+    def to_near(key, source, everywhere):
+        for j in (1, 2):
+            remote((key, j), source, everywhere.at[w], 0, j)
+
+    def pass_to_core(key, everywhere):
+        slot = everywhere.at[bit_xor(w, 2)]
+        arrived((key, 2), slot)
+        remote((key, 3), slot, slot, 0, 1)
+
+    def from_near(key, everywhere):
+        for j in (1, 3):
+            arrived((key, j), everywhere.at[bit_xor(w, j)])
+
     score_scale = 1.0 / math.sqrt(HD)
-
-    def head(ref, block, h):
-        return ref[block, pl.ds(first_row + HD * h, HD), :]
-
-    def wide_queries(h):
-        return jnp.concatenate([head(S.qt, i, h) for i in range(4)], axis=1)
 
     def wide(ref, h):
         return jnp.concatenate([ref[i, HD * h : HD * (h + 1), :] for i in range(4)], axis=1)
@@ -810,29 +874,30 @@
     S.total[...] = jnp.zeros(S.total.shape, F32)
 
     def attend_block(block):
-        project(block)
         allowed = key_code(block) == query_code
         for h in range(HEADS):
-            scores = tn(head(S.kt, block, h), wide_queries(h)) * score_scale
+            scores = tn(S.kv[block, HD * h : HD * (h + 1), :], wide(S.q, h)) * score_scale
             weights = jnp.exp(jnp.where(allowed, scores, MASKED))
             S.weights[block, h] = weights
             S.total[h, 0:1, :] += jnp.sum(weights, axis=0, keepdims=True)
-            S.mix[h] += matmul(head(S.vt, block, h), weights.astype(BF))
+            value_t = S.kv[block, HW + HD * h : HW + HD * (h + 1), :]
+            S.mix[h] += matmul(value_t, weights.astype(BF))
 
     @pl.loop(0, 4)
-    def attend_line(j):
-        attend_block(block_on(j, b))
+    def attend_line(i):
+        attend_block(2 * i + b)
 
     pump_second(O)
-    pump_x(IN)
-    pair_base = numbers.take((X_PAIR,), 4)
-
-    @pl.loop(0, 4)
-    def attend_pair(j):
-        block = block_on(j, 1 - b)
-        landing = S.xt.at[block]
-        pltpu.make_async_copy(landing, landing, recv_sems.at[pair_base + j]).wait()
-        attend_block(block)
+    pump_x(IN, 3)
+    pump_second(IN, 0)
+    pump_x(OUT, 0)
+    for j in range(4):
+        arrived((KEY_VALUE, j), S.kv.at[block_on(j, 1 - b)])
+        attend_block(block_on(j, 1 - b))
+        if j == 0:
+            pump_second(IN, 1)
+        if j == 2:
+            pump_x(OUT, 1)
 
     for h in range(HEADS):
         context_t = (S.mix[h] / S.total[h, 0:1, :]).astype(BF)
@@ -840,11 +905,12 @@
             S.ctx_send[i, HD * h : HD * (h + 1), :] = context_t[:, ROWS * i : ROWS * (i + 1)]
     for j in (1, 2, 3):
         to = bit_xor(a, j)
-        remote((CONTEXT, j), S.ctx_send.at[to], S.ctx.at[a], bit_xor(c, 2 * j), w)
+        remote((CONTEXT, j), S.ctx_send.at[to], S.ctx.at[a], 2 * j, 0)
     S.ctx[a] = S.ctx_send[a]
-    pump_second(IN)
-    pump_x(OUT)
     weight_ready(O)
+    pump_second(IN, 2)
+    pump_x(OUT, 2)
+    pump_second(OUT, 0)
     for j in (1, 2, 3):
         arrived((CONTEXT, j), S.ctx.at[bit_xor(a, j)])
 
@@ -857,22 +923,34 @@
     settled_low = settled.astype(BF)
     S.first[...] = normal_one
     S.keep[...] = settled
-    for i in range(2):
-        S.set_half[i] = settled_low[:, 384 * i : 384 * (i + 1)]
-    to_group((SETTLED_ALL,), lambda to: S.set_half.at[to // 2], S.set_all)
-    S.set_all[w] = S.set_half[x]
-    weight_ready(IN)
-    pump_second(OUT)
+    S.set_low[...] = settled_low
+    to_near(SETTLED_ALL, S.set_low, S.set_all)
+    S.set_all[w] = settled_low
+    pump_second(IN, 3)
+    pump_x(OUT, 3)
+    pump_second(OUT, 1)
+
+    def gelu(inner):
+        return 0.5 * inner * (1.0 + jnp.tanh(GELU_C * (inner + 0.044715 * inner * inner * inner)))
+
+    def gelu_slope(inner):
+        squared = inner * inner
+        bend = jnp.tanh(GELU_C * (inner + 0.044715 * squared * inner))
+        return 0.5 * (1.0 + bend) + 0.5 * inner * (1.0 - bend * bend) * (
+            GELU_C * (1.0 + 3 * 0.044715 * squared)
+        )
+
     for t in range(4):
+        weight_ready(IN, (t,), t == 0)
         w_part = S.full[IN][:, :, D * t : D * (t + 1)].reshape(D, D)
         inner = matmul(settled_low, w_part) + vector(8 + t)
         S.inner[t] = inner
-        S.act[t] = (
-            0.5 * inner * (1.0 + jnp.tanh(GELU_C * (inner + 0.044715 * inner * inner * inner)))
-        ).astype(BF)
-    to_group((ACTIVATED_ALL,), lambda to: S.act.at[to], S.act_all)
-    S.act_all[w] = S.act[w]
-    weight_ready(OUT)
+        S.act[t] = gelu(inner).astype(BF)
+        if t == 1:
+            pump_second(OUT, 2)
+    pump_second(OUT, 3)
+    pass_to_core(SETTLED_ALL, S.set_all)
+    weight_ready(OUT, range(4))
     branch = vector(5)
     for t in range(4):
         branch = branch + matmul(S.act[t], S.full[OUT][t])
@@ -897,29 +975,18 @@
     d_second = norm_back(upstream * vector(6), normal_two, inverse_two)
     branch_grad = d_second.astype(BF)
     S.bg[...] = branch_grad
-    for name in (K, V, Q):
-        pump_x(name)
-    to_group((BRANCH_GRAD_ALL,), lambda to: S.bg, S.bg_all)
+    to_near(BRANCH_GRAD_ALL, S.bg, S.bg_all)
     S.bg_all[w] = branch_grad
     note(5, branch_grad)
     d_settled = d_second
     for t in range(4):
         d_act = right_product(branch_grad, S.full[OUT][t])
         inner = S.inner[t]
-        squared = inner * inner
-        bend = jnp.tanh(GELU_C * (inner + 0.044715 * squared * inner))
-        slope = 0.5 * (1.0 + bend) + 0.5 * inner * (1.0 - bend * bend) * (
-            GELU_C * (1.0 + 3 * 0.044715 * squared)
-        )
-        inner_grad = (d_act * slope).astype(BF)
-        S.ig_half[t // 2, :, D * (t % 2) : D * (t % 2 + 1)] = inner_grad
+        inner_grad = (d_act * gelu_slope(inner)).astype(BF)
         note(8 + t, inner_grad)
         w_part = S.full[IN][:, :, D * t : D * (t + 1)].reshape(D, D)
         d_settled = d_settled + right_product(inner_grad, w_part)
-    for name in (K, V, Q):
-        pump_second(name)
-    to_group((INNER_GRAD_ALL,), lambda to: S.ig_half.at[to % 2], S.ig_all)
-    S.ig_all[w] = S.ig_half[core]
+    pass_to_core(BRANCH_GRAD_ALL, S.bg_all)
     normal_one = S.first[...]
     note(3, d_settled * normal_one)
     note(4, d_settled)
@@ -932,281 +999,373 @@
         S.cg_send[i] = context_grad[HW * i : HW * (i + 1), :]
     for j in (1, 2, 3):
         to = bit_xor(a, j)
-        remote((CONTEXT_GRAD, j), S.cg_send.at[to], S.cg.at[a], bit_xor(c, 2 * j), w)
+        remote((CONTEXT_GRAD, j), S.cg_send.at[to], S.cg.at[a], 2 * j, 0)
     S.cg[a] = S.cg_send[a]
     for i in range(2):
         S.ag_half[i] = attn_grad[:, 384 * i : 384 * (i + 1)]
     to_group((ATTN_GRAD_ALL,), lambda to: S.ag_half.at[to % 2], S.ag_all)
     S.ag_all[w] = S.ag_half[core]
 
-    def reduce_send(name, stage):
-        mask = HALVING[name][stage]
-        source = S.part[name] if stage == 0 else S.sum[name][stage - 1]
-        there = source.at[1 - bit(c, mask)]
-        remote((REDUCE, name, stage), there, S.got[name][stage], bit_xor(c, mask), w)
-
-    def slot(name):
-        return [bit(c, mask) for mask in HALVING[name]]
-
-    def reduce_add(name, stage):
-        source = S.part[name] if stage == 0 else S.sum[name][stage - 1]
-        got = S.got[name][stage]
-        arrived((REDUCE, name, stage), got)
-        total = source[bit(c, HALVING[name][stage])].astype(F32) + got[...].astype(F32)
-        if stage == 2:
-            i, j, k = slot(name)
-            S.done[name][i, j, k] = total.astype(BF)
-        else:
-            rows, cols = PART_SHAPES[name]
-            S.sum[name][stage][...] = total.astype(BF).reshape(2, rows >> (stage + 2), cols)
-
-    def spread_send(name, stage):
-        i, j, k = slot(name)
-        part = S.done[name].at[i, j, k] if stage == 2 else S.done[name].at[i, j]
-        remote((SPREAD, name, stage), part, part, bit_xor(c, HALVING[name][stage]), w)
-
-    def spread_wait(name, stage):
-        i, j, k = slot(name)
-        part = S.done[name].at[i, j, 1 - k] if stage == 2 else S.done[name].at[i, 1 - j]
-        arrived((SPREAD, name, stage), part)
-
-    def give(name):
-        mask = HALVING[name][0]
-        half = bit(c, mask)
-        done, out = S.done[name].at[half], grad_out[name]
-        if name == OUT:
-            remote((GIVE, name), done, out.at[half], bit_xor(c, mask), w)
-            finishing.append(local((GIVE, name), done, out.at[half]))
+    half = a // 2
+
+    def reduce_pair(lot):
+        remote((REDUCE, lot, 0), S.part[lot].at[1 - b], S.got[lot][0], 1, 0)
+
+    def reduce_end(lot):
+        got = S.got[lot][0]
+        arrived((REDUCE, lot, 0), got)
+        total = S.part[lot][b].astype(F32) + got[...].astype(F32)
+        S.sum[lot][0][...] = total.astype(BF)
+
+        @only(True)
+        def to_middle():
+            target = S.got[lot][1]
+            remote((REDUCE, lot, 1), S.sum[lot][0], target, 2, 0, like=lambda: target)
+
+    def reduce_middle(lot):
+        @only(False)
+        def swap_halves():
+            got = S.got[lot][1]
+            arrived((REDUCE, lot, 1), got)
+            total = S.sum[lot][0][...].astype(F32) + got[...].astype(F32)
+            S.sum[lot][1][...] = total.astype(BF)
+            there, target = S.sum[lot][1].at[1 - half], S.got[lot][2]
+            remote((REDUCE, lot, 2), there, target, 6, 0, like=lambda: target)
+
+    def reduce_last(lot):
+        @only(False)
+        def own_half():
+            got = S.got[lot][2]
+            arrived((REDUCE, lot, 2), got)
+            total = (S.sum[lot][1][half].astype(F32) + got[...].astype(F32)).astype(BF)
+            if lot in LOT_IN:
+                own, done = S.own[lot], S.done[lot]
+                own[...] = total
+                done[b, half, w] = own[w]
+                for q in (1, 2, 3):
+                    slot = done.at[b, half, w]
+                    to = bit_xor(w, q)
+                    remote((GROUP_X, lot, q), own.at[to], slot, 0, q, like=lambda: own.at[0])
+            else:
+                S.done[lot][b, half] = total
+                spread_middle(lot)
+
+    def spread_middle(lot):
+        part = S.done[lot].at[b, half]
+        remote((SPREAD, lot, 0), part, part, 6, 0, like=lambda: S.done[lot].at[0, 0])
+
+    def spread_group(lot):
+        @only(False)
+        def gathered():
+            for q in (1, 2, 3):
+                arrived((GROUP_X, lot, q), S.done[lot].at[b, half, bit_xor(w, q)])
+            spread_middle(lot)
+
+    def spread_end(lot):
+        @only(False)
+        def to_end():
+            arrived((SPREAD, lot, 0), S.done[lot].at[b, 1 - half])
+            done = S.done[lot].at[b]
+            remote((SPREAD, lot, 1), done, done, 2, 0, like=lambda: S.done[lot].at[0])
+
+    def result_of(lot):
+        return grad_in[lot - LOT_IN[0]] if lot in LOT_IN else grad_out.at[lot - LOT_OUT[0]]
+
+    def give(lot):
+        @only(True)
+        def from_middle_device():
+            arrived((SPREAD, lot, 1), S.done[lot].at[b])
+
+        done = S.done[lot].at[b]
+        if lot not in LOT_O:
+            out = result_of(lot).at[b]
+            remote((GIVE, lot), done, out, 1, 0)
+            finishing.append(local((GIVE, lot), done, out))
             return
-        remote((GIVE, name), done, out.at[core], bit_xor(c, mask), 2 * x + half, core, 2)
-
-        @pl.when(core == half)
+        remote((GIVE, lot), done, grad_o.at[core], 1, 0, core, 2, 2 * x + b)
+
+        @pl.when(core == b)
         def keep_own():
-            local((OWN, name), done, out.at[core])
-
-        @pl.when(core != half)
+            local((OWN, lot), done, grad_o.at[core])
+
+        @pl.when(core != b)
         def give_core():
-            remote((OWN, name), done, out.at[core], c, bit_xor(w, 1))
+            remote((OWN, lot), done, grad_o.at[core], 0, 1)
             started.pop()
 
-    def settle(name):
-        half = bit(c, HALVING[name][0])
-        done, out = S.done[name].at[half], grad_out[name]
-        if name == OUT:
-            arrived((GIVE, name), out.at[1 - half])
+    def settle(lot):
+        if lot not in LOT_O:
+            arrived((GIVE, lot), result_of(lot).at[1 - b])
             return
-
-        @pl.when(core == half)
+        done = S.done[lot].at[b]
+
+        @pl.when(core == b)
         def from_chip():
             pltpu.make_async_copy(
-                done, out.at[core], local_sems.at[locals_.take((OWN, name))]
+                done, grad_o.at[core], local_sems.at[locals_.take((OWN, lot))]
             ).wait()
-            arrived((OWN, name), out.at[1 - core])
-
-        @pl.when(core != half)
+            arrived((OWN, lot), grad_o.at[1 - core])
+
+        @pl.when(core != b)
         def from_partner():
-            arrived((GIVE, name), out.at[0], 0)
-            arrived((GIVE, name), out.at[1], 1)
-            sent = numbers.take((OWN, name))
+            arrived((GIVE, lot), grad_o.at[0], 0)
+            arrived((GIVE, lot), grad_o.at[1], 1)
+            sent = numbers.take((OWN, lot))
             pltpu.make_async_copy(done, done, send_sems.at[sent]).wait()
 
-    from_group((ACTIVATED_ALL,), S.act_all)
-    from_group((BRANCH_GRAD_ALL,), S.bg_all)
-    S.part[OUT][...] = (
-        tn(S.act_all[...].reshape(GROUP * ROWS, D), S.bg_all[...].reshape(GROUP * ROWS, D))
-        .astype(BF)
-        .reshape(2, D // 2, D)
-    )
-    reduce_send(OUT, 0)
-
-    for j in (1, 2, 3):
-        arrived((CONTEXT_GRAD, j), S.cg.at[bit_xor(a, j)])
-    for h in range(HEADS):
-        grad = wide(S.cg, h).astype(F32)
-        row_total = S.total[h, 0:1, :]
-        S.wg[h] = (grad / row_total).astype(BF)
-        S.total[h, 1:2, :] = -jnp.sum(grad * S.mix[h], axis=0, keepdims=True) / (
-            row_total * row_total
+    def lanes(parts):
+        return jnp.concatenate(parts, axis=1)
+
+    def inner_again():
+        from_near(SETTLED_ALL, S.set_all)
+        settled_all = S.set_all[...].reshape(GROUP * ROWS, D)
+        hidden = pl.ds(pl.multiple_of(D * w, D), D)
+        S.inner_all[...] = (
+            matmul(settled_all, S.full[IN][:, :, hidden].reshape(D, D))
+            + S.vectors[pl.ds(8 + w, 1), :]
         )
-    S.mix[...] = jnp.zeros(S.mix.shape, F32)
-
-    @pl.loop(0, CTX)
-    def attend_back(block):
+        S.act_all[...] = gelu(S.inner_all[...]).astype(BF)
+
+    def out_part():
+        from_near(BRANCH_GRAD_ALL, S.bg_all)
+        grad = tn(S.act_all[...], S.bg_all[...].reshape(GROUP * ROWS, D)).astype(BF)
+        for i, lot in enumerate(LOT_OUT):
+            S.part[lot][...] = grad[HW * i : HW * (i + 1)].reshape(2, 2, 48, D)
+            reduce_pair(lot)
+
+    def in_part():
+        branch_grad_all = S.bg_all[...].reshape(GROUP * ROWS, D)
+        inner_grad_all = (
+            right_product(branch_grad_all, S.full[OUT][w]) * gelu_slope(S.inner_all[...])
+        ).astype(BF)
+        grad = tn(S.set_all[...].reshape(GROUP * ROWS, D), inner_grad_all).astype(BF)
+        for i, lot in enumerate(LOT_IN):
+            for j in range(2):
+                side = grad[:, 384 * j : 384 * (j + 1)].reshape(4, 2, 2, 48, 384)
+                for k in range(2):
+                    S.part[lot][j, k] = side[:, k, i]
+            reduce_pair(lot)
+
+    def attention_back():
+        for j in (1, 2, 3):
+            arrived((CONTEXT_GRAD, j), S.cg.at[bit_xor(a, j)])
         for h in range(HEADS):
-            key_rows = slice(HD * h, HD * (h + 1))
-            value_rows = slice(HW + HD * h, HW + HD * (h + 1))
-            weights = S.weights[block, h]
-            grad = S.wg[h]
-            weight_grad = tn(head(S.vt, block, h), grad) + S.total[h, 1:2, :]
-            score_grad = (weights * weight_grad).astype(BF)
-            S.mix[h] += matmul(head(S.kt, block, h), score_grad)
-            S.dkv_send[block, key_rows, :] = (
-                right_product(wide_queries(h), score_grad) * score_scale
+            grad = wide(S.cg, h).astype(F32)
+            row_total = S.total[h, 0:1, :]
+            S.wg[h] = (grad / row_total).astype(BF)
+            S.total[h, 1:2, :] = -jnp.sum(grad * S.mix[h], axis=0, keepdims=True) / (
+                row_total * row_total
+            )
+        S.mix[...] = jnp.zeros(S.mix.shape, F32)
+
+        def attend_back(pair, i):
+            block = 2 * i + pair
+            for h in range(HEADS):
+                key_rows = slice(HD * h, HD * (h + 1))
+                value_rows = slice(HW + HD * h, HW + HD * (h + 1))
+                weights = S.weights[block, h]
+                grad = S.wg[h]
+                weight_grad = tn(S.kv[block, value_rows, :], grad) + S.total[h, 1:2, :]
+                score_grad = (weights * weight_grad).astype(BF)
+                S.mix[h] += matmul(S.kv[block, key_rows, :], score_grad)
+                S.dkv[pair, i, key_rows, :] = (
+                    right_product(wide(S.q, h), score_grad) * score_scale
+                ).astype(BF)
+                value_grad = right_product(grad, weights.astype(BF))
+                S.dkv[pair, i, value_rows, :] = value_grad.astype(BF)
+
+        @pl.loop(0, CTX)
+        def every_block(block):
+            attend_back(block % 2, block // 2)
+
+        remote((KEY_VALUE_GRAD,), S.dkv.at[1 - b], S.dkv_pair, 1, 0)
+        for h in range(HEADS):
+            rows = slice(2 * HW + HD * h, 2 * HW + HD * (h + 1))
+            S.grads[rows, :] = (S.mix[h] * score_scale).astype(BF)
+        S.grads[3 * HW :, :] = jnp.zeros((HEAD_COLS - 3 * HW, 4 * ROWS), BF)
+
+    def o_part():
+        from_group((CONTEXT_ALL,), S.ctx_all)
+        from_group((ATTN_GRAD_ALL,), S.ag_all)
+        context_all = lanes([S.ctx_all[i].reshape(384, ROWS) for i in range(GROUP)])
+        grad = matmul(context_all, S.ag_all[...].reshape(GROUP * ROWS, 384))
+        S.part[LOT_O[0]][...] = grad.astype(BF).reshape(2, 2, 96, 384)
+        reduce_pair(LOT_O[0])
+
+    def heads_part():
+        arrived((KEY_VALUE_GRAD,), S.dkv_pair)
+        for i in range(4):
+            S.grads[0 : 2 * HW, ROWS * i : ROWS * (i + 1)] = (
+                S.dkv[b, i].astype(F32) + S.dkv_pair[i].astype(F32)
             ).astype(BF)
-            S.dkv_send[block, value_rows, :] = right_product(grad, weights.astype(BF)).astype(BF)
-
-    for j in range(1, CTX):
-        to = bit_xor(c, j)
-        remote((KEY_VALUE_GRAD, j), S.dkv_send.at[to], S.dkv.at[c], to, w)
-    S.dkv[c] = S.dkv_send[c]
-    for h in range(HEADS):
-        query_t = (S.mix[h] * score_scale).astype(BF)
+        own_inputs = lanes([S.xt[2 * i + b] for i in range(4)])
+        heads = right_product(own_inputs, S.grads[...]).astype(BF)
+        S.heads[...] = heads.reshape(2, 2, HW, HEAD_COLS)
+        for i in range(2):
+            remote((HEADS_CORE, i), S.heads.at[i, 1 - core], S.heads_core.at[i], 0, 1)
+
+    def input_parts():
+        parts = tn(S.grads[0 : 3 * HW, :], S.head_weight[...])
+        S.dx_send[...] = parts.astype(BF).reshape(4, ROWS, D)
+        for j in (1, 2, 3):
+            to = bit_xor(a, j)
+            remote((INPUT_PARTS, j), S.dx_send.at[to], S.dx.at[a], 2 * j, 0)
+        S.dx[a] = S.dx_send[a]
+
+    def vectors_group():
+        S.column[...] = jnp.zeros((D, ROWS), F32)
+        heads_rows = pl.ds(pl.multiple_of(HW * a, HW), HW)
+        for row, first in ((1, HW), (0, 2 * HW)):
+            sums = jnp.sum(S.grads[first : first + HW, :].astype(F32), axis=1, keepdims=True)
+            S.column[heads_rows, :] = jnp.broadcast_to(sums, (HW, ROWS))
+            S.sg[row : row + 1, :] = S.column[...].T[0:1, :]
+        for j in (1, 2, 3):
+            remote((VECTORS_W, j), S.sg, S.sg_w.at[w], 0, j)
+        S.sg_w[w] = S.sg[...]
+
+    def vectors_line():
+        for j in (1, 2, 3):
+            arrived((VECTORS_W, j), S.sg_w.at[bit_xor(w, j)])
+        S.sg_z[a] = (S.sg_w[0] + S.sg_w[1]) + (S.sg_w[2] + S.sg_w[3])
+        for j in (1, 2, 3):
+            remote((VECTORS_Z, j), S.sg_z.at[a], S.sg_z.at[a], 2 * j, 0)
+
+    def vectors_pair():
+        for j in (1, 2, 3):
+            arrived((VECTORS_Z, j), S.sg_z.at[bit_xor(a, j)])
+        S.sg_y[b] = (S.sg_z[0] + S.sg_z[1]) + (S.sg_z[2] + S.sg_z[3])
+        remote(VECTORS_Y, S.sg_y.at[b], S.sg_y.at[b], 1, 0)
+
+    def vectors_done():
+        arrived(VECTORS_Y, S.sg_y.at[1 - b])
+        everything = S.sg_y[0] + S.sg_y[1]
+        S.sg_rows[...] = everything
         for i in range(4):
-            S.dq_send[i, HD * h : HD * (h + 1), :] = query_t[:, ROWS * i : ROWS * (i + 1)]
-    for j in (1, 2, 3):
-        to = bit_xor(a, j)
-        remote((QUERY_GRAD, j), S.dq_send.at[to], S.dq.at[a], bit_xor(c, 2 * j), w)
-    S.dq[a] = S.dq_send[a]
-
-    def lanes(ref, pair):
-        return jnp.concatenate([ref[2 * i + pair] for i in range(4)], axis=1)
-
-    own_grads = jnp.concatenate(
-        [
-            lanes(S.dkv_send, b),
-            jnp.concatenate([S.dq_send[i] for i in range(4)], axis=1),
-            jnp.zeros((HEAD_COLS - 3 * HW, 4 * ROWS), BF),
-        ],
-        axis=0,
-    )
-    other = right_product(lanes(S.xt, 1 - b), lanes(S.dkv_send, 1 - b))
-    heads = right_product(lanes(S.xt, b), own_grads)
-    heads = jnp.concatenate([heads[:, : 2 * HW] + other, heads[:, 2 * HW :]], axis=1).astype(BF)
-    S.heads[...] = heads.reshape(2, 2, HW, HEAD_COLS)
-    for i in range(2):
-        remote((HEADS_CORE, i), S.heads.at[i, 1 - core], S.heads_core.at[i], c, bit_xor(w, 1))
-
-    from_group((SETTLED_ALL,), S.set_all)
-    from_group((INNER_GRAD_ALL,), S.ig_all)
-    S.part[IN][...] = (
-        tn(S.set_all[...].reshape(GROUP * ROWS, 384), S.ig_all[...].reshape(GROUP * ROWS, 1536))
-        .astype(BF)
-        .reshape(2, HW, 1536)
-    )
-    reduce_send(IN, 0)
-    for i in range(2):
-        arrived((HEADS_CORE, i), S.heads_core.at[i])
-        S.heads_sum[i] = (S.heads[i, core].astype(F32) + S.heads_core[i].astype(F32)).astype(BF)
-    remote((HEADS_X,), S.heads_sum.at[1 - x], S.heads_x, c, bit_xor(w, 2))
-    reduce_add(OUT, 0)
-    reduce_send(OUT, 1)
-    from_group((CONTEXT_ALL,), S.ctx_all)
-    from_group((ATTN_GRAD_ALL,), S.ag_all)
-    context_all = jnp.concatenate(
-        [S.ctx_all[i].reshape(384, ROWS) for i in range(GROUP)], axis=1
-    )
-    S.part[O][...] = (
-        matmul(context_all, S.ag_all[...].reshape(GROUP * ROWS, 384)).astype(BF).reshape(2, HW, 384)
-    )
-    reduce_send(O, 0)
-    arrived((HEADS_X,), S.heads_x)
-    S.heads_row[...] = (
-        (S.heads_sum[x].astype(F32) + S.heads_x[...].astype(F32))
-        .astype(BF)
-        .reshape(2, HW // 2, HEAD_COLS)
-    )
-    remote((HEADS_Y,), S.heads_row.at[1 - b], S.heads_y, bit_xor(c, 1), w)
-    reduce_add(OUT, 1)
-    reduce_send(OUT, 2)
-    reduce_add(IN, 0)
-    reduce_send(IN, 1)
-    reduce_add(OUT, 2)
-    spread_send(OUT, 2)
-    arrived((HEADS_Y,), S.heads_y)
-    S.heads_done[a] = (S.heads_row[b].astype(F32) + S.heads_y[...].astype(F32)).astype(BF)
-    for j in (1, 2, 3):
-        remote((HEADS_LINE, j), S.heads_done.at[a], S.heads_done.at[a], bit_xor(c, 2 * j), w)
-
-    for name in (K, V, Q):
-        weight_ready(name)
-    for j in range(1, CTX):
-        arrived((KEY_VALUE_GRAD, j), S.dkv.at[bit_xor(c, j)])
-    for j in (1, 2, 3):
-        arrived((QUERY_GRAD, j), S.dq.at[bit_xor(a, j)])
-
-    def summed(first):
-        parts = []
+            S.smalls[i] = everything[:, HW * i : HW * (i + 1)]
+        finishing.append(local(VECTORS_Y, S.smalls, smalls_out))
+        finishing.append(local(VECTORS_Z, S.sg_rows, rows_out))
+
+    def heads_x():
+        for i in range(2):
+            arrived((HEADS_CORE, i), S.heads_core.at[i])
+        for i in range(2):
+            S.heads_sum[i] = (S.heads[i, core].astype(F32) + S.heads_core[i].astype(F32)).astype(BF)
+        remote((HEADS_X,), S.heads_sum.at[1 - x], S.heads_x, 0, 2)
+
+    def heads_y():
+        arrived((HEADS_X,), S.heads_x)
+        S.heads_row[...] = (
+            (S.heads_sum[x].astype(F32) + S.heads_x[...].astype(F32))
+            .astype(BF)
+            .reshape(2, HW // 2, HEAD_COLS)
+        )
+        remote((HEADS_Y,), S.heads_row.at[1 - b], S.heads_y, 1, 0)
+
+    def heads_line():
+        arrived((HEADS_Y,), S.heads_y)
+        S.heads_done[a] = (S.heads_row[b].astype(F32) + S.heads_y[...].astype(F32)).astype(BF)
+        for j in (1, 2, 3):
+            remote((HEADS_LINE, j), S.heads_done.at[a], S.heads_done.at[a], 2 * j, 0)
+
+    def heads_pair():
+        for j in (1, 2, 3):
+            arrived((HEADS_LINE, j), S.heads_done.at[bit_xor(a, j)])
+        remote((HEADS_PAIR,), S.heads_done, heads_out.at[b], 1, 0)
+        finishing.append(local((HEADS_PAIR,), S.heads_done, heads_out.at[b]))
+
+    def input_done():
+        for j in (1, 2, 3):
+            arrived((INPUT_PARTS, j), S.dx.at[bit_xor(a, j)])
+        total = S.keep[...]
         for i in range(4):
-            rows = slice(first, first + HW)
-            both = S.dkv[2 * i, rows, :].astype(F32) + S.dkv[2 * i + 1, rows, :].astype(F32)
-            parts.append(both)
-        return jnp.concatenate(parts, axis=0).T.astype(BF)
-
-    grads = {V: summed(HW), K: summed(0), Q: S.dq[...].reshape(D, ROWS).T}
-    note(1, grads[V])
-    note(0, grads[Q])
-    for j in (1, 2, 3):
-        remote((VECTORS_W, j), S.sg, S.sg_w.at[w], c, bit_xor(w, j))
-    S.sg_w[w] = S.sg[...]
-    input_grad = S.keep[...]
-    for name in (Q, K, V):
-        input_grad = input_grad + right_product(grads[name], square(name))
-    S.first[...] = input_grad
-    finishing.append(local(INPUT_GRAD, S.first, input_grad_out))
-
-    reduce_add(IN, 1)
-    reduce_send(IN, 2)
-    spread_wait(OUT, 2)
-    spread_send(OUT, 1)
-    reduce_add(O, 0)
-    reduce_send(O, 1)
-    reduce_add(IN, 2)
-    spread_send(IN, 2)
-    for j in (1, 2, 3):
-        arrived((VECTORS_W, j), S.sg_w.at[bit_xor(w, j)])
-    S.sg_z[a] = (S.sg_w[0] + S.sg_w[1]) + (S.sg_w[2] + S.sg_w[3])
-    for j in (1, 2, 3):
-        remote((VECTORS_Z, j), S.sg_z.at[a], S.sg_z.at[a], bit_xor(c, 2 * j), w)
-    reduce_add(O, 1)
-    reduce_send(O, 2)
-    spread_wait(OUT, 1)
-    give(OUT)
-    spread_wait(IN, 2)
-    spread_send(IN, 1)
-    for j in (1, 2, 3):
-        arrived((HEADS_LINE, j), S.heads_done.at[bit_xor(a, j)])
-    remote((HEADS_PAIR,), S.heads_done, heads_out.at[b], bit_xor(c, 1), w)
-    finishing.append(local((HEADS_PAIR,), S.heads_done, heads_out.at[b]))
-    reduce_add(O, 2)
-    spread_send(O, 2)
-    for j in (1, 2, 3):
-        arrived((VECTORS_Z, j), S.sg_z.at[bit_xor(a, j)])
-    S.sg_y[b] = (S.sg_z[0] + S.sg_z[1]) + (S.sg_z[2] + S.sg_z[3])
-    remote(VECTORS_Y, S.sg_y.at[b], S.sg_y.at[b], bit_xor(c, 1), w)
-    spread_wait(IN, 1)
-    give(IN)
-    spread_wait(O, 2)
-    spread_send(O, 1)
-    arrived(VECTORS_Y, S.sg_y.at[1 - b])
-    everything = S.sg_y[0] + S.sg_y[1]
-    S.sg_rows[...] = everything
-    for i in range(4):
-        S.smalls[i] = everything[:, HW * i : HW * (i + 1)]
-    finishing.append(local(VECTORS_Y, S.smalls, smalls_out))
-    finishing.append(local(VECTORS_Z, S.sg_rows, rows_out))
-    spread_wait(O, 1)
-    give(O)
+            total = total + S.dx[i].astype(F32)
+        S.first[...] = total
+        finishing.append(local(INPUT_GRAD, S.first, input_grad_out))
+
+    for step, *lot in (
+        (inner_again,),
+        (out_part,),
+        (reduce_end, 3),
+        (reduce_middle, 3),
+        (in_part,),
+        (reduce_end, 4),
+        (reduce_end, 5),
+        (reduce_middle, 4),
+        (reduce_end, 6),
+        (reduce_end, 1),
+        (reduce_middle, 6),
+        (reduce_last, 4),
+        (attention_back,),
+        (reduce_last, 6),
+        (reduce_end, 2),
+        (reduce_middle, 5),
+        (reduce_last, 3),
+        (o_part,),
+        (reduce_middle, 1),
+        (spread_end, 4),
+        (reduce_last, 5),
+        (spread_end, 3),
+        (spread_end, 6),
+        (reduce_middle, 2),
+        (reduce_last, 1),
+        (heads_part,),
+        (give, 3),
+        (vectors_group,),
+        (spread_group, 1),
+        (reduce_end, 0),
+        (give, 6),
+        (spread_end, 5),
+        (reduce_last, 2),
+        (heads_x,),
+        (vectors_line,),
+        (spread_end, 1),
+        (spread_group, 2),
+        (reduce_middle, 0),
+        (give, 5),
+        (heads_y,),
+        (give, 4),
+        (spread_end, 2),
+        (reduce_last, 0),
+        (vectors_pair,),
+        (heads_line,),
+        (give, 1),
+        (input_parts,),
+        (vectors_done,),
+        (spread_end, 0),
+        (give, 2),
+        (heads_pair,),
+        (give, 0),
+        (input_done,),
+
+    ):
+        step(*lot)
+
     arrived((HEADS_PAIR,), heads_out.at[1 - b])
-    for name in (OUT, IN, O):
-        settle(name)
+    for lot in range(len(LOTS)):
+        settle(lot)
     for copy in finishing:
         copy.wait()
     for copy in started:
         copy.wait_send()
+    for end, like, number in sent_by_role:
+
+        @only(end)
+        def sent():
+            source = like()
+            pltpu.make_async_copy(source, source, send_sems.at[number]).wait()
 
 
 def finish_kernel(*refs):
-    g_o, g_in, g_out, heads, smalls, rows, output, input_grad = refs[:8]
-    r_q, r_k, r_v, r_o, r_in, r_out = refs[8:14]
-    vectors, inner_bias, loss, r_output, r_input = refs[14:22], refs[22], refs[23], refs[24], refs[25]
+    g_o, g_in0, g_in1, g_out, heads, smalls, rows, output, input_grad = refs[:9]
+    r_q, r_k, r_v, r_o, r_in, r_out = refs[9:15]
+    vectors, inner_bias, loss, r_output, r_input = refs[15:23], *refs[23:]
     step = pl.program_id(0)
-    for source, result in ((g_o, r_o), (g_in, r_in)):
-        width = source.shape[-1]
-        rest = result.shape[0]
-        for i in range(2):
-            result[:, width * i : width * (i + 1)] = (
-                source[i].reshape(rest, width).astype(F32)
-            )
+    for i in range(2):
+        r_o[:, 384 * i : 384 * (i + 1)] = g_o[i].reshape(HW // 2, 384).astype(F32)
+        for j in range(4):
+            first = D * j + 384 * i
+            for k, source in enumerate((g_in0, g_in1)):
+                r_in[48 * k : 48 * (k + 1), first : first + 384] = source[i, 0, j].astype(F32)
     r_out[...] = g_out[...].reshape(D // 2, D).astype(F32)
     for i, result in ((0, r_k), (1, r_v), (2, r_q)):
         result[...] = jnp.concatenate(
@@ -1249,20 +1408,21 @@
     vmem = pl.BlockSpec(memory_space=pltpu.VMEM)
     low = lambda *shape: jax.ShapeDtypeStruct(shape, BF)
     full = lambda *shape: jax.ShapeDtypeStruct(shape, F32)
-    output, input_grad, g_o, g_in, g_out, heads, smalls, rows = pl.pallas_call(
+    output, input_grad, g_o, g_in0, g_in1, g_out, heads, smalls, rows = pl.pallas_call(
         fused_kernel,
         out_shape=(
             low(ROWS, D),
             full(ROWS, D),
-            low(2, 2, 2, 48, 384),
-            low(2, 2, 2, 48, 1536),
-            low(2, 2, 2, 96, D),
+            low(2, 2, 96, 384),
+            low(2, 2, 4, 48, 384),
+            low(2, 2, 4, 48, 384),
+            low(4, 2, 2, 48, D),
             low(2, 4, HW // 2, HEAD_COLS),
             full(GROUP, 16, HW),
             full(16, D),
         ),
         in_specs=[hbm] * 8 + [smem] * 2 + [vmem] * 9,
-        out_specs=[hbm] * 8,
+        out_specs=[hbm] * 9,
         scratch_shapes=scratch_shapes()[0]
         + [
             pltpu.SemaphoreType.DMA((REMOTE_SEMS,)),
@@ -1307,9 +1467,10 @@
         + (full(HW),) * 8
         + (full(D), full(1), low(1, ROWS, D), full(1, ROWS, D)),
         in_specs=[
-            pl.BlockSpec((2, 1, 2, 48, 384), lambda i: (0, i, 0, 0, 0)),
-            pl.BlockSpec((2, 1, 2, 48, 1536), lambda i: (0, i, 0, 0, 0)),
-            pl.BlockSpec((1, 2, 2, 96, D), lambda i: (i, 0, 0, 0, 0)),
+            pl.BlockSpec((2, 1, 96, 384), lambda i: (0, i, 0, 0)),
+            pl.BlockSpec((2, 1, 4, 48, 384), lambda i: (0, i, 0, 0, 0)),
+            pl.BlockSpec((2, 1, 4, 48, 384), lambda i: (0, i, 0, 0, 0)),
+            pl.BlockSpec((2, 2, 2, 48, D), lambda i: (i, 0, 0, 0, 0)),
             pl.BlockSpec((1, 4, HW // 2, HEAD_COLS), lambda i: (i, 0, 0, 0)),
             whole(GROUP, 16, HW),
             whole(16, D),
@@ -1330,7 +1491,7 @@
         ],
         compiler_params=pltpu.CompilerParams(dimension_semantics=("arbitrary",)),
         name="finish",
-    )(g_o, g_in, g_out, heads, smalls, rows, output, input_grad)
+    )(g_o, g_in0, g_in1, g_out, heads, smalls, rows, output, input_grad)
     r_q, r_k, r_v, r_o, r_in, r_out = results[:6]
     vectors, inner_bias, loss, r_output, r_input = results[6:14], *results[14:]
     return (

time: 199 us -> 169 us (0.85)
  Pallas kernels: 194 us -> 164 us
    pallas_call x1, Pallas kernels: 189 us -> 159 us  [fused_body(): pl.pallas_call(fused_kernel, out_shape=(low(ROWS, D), full(ROWS, D), low(...]
where the time goes in v3:
time: 169 us; the launch traced here: 166 us
  Pallas kernels  164 us (97%)
    pallas_call x1, Pallas kernels, fused_body(): pl.pallas_call(fused_kernel, out_shape=(low(ROWS, D), full(ROWS, D), low(...  159 us
    pallas_call x1, Pallas kernels, fused_body(): pl.pallas_call(finish_kernel, grid=(steps,), out_shape=(full(HW, D),) * 4...  5.18 us

profile of v3, /device:TPU:0, one launch (start us, length us, event | category | flops | bytes accessed | tf_op | source)
XLA Modules:
  0.0 165.6 jit_solution(15150561589615924383)
XLA Ops:
  1.3 159.0 %layer.1 = (bf16[128,768]{1,0:T(8,128)(2,1)}, f32[128,768]{1,0:T(8,128)}, bf16[2,2,96,384]{3,2,1,0:T(8,128)(2,1)}, bf16[2,2,4,48,384]{4,3,2,1,0:T(8,128)(2,1)}, ...) custom-call(bf16[1,128,768]{2,1,0:T(8,128)(2,1)} %refs_0_.1, ...), custom_call_target="tpu_custom_call" | custom-call | tf_op jit(solution)/shard_map/layer/pallas_call | solution.py:1411
  160.3 5.2 %finish.1 = (f32[192,768]{1,0:T(8,128)}, f32[192,768]{1,0:T(8,128)}, f32[192,768]{1,0:T(8,128)}, f32[192,768]{1,0:T(8,128)}, f32[192,3072]{1,0:T(8,128)}, /*inde...) custom-call(bf16[2,2,96,384]{3,2,1,0:T(8,128)(2,1)} %get-tuple-eleme, ...), custom_call_target="tpu_custom_call" | custom-call | tf_op jit(solution)/shard_map/finish/pallas_call | solution.py:1462

commit v4 on v3

--- a/solution.py
+++ b/solution.py
@@ -405,6 +405,7 @@
 WEIGHT_SHAPES = [(192, 768)] * 4 + [(192, 3072), (768, 768)] + [(192, SLICE)] * 3
 SECOND_WAY = {O: 1, IN: 1, OUT: 2, PART_Q: 1, PART_K: 1, PART_V: 1}
 LOT_O, LOT_IN, LOT_OUT = (0,), (1, 2), (3, 4, 5, 6)
+LOT_PAIR = LOT_O + LOT_IN + LOT_OUT[:3]
 LOTS = [(96, 384)] + [(4, 48, 384)] * 2 + [(48, D)] * 4
 PIECES = {IN: (1, 4), OUT: (4, 1)}
 HEAD_COLS = 640
@@ -436,16 +437,18 @@
     HEADS_X,
     HEADS_Y,
     HEADS_LINE,
+    HEADS_EDGE,
     HEADS_PAIR,
     VECTORS_W,
     VECTORS_Z,
     VECTORS_Y,
+    VECTORS_CORE,
     TOKENS,
     TEACHER,
     OUTPUT,
     INPUT_GRAD,
     LOAD,
-) = range(35)
+) = range(37)
 
 
 def fused_fits(mesh):
@@ -512,6 +515,7 @@
     s.act = pltpu.VMEM((4, ROWS, D), BF)
     s.first = pltpu.VMEM((ROWS, D), F32)
     s.keep = pltpu.VMEM((ROWS, D), F32)
+    s.inverse = pltpu.VMEM((ROWS, 128), F32)
     s.set_low = pltpu.VMEM((ROWS, D), BF)
     s.ag_half = pltpu.VMEM((2, ROWS, 384), BF)
     s.bg = pltpu.VMEM((ROWS, D), BF)
@@ -528,7 +532,11 @@
     s.dkv_pair = pltpu.VMEM((4, 2 * HW, ROWS), BF)
     s.grads = pltpu.VMEM((HEAD_COLS, 4 * ROWS), BF)
     s.dx_send = pltpu.VMEM((4, ROWS, D), BF)
-    s.dx = pltpu.VMEM((4, ROWS, D), BF)
+    s.dx_end = pltpu.VMEM((3, ROWS, D), BF)
+    s.dx_middle = pltpu.VMEM((2, ROWS, D), BF)
+    s.dx_got = pltpu.VMEM((2, ROWS, D), BF)
+    s.dx_back = pltpu.VMEM((ROWS, D), BF)
+    s.dx_last = pltpu.VMEM((ROWS, D), BF)
     s.column = pltpu.VMEM((D, ROWS), F32)
     s.heads = pltpu.VMEM((2, 2, HW, HEAD_COLS), BF)
     s.heads_core = pltpu.VMEM((2, HW, HEAD_COLS), BF)
@@ -538,19 +546,23 @@
     s.heads_y = pltpu.VMEM((HW // 2, HEAD_COLS), BF)
     s.heads_done = pltpu.VMEM((4, HW // 2, HEAD_COLS), BF)
     s.part = [pltpu.VMEM((2, 2, *shape), BF) for shape in LOTS]
-    s.got = [
-        [pltpu.VMEM((2, *shape), BF), pltpu.VMEM((2, *shape), BF), pltpu.VMEM(shape, BF)]
-        for shape in LOTS
-    ]
-    s.sum = [[pltpu.VMEM((2, *shape), BF), pltpu.VMEM((2, *shape), BF)] for shape in LOTS]
-    s.own = {lot: pltpu.VMEM(LOTS[lot], BF) for lot in LOT_IN}
+    def lots(*dims):
+        return [
+            pltpu.VMEM((*dims[1 if k in LOT_PAIR else 0], *shape), BF) for k, shape in enumerate(LOTS)
+        ]
+
+    steps = [((2, 2), (2,)), ((2,), (2,)), ((), ())]
+    s.got = [list(lot) for lot in zip(*(lots(*step) for step in steps))]
+    s.sum = [list(lot) for lot in zip(*(lots(*step) for step in steps[:2]))]
+    s.own = {k: pltpu.VMEM(LOTS[k], BF) for k in LOT_IN}
     s.done = [pltpu.VMEM((2, 2, *shape), BF) for shape in LOTS]
     s.smalls = pltpu.VMEM((GROUP, 16, HW), F32)
     s.sg = pltpu.VMEM((16, D), F32)
-    s.sg_rows = pltpu.VMEM((16, D), F32)
+    s.sg_all = pltpu.VMEM((16, D), F32)
+    s.sg_rows = pltpu.VMEM((2, 8, D), F32)
     s.sg_w = pltpu.VMEM((GROUP, 16, D), F32)
-    s.sg_z = pltpu.VMEM((4, 16, D), F32)
-    s.sg_y = pltpu.VMEM((2, 16, D), F32)
+    s.sg_z = pltpu.VMEM((4, 8, D), F32)
+    s.sg_y = pltpu.VMEM((2, 8, D), F32)
     s.out_low = pltpu.VMEM((ROWS, D), BF)
     return vars(s)
 
@@ -772,106 +784,98 @@
         arrived((key, j), block)
         remote(onward, block, block, bits, 0, like=lambda: S.xt.at[0])
 
-    pump_x(PART_K)
-    pump_x(PART_V)
-    pump_x(PART_Q)
-    for j in (1, 2, 3):
-        arrived((SMALL, j), S.small.at[bit_xor(w, j)])
-    S.vectors[0:8, :] = jnp.concatenate(
-        [S.small[i, 0:8, 0:HW].astype(F32) for i in range(GROUP)], axis=1
-    )
-    small = [S.small[i, 8:16, :].astype(F32) for i in range(GROUP)]
-    S.vectors[8:16, :] = jnp.concatenate(
-        [part[0:1] for part in small]
-        + [sum(part[1:2] + part[2:3] for part in small), jnp.zeros((3, D), F32)],
-        axis=0,
-    )
-
     def vector(row):
         return S.vectors[row : row + 1, :]
 
-    arrived((X_LINE, 1), S.xt.at[block_on(1, b)])
-
-    @only(False)
+    def to_group(key, source_of, everywhere):
+        for j in (1, 2, 3):
+            to = bit_xor(w, j)
+            remote((*key, j), source_of(to), everywhere.at[w], 0, j)
+
+    def from_group(key, everywhere):
+        for j in (1, 2, 3):
+            arrived((*key, j), everywhere.at[bit_xor(w, j)])
+
+    def to_near(key, source, everywhere):
+        for j in (1, 2):
+            remote((key, j), source, everywhere.at[w], 0, j)
+
+    def pass_to_core(key, everywhere):
+        slot = everywhere.at[bit_xor(w, 2)]
+        arrived((key, 2), slot)
+        remote((key, 3), slot, slot, 0, 1)
+
+    def from_near(key, everywhere):
+        for j in (1, 3):
+            arrived((key, j), everywhere.at[bit_xor(w, j)])
+
+    def lanes(parts):
+        return jnp.concatenate(parts, axis=1)
+
+    finishing = []
+
+    def small_vectors():
+        for j in (1, 2, 3):
+            arrived((SMALL, j), S.small.at[bit_xor(w, j)])
+        S.vectors[0:8, :] = jnp.concatenate(
+            [S.small[i, 0:8, 0:HW].astype(F32) for i in range(GROUP)], axis=1
+        )
+        small = [S.small[i, 8:16, :].astype(F32) for i in range(GROUP)]
+        S.vectors[8:16, :] = jnp.concatenate(
+            [part[0:1] for part in small]
+            + [sum(part[1:2] + part[2:3] for part in small), jnp.zeros((3, D), F32)],
+            axis=0,
+        )
+
     def pass_near_end():
-        block = S.xt.at[block_on(1, b)]
-        remote((X_LINE, 2), block, block, 6, 0, like=lambda: S.xt.at[0])
-        pass_x(X_LINE, 3, (X_EDGE, 2), 2)
-
-    pump_second(PART_K)
-    pump_second(PART_V)
-    pump_second(PART_Q)
-    for i, (name, bias) in enumerate(((PART_K, None), (PART_V, 1), (PART_Q, 0))):
-        rows = slice(HW * i, HW * (i + 1))
-        weight_ready(name)
-        S.turned[...] = S.full[name][...].reshape(D, SLICE).T
-        S.head_weight[rows, :] = S.turned[pl.ds(first_row, HW), :]
-        if bias is None:
-            S.head_bias[rows, :] = jnp.zeros((HW, ROWS), F32)
-        else:
-            row = S.vectors[bias : bias + 1, pl.ds(first_col, SLICE)]
-            S.tall_bias[...] = jnp.broadcast_to(row, (ROWS, SLICE)).T
-            S.head_bias[rows, :] = S.tall_bias[pl.ds(first_row, HW), :]
+        arrived((X_LINE, 1), S.xt.at[block_on(1, b)])
+
+        @only(False)
+        def to_other_middle():
+            block = S.xt.at[block_on(1, b)]
+            remote((X_LINE, 2), block, block, 6, 0, like=lambda: S.xt.at[0])
+
+    def pass_middle():
+        @only(False)
+        def to_near_end():
+            pass_x(X_LINE, 3, (X_EDGE, 2), 2)
+
+    def pass_far_end():
+        @only(False)
+        def to_near_end():
+            pass_x(X_LINE, 2, (X_EDGE, 3), 2)
+
+    def head_weights():
+        for name in (PART_K, PART_V, PART_Q):
+            weight_ready(name)
+        for i, (name, bias) in enumerate(((PART_K, None), (PART_V, 1), (PART_Q, 0))):
+            rows = slice(HW * i, HW * (i + 1))
+            S.turned[...] = S.full[name][...].reshape(D, SLICE).T
+            S.head_weight[rows, :] = S.turned[pl.ds(first_row, HW), :]
+            if bias is None:
+                S.head_bias[rows, :] = jnp.zeros((HW, ROWS), F32)
+            else:
+                row = S.vectors[bias : bias + 1, pl.ds(first_col, SLICE)]
+                S.tall_bias[...] = jnp.broadcast_to(row, (ROWS, SLICE)).T
+                S.head_bias[rows, :] = S.tall_bias[pl.ds(first_row, HW), :]
 
     def project(j):
+        if j > 1:
+
+            @only(True)
+            def from_middle():
+                arrived((X_EDGE, j), S.xt.at[block_on(j, b)])
+
         block = block_on(j, b)
         out = matmul(S.head_weight[...], S.xt[block]) + S.head_bias[...]
         S.kv[block] = out[0 : 2 * HW].astype(BF)
         S.q[block // 2] = out[2 * HW :].astype(BF)
         remote((KEY_VALUE, j), S.kv.at[block], S.kv.at[block], 1, 0)
 
-    project(0)
-    project(1)
-    pump_x(O)
-    pump_x(IN, 0)
-
-    @only(False)
-    def pass_far_end():
-        pass_x(X_LINE, 2, (X_EDGE, 3), 2)
-
-    @only(True)
-    def from_middle():
-        arrived((X_EDGE, 2), S.xt.at[block_on(2, b)])
-
-    project(2)
-    pump_x(IN, 1)
-
-    @only(True)
-    def from_far_end():
-        arrived((X_EDGE, 3), S.xt.at[block_on(3, b)])
-
-    project(3)
-    pump_x(IN, 2)
-
-    def to_group(key, source_of, everywhere):
-        for j in (1, 2, 3):
-            to = bit_xor(w, j)
-            remote((*key, j), source_of(to), everywhere.at[w], 0, j)
-
-    def from_group(key, everywhere):
-        for j in (1, 2, 3):
-            arrived((*key, j), everywhere.at[bit_xor(w, j)])
-
-    def to_near(key, source, everywhere):
-        for j in (1, 2):
-            remote((key, j), source, everywhere.at[w], 0, j)
-
-    def pass_to_core(key, everywhere):
-        slot = everywhere.at[bit_xor(w, 2)]
-        arrived((key, 2), slot)
-        remote((key, 3), slot, slot, 0, 1)
-
-    def from_near(key, everywhere):
-        for j in (1, 3):
-            arrived((key, j), everywhere.at[bit_xor(w, j)])
-
     score_scale = 1.0 / math.sqrt(HD)
 
     def wide(ref, h):
-        return jnp.concatenate([ref[i, HD * h : HD * (h + 1), :] for i in range(4)], axis=1)
-
-    S.mix[...] = jnp.zeros(S.mix.shape, F32)
-    S.total[...] = jnp.zeros(S.total.shape, F32)
+        return lanes([ref[i, HD * h : HD * (h + 1), :] for i in range(4)])
 
     def attend_block(block):
         allowed = key_code(block) == query_code
@@ -883,52 +887,46 @@
             value_t = S.kv[block, HW + HD * h : HW + HD * (h + 1), :]
             S.mix[h] += matmul(value_t, weights.astype(BF))
 
-    @pl.loop(0, 4)
-    def attend_line(i):
-        attend_block(2 * i + b)
-
-    pump_second(O)
-    pump_x(IN, 3)
-    pump_second(IN, 0)
-    pump_x(OUT, 0)
-    for j in range(4):
+    def attend_line():
+        S.mix[...] = jnp.zeros(S.mix.shape, F32)
+        S.total[...] = jnp.zeros(S.total.shape, F32)
+
+        @pl.loop(0, 4)
+        def every_block(i):
+            attend_block(2 * i + b)
+
+    def attend_pair(j):
         arrived((KEY_VALUE, j), S.kv.at[block_on(j, 1 - b)])
         attend_block(block_on(j, 1 - b))
-        if j == 0:
-            pump_second(IN, 1)
-        if j == 2:
-            pump_x(OUT, 1)
-
-    for h in range(HEADS):
-        context_t = (S.mix[h] / S.total[h, 0:1, :]).astype(BF)
-        for i in range(4):
-            S.ctx_send[i, HD * h : HD * (h + 1), :] = context_t[:, ROWS * i : ROWS * (i + 1)]
-    for j in (1, 2, 3):
-        to = bit_xor(a, j)
-        remote((CONTEXT, j), S.ctx_send.at[to], S.ctx.at[a], 2 * j, 0)
-    S.ctx[a] = S.ctx_send[a]
-    weight_ready(O)
-    pump_second(IN, 2)
-    pump_x(OUT, 2)
-    pump_second(OUT, 0)
-    for j in (1, 2, 3):
-        arrived((CONTEXT, j), S.ctx.at[bit_xor(a, j)])
-
-    to_group((CONTEXT_ALL,), lambda to: S.ctx.at[pl.ds(2 * (to // 2), 2)], S.ctx_all)
-    S.ctx_all[w] = S.ctx[pl.ds(2 * x, 2)]
-    attn = tn(S.ctx[...].reshape(D, ROWS), square(O)) + vector(2)
-    first_sum = x_low.astype(F32) + attn
-    normal_one, inverse_one = norm_parts(first_sum)
-    settled = normal_one * vector(3) + vector(4)
-    settled_low = settled.astype(BF)
-    S.first[...] = normal_one
-    S.keep[...] = settled
-    S.set_low[...] = settled_low
-    to_near(SETTLED_ALL, S.set_low, S.set_all)
-    S.set_all[w] = settled_low
-    pump_second(IN, 3)
-    pump_x(OUT, 3)
-    pump_second(OUT, 1)
+
+    def send_context():
+        for h in range(HEADS):
+            context_t = (S.mix[h] / S.total[h, 0:1, :]).astype(BF)
+            for i in range(4):
+                S.ctx_send[i, HD * h : HD * (h + 1), :] = context_t[:, ROWS * i : ROWS * (i + 1)]
+        for j in (1, 2, 3):
+            to = bit_xor(a, j)
+            remote((CONTEXT, j), S.ctx_send.at[to], S.ctx.at[a], 2 * j, 0)
+        S.ctx[a] = S.ctx_send[a]
+
+    def first_norm():
+        weight_ready(O)
+        for j in (1, 2, 3):
+            arrived((CONTEXT, j), S.ctx.at[bit_xor(a, j)])
+        attn = tn(S.ctx[...].reshape(D, ROWS), square(O)) + vector(2)
+        normal_one, inverse_one = norm_parts(S.x[...].astype(F32) + attn)
+        settled = normal_one * vector(3) + vector(4)
+        S.first[...] = normal_one
+        S.inverse[...] = jnp.broadcast_to(inverse_one, (ROWS, 128))
+        S.keep[...] = settled
+        S.set_low[...] = settled.astype(BF)
+        to_near(SETTLED_ALL, S.set_low, S.set_all)
+        S.set_all[w] = S.set_low[...]
+        to_group((CONTEXT_ALL,), lambda to: S.ctx.at[pl.ds(2 * (to // 2), 2)], S.ctx_all)
+        S.ctx_all[w] = S.ctx[pl.ds(2 * x, 2)]
+
+    def pass_settled():
+        pass_to_core(SETTLED_ALL, S.set_all)
 
     def gelu(inner):
         return 0.5 * inner * (1.0 + jnp.tanh(GELU_C * (inner + 0.044715 * inner * inner * inner)))
@@ -940,99 +938,99 @@
             GELU_C * (1.0 + 3 * 0.044715 * squared)
         )
 
-    for t in range(4):
+    def feed_in(t):
         weight_ready(IN, (t,), t == 0)
         w_part = S.full[IN][:, :, D * t : D * (t + 1)].reshape(D, D)
-        inner = matmul(settled_low, w_part) + vector(8 + t)
+        inner = matmul(S.set_low[...], w_part) + vector(8 + t)
         S.inner[t] = inner
         S.act[t] = gelu(inner).astype(BF)
-        if t == 1:
-            pump_second(OUT, 2)
-    pump_second(OUT, 3)
-    pass_to_core(SETTLED_ALL, S.set_all)
-    weight_ready(OUT, range(4))
-    branch = vector(5)
-    for t in range(4):
-        branch = branch + matmul(S.act[t], S.full[OUT][t])
-    normal_two, inverse_two = norm_parts(S.keep[...] + branch)
-    result = normal_two * vector(6) + vector(7)
-    S.out_low[...] = result.astype(BF)
-    finishing = [local(OUTPUT, S.out_low, output)]
-    loads[TEACHER].wait()
-    diff = jnp.where(own_live, result - S.teacher[...].astype(F32), 0.0)
-    count = vector(12)
-    upstream = diff * ((ROWS * CTX * GROUP) / count)
-    S.sg[...] = jnp.zeros((16, D), F32)
 
     def note(row, value):
         S.sg[row : row + 1, :] = jnp.sum(value.astype(F32), axis=0, keepdims=True)
 
-    note(12, diff * diff)
-    S.sg[13:14, :] = count * (1.0 / (CTX * GROUP))
-    note(6, upstream * normal_two)
-    note(7, upstream)
-
-    d_second = norm_back(upstream * vector(6), normal_two, inverse_two)
-    branch_grad = d_second.astype(BF)
-    S.bg[...] = branch_grad
-    to_near(BRANCH_GRAD_ALL, S.bg, S.bg_all)
-    S.bg_all[w] = branch_grad
-    note(5, branch_grad)
-    d_settled = d_second
-    for t in range(4):
-        d_act = right_product(branch_grad, S.full[OUT][t])
-        inner = S.inner[t]
-        inner_grad = (d_act * gelu_slope(inner)).astype(BF)
-        note(8 + t, inner_grad)
-        w_part = S.full[IN][:, :, D * t : D * (t + 1)].reshape(D, D)
-        d_settled = d_settled + right_product(inner_grad, w_part)
-    pass_to_core(BRANCH_GRAD_ALL, S.bg_all)
-    normal_one = S.first[...]
-    note(3, d_settled * normal_one)
-    note(4, d_settled)
-    d_first = norm_back(d_settled * vector(3), normal_one, inverse_one)
-    S.keep[...] = d_first
-    attn_grad = d_first.astype(BF)
-    note(2, attn_grad)
-    context_grad = right_product(attn_grad, square(O)).T.astype(BF)
-    for i in range(4):
-        S.cg_send[i] = context_grad[HW * i : HW * (i + 1), :]
-    for j in (1, 2, 3):
-        to = bit_xor(a, j)
-        remote((CONTEXT_GRAD, j), S.cg_send.at[to], S.cg.at[a], 2 * j, 0)
-    S.cg[a] = S.cg_send[a]
-    for i in range(2):
-        S.ag_half[i] = attn_grad[:, 384 * i : 384 * (i + 1)]
-    to_group((ATTN_GRAD_ALL,), lambda to: S.ag_half.at[to % 2], S.ag_all)
-    S.ag_all[w] = S.ag_half[core]
+    def result_and_loss():
+        weight_ready(OUT, range(4))
+        branch = vector(5)
+        for t in range(4):
+            branch = branch + matmul(S.act[t], S.full[OUT][t])
+        normal_two, inverse_two = norm_parts(S.keep[...] + branch)
+        result = normal_two * vector(6) + vector(7)
+        S.out_low[...] = result.astype(BF)
+        finishing.append(local(OUTPUT, S.out_low, output))
+        loads[TEACHER].wait()
+        diff = jnp.where(own_live, result - S.teacher[...].astype(F32), 0.0)
+        count = vector(12)
+        upstream = diff * ((ROWS * CTX * GROUP) / count)
+        d_second = norm_back(upstream * vector(6), normal_two, inverse_two)
+        S.bg[...] = d_second.astype(BF)
+        to_near(BRANCH_GRAD_ALL, S.bg, S.bg_all)
+        S.bg_all[w] = S.bg[...]
+        S.keep[...] = d_second
+        S.sg[...] = jnp.zeros((16, D), F32)
+        note(12, diff * diff)
+        S.sg[13:14, :] = count * (1.0 / (CTX * GROUP))
+        note(6, upstream * normal_two)
+        note(7, upstream)
+        note(5, S.bg[...])
+
+    def feed_back():
+        d_settled = S.keep[...]
+        for t in range(4):
+            d_act = right_product(S.bg[...], S.full[OUT][t])
+            inner_grad = (d_act * gelu_slope(S.inner[t])).astype(BF)
+            note(8 + t, inner_grad)
+            w_part = S.full[IN][:, :, D * t : D * (t + 1)].reshape(D, D)
+            d_settled = d_settled + right_product(inner_grad, w_part)
+        S.keep[...] = d_settled
+
+    def pass_branch_grad():
+        pass_to_core(BRANCH_GRAD_ALL, S.bg_all)
+
+    def first_norm_back():
+        d_settled, normal_one = S.keep[...], S.first[...]
+        d_first = norm_back(d_settled * vector(3), normal_one, S.inverse[:, 0:1])
+        attn_grad = d_first.astype(BF)
+        context_grad = right_product(attn_grad, square(O)).T.astype(BF)
+        for i in range(4):
+            S.cg_send[i] = context_grad[HW * i : HW * (i + 1), :]
+        for j in (1, 2, 3):
+            to = bit_xor(a, j)
+            remote((CONTEXT_GRAD, j), S.cg_send.at[to], S.cg.at[a], 2 * j, 0)
+        S.cg[a] = S.cg_send[a]
+        for i in range(2):
+            S.ag_half[i] = attn_grad[:, 384 * i : 384 * (i + 1)]
+        to_group((ATTN_GRAD_ALL,), lambda to: S.ag_half.at[to % 2], S.ag_all)
+        S.ag_all[w] = S.ag_half[core]
+        note(3, d_settled * normal_one)
+        note(4, d_settled)
+        note(2, attn_grad)
+        S.keep[...] = d_first
 
     half = a // 2
 
-    def reduce_pair(lot):
-        remote((REDUCE, lot, 0), S.part[lot].at[1 - b], S.got[lot][0], 1, 0)
-
-    def reduce_end(lot):
-        got = S.got[lot][0]
-        arrived((REDUCE, lot, 0), got)
-        total = S.part[lot][b].astype(F32) + got[...].astype(F32)
-        S.sum[lot][0][...] = total.astype(BF)
+    def y_end(lot):
+        got, total = S.got[lot], S.sum[lot]
+        arrived((REDUCE, lot, 0), got[0])
+        total[0][...] = (S.part[lot][b].astype(F32) + got[0][...].astype(F32)).astype(BF)
 
         @only(True)
         def to_middle():
-            target = S.got[lot][1]
-            remote((REDUCE, lot, 1), S.sum[lot][0], target, 2, 0, like=lambda: target)
-
-    def reduce_middle(lot):
+            remote((REDUCE, lot, 1), total[0], got[1], 2, 0, like=lambda: got[1])
+
+    def y_middle(lot):
         @only(False)
         def swap_halves():
-            got = S.got[lot][1]
-            arrived((REDUCE, lot, 1), got)
-            total = S.sum[lot][0][...].astype(F32) + got[...].astype(F32)
-            S.sum[lot][1][...] = total.astype(BF)
-            there, target = S.sum[lot][1].at[1 - half], S.got[lot][2]
-            remote((REDUCE, lot, 2), there, target, 6, 0, like=lambda: target)
-
-    def reduce_last(lot):
+            got, total = S.got[lot], S.sum[lot]
+            arrived((REDUCE, lot, 1), got[1])
+            total[1][...] = (total[0][...].astype(F32) + got[1][...].astype(F32)).astype(BF)
+            there = total[1].at[1 - half]
+            remote((REDUCE, lot, 2), there, got[2], 6, 0, like=lambda: got[2])
+
+    def y_spread_middle(lot):
+        part = S.done[lot].at[b, half]
+        remote((SPREAD, lot, 0), part, part, 6, 0, like=lambda: S.done[lot].at[0, 0])
+
+    def y_last(lot):
         @only(False)
         def own_half():
             got = S.got[lot][2]
@@ -1048,73 +1046,132 @@
                     remote((GROUP_X, lot, q), own.at[to], slot, 0, q, like=lambda: own.at[0])
             else:
                 S.done[lot][b, half] = total
-                spread_middle(lot)
-
-    def spread_middle(lot):
-        part = S.done[lot].at[b, half]
-        remote((SPREAD, lot, 0), part, part, 6, 0, like=lambda: S.done[lot].at[0, 0])
-
-    def spread_group(lot):
+                y_spread_middle(lot)
+
+    def y_group(lot):
         @only(False)
         def gathered():
             for q in (1, 2, 3):
                 arrived((GROUP_X, lot, q), S.done[lot].at[b, half, bit_xor(w, q)])
-            spread_middle(lot)
-
-    def spread_end(lot):
+            y_spread_middle(lot)
+
+    def y_spread_end(lot):
         @only(False)
         def to_end():
+            done = S.done[lot].at[b]
             arrived((SPREAD, lot, 0), S.done[lot].at[b, 1 - half])
-            done = S.done[lot].at[b]
             remote((SPREAD, lot, 1), done, done, 2, 0, like=lambda: S.done[lot].at[0])
 
     def result_of(lot):
         return grad_in[lot - LOT_IN[0]] if lot in LOT_IN else grad_out.at[lot - LOT_OUT[0]]
 
-    def give(lot):
+    def y_give(lot):
+        done = S.done[lot].at[b]
+
         @only(True)
         def from_middle_device():
-            arrived((SPREAD, lot, 1), S.done[lot].at[b])
-
-        done = S.done[lot].at[b]
+            arrived((SPREAD, lot, 1), done)
+
         if lot not in LOT_O:
             out = result_of(lot).at[b]
             remote((GIVE, lot), done, out, 1, 0)
             finishing.append(local((GIVE, lot), done, out))
             return
-        remote((GIVE, lot), done, grad_o.at[core], 1, 0, core, 2, 2 * x + b)
+        remote((GIVE, 0), done, grad_o.at[core], 1, 0, core, 2, 2 * x + b)
 
         @pl.when(core == b)
         def keep_own():
-            local((OWN, lot), done, grad_o.at[core])
+            local((OWN, 0), done, grad_o.at[core])
 
         @pl.when(core != b)
         def give_core():
-            remote((OWN, lot), done, grad_o.at[core], 0, 1)
+            remote((OWN, 0), done, grad_o.at[core], 0, 1)
             started.pop()
 
-    def settle(lot):
-        if lot not in LOT_O:
+    def settle():
+        for lot in LOT_PAIR[1:]:
             arrived((GIVE, lot), result_of(lot).at[1 - b])
-            return
-        done = S.done[lot].at[b]
+        done = S.done[0].at[b]
 
         @pl.when(core == b)
         def from_chip():
             pltpu.make_async_copy(
-                done, grad_o.at[core], local_sems.at[locals_.take((OWN, lot))]
+                done, grad_o.at[core], local_sems.at[locals_.take((OWN, 0))]
             ).wait()
-            arrived((OWN, lot), grad_o.at[1 - core])
+            arrived((OWN, 0), grad_o.at[1 - core])
 
         @pl.when(core != b)
         def from_partner():
-            arrived((GIVE, lot), grad_o.at[0], 0)
-            arrived((GIVE, lot), grad_o.at[1], 1)
-            sent = numbers.take((OWN, lot))
+            arrived((GIVE, 0), grad_o.at[0], 0)
+            arrived((GIVE, 0), grad_o.at[1], 1)
+            sent = numbers.take((OWN, 0))
             pltpu.make_async_copy(done, done, send_sems.at[sent]).wait()
 
-    def lanes(parts):
-        return jnp.concatenate(parts, axis=1)
+    def reduce_start(lot):
+        @only(True)
+        def to_middle():
+            target = S.got[lot][0]
+            remote((REDUCE, lot, 0), S.part[lot], target, 2, 0, like=lambda: target)
+
+    def reduce_middle(lot):
+        @only(False)
+        def swap_halves():
+            got = S.got[lot][0]
+            arrived((REDUCE, lot, 0), got)
+            total = S.part[lot][...].astype(F32) + got[...].astype(F32)
+            S.sum[lot][0][...] = total.astype(BF)
+            there, target = S.sum[lot][0].at[1 - half], S.got[lot][1]
+            remote((REDUCE, lot, 1), there, target, 6, 0, like=lambda: target)
+
+    def reduce_pair(lot):
+        @only(False)
+        def swap_quarters():
+            got = S.got[lot][1]
+            arrived((REDUCE, lot, 1), got)
+            total = S.sum[lot][0][half].astype(F32) + got[...].astype(F32)
+            S.sum[lot][1][...] = total.astype(BF)
+            there, target = S.sum[lot][1].at[1 - b], S.got[lot][2]
+            remote((REDUCE, lot, 2), there, target, 1, 0, like=lambda: target)
+
+    def reduce_last(lot):
+        @only(False)
+        def own_quarter():
+            got = S.got[lot][2]
+            arrived((REDUCE, lot, 2), got)
+            total = (S.sum[lot][1][b].astype(F32) + got[...].astype(F32)).astype(BF)
+            S.done[lot][half, b] = total
+            part = S.done[lot].at[half, b]
+            remote((SPREAD, lot, 0), part, part, 1, 0, like=lambda: S.done[lot].at[0, 0])
+
+    def spread_middle(lot):
+        @only(False)
+        def swap_back():
+            arrived((SPREAD, lot, 0), S.done[lot].at[half, 1 - b])
+            part = S.done[lot].at[half]
+            remote((SPREAD, lot, 1), part, part, 6, 0, like=lambda: S.done[lot].at[0])
+
+    def spread_end(lot):
+        @only(False)
+        def to_end():
+            done = S.done[lot]
+            arrived((SPREAD, lot, 1), done.at[1 - half])
+            part = done.at[:, b]
+            remote((SPREAD, lot, 2), part, part, 2, 0, like=lambda: done.at[:, 0])
+
+    def spread_ends(lot):
+        @only(True)
+        def swap_at_ends():
+            done = S.done[lot]
+            part = done.at[:, b]
+            arrived((SPREAD, lot, 2), part)
+            remote((SPREAD, lot, 3), part, part, 1, 0, like=lambda: done.at[:, 0])
+
+    def finish_lot(lot):
+        @only(True)
+        def from_pair():
+            arrived((SPREAD, lot, 3), S.done[lot].at[:, 1 - b])
+
+        finishing.append(local((GIVE, lot), S.done[lot], grad_out.at[lot - LOT_OUT[0]]))
 
     def inner_again():
         from_near(SETTLED_ALL, S.set_all)
@@ -1131,7 +1188,10 @@
         grad = tn(S.act_all[...], S.bg_all[...].reshape(GROUP * ROWS, D)).astype(BF)
         for i, lot in enumerate(LOT_OUT):
             S.part[lot][...] = grad[HW * i : HW * (i + 1)].reshape(2, 2, 48, D)
-            reduce_pair(lot)
+            if lot in LOT_PAIR:
+                remote((REDUCE, lot, 0), S.part[lot].at[1 - b], S.got[lot][0], 1, 0)
+            else:
+                reduce_start(lot)
 
     def in_part():
         branch_grad_all = S.bg_all[...].reshape(GROUP * ROWS, D)
@@ -1144,7 +1204,7 @@
                 side = grad[:, 384 * j : 384 * (j + 1)].reshape(4, 2, 2, 48, 384)
                 for k in range(2):
                     S.part[lot][j, k] = side[:, k, i]
-            reduce_pair(lot)
+            remote((REDUCE, lot, 0), S.part[lot].at[1 - b], S.got[lot][0], 1, 0)
 
     def attention_back():
         for j in (1, 2, 3):
@@ -1189,8 +1249,8 @@
         from_group((ATTN_GRAD_ALL,), S.ag_all)
         context_all = lanes([S.ctx_all[i].reshape(384, ROWS) for i in range(GROUP)])
         grad = matmul(context_all, S.ag_all[...].reshape(GROUP * ROWS, 384))
-        S.part[LOT_O[0]][...] = grad.astype(BF).reshape(2, 2, 96, 384)
-        reduce_pair(LOT_O[0])
+        S.part[0][...] = grad.astype(BF).reshape(2, 2, 96, 384)
+        remote((REDUCE, 0, 0), S.part[0].at[1 - b], S.got[0][0], 1, 0)
 
     def heads_part():
         arrived((KEY_VALUE_GRAD,), S.dkv_pair)
@@ -1207,10 +1267,30 @@
     def input_parts():
         parts = tn(S.grads[0 : 3 * HW, :], S.head_weight[...])
         S.dx_send[...] = parts.astype(BF).reshape(4, ROWS, D)
-        for j in (1, 2, 3):
-            to = bit_xor(a, j)
-            remote((INPUT_PARTS, j), S.dx_send.at[to], S.dx.at[a], 2 * j, 0)
-        S.dx[a] = S.dx_send[a]
+
+        @only(True)
+        def to_middle():
+            for j in (1, 2, 3):
+                source, target = S.dx_send.at[bit_xor(a, j)], S.dx_end.at[j - 1]
+                remote((INPUT_PARTS, j), source, target, 2, 0, like=lambda: S.dx_end.at[0])
+
+    def input_middle():
+        @only(False)
+        def to_other_middle():
+            for j in (1, 2, 3):
+                arrived((INPUT_PARTS, j), S.dx_end.at[j - 1])
+            for i, j in enumerate((3, 2)):
+                both = S.dx_send[bit_xor(a, j)].astype(F32) + S.dx_end[i + 1].astype(F32)
+                S.dx_middle[i] = both.astype(BF)
+            remote((INPUT_PARTS, 4), S.dx_middle, S.dx_got, 6, 0, like=lambda: S.dx_middle)
+
+    def input_end():
+        @only(False)
+        def to_near_end():
+            arrived((INPUT_PARTS, 4), S.dx_got)
+            both = S.dx_send[bit_xor(a, 1)].astype(F32) + S.dx_got[1].astype(F32)
+            S.dx_back[...] = both.astype(BF)
+            remote((INPUT_PARTS, 5), S.dx_back, S.dx_last, 2, 0, like=lambda: S.dx_back)
 
     def vectors_group():
         S.column[...] = jnp.zeros((D, ROWS), F32)
@@ -1223,10 +1303,13 @@
             remote((VECTORS_W, j), S.sg, S.sg_w.at[w], 0, j)
         S.sg_w[w] = S.sg[...]
 
+    own_rows = pl.ds(pl.multiple_of(8 * core, 8), 8)
+
     def vectors_line():
         for j in (1, 2, 3):
             arrived((VECTORS_W, j), S.sg_w.at[bit_xor(w, j)])
-        S.sg_z[a] = (S.sg_w[0] + S.sg_w[1]) + (S.sg_w[2] + S.sg_w[3])
+        S.sg_all[...] = (S.sg_w[0] + S.sg_w[1]) + (S.sg_w[2] + S.sg_w[3])
+        S.sg_z[a] = S.sg_all[own_rows, :]
         for j in (1, 2, 3):
             remote((VECTORS_Z, j), S.sg_z.at[a], S.sg_z.at[a], 2 * j, 0)
 
@@ -1234,16 +1317,20 @@
         for j in (1, 2, 3):
             arrived((VECTORS_Z, j), S.sg_z.at[bit_xor(a, j)])
         S.sg_y[b] = (S.sg_z[0] + S.sg_z[1]) + (S.sg_z[2] + S.sg_z[3])
-        remote(VECTORS_Y, S.sg_y.at[b], S.sg_y.at[b], 1, 0)
+        remote((VECTORS_Y,), S.sg_y.at[b], S.sg_y.at[b], 1, 0)
+
+    def vectors_core():
+        arrived((VECTORS_Y,), S.sg_y.at[1 - b])
+        S.sg_rows[core] = S.sg_y[0] + S.sg_y[1]
+        remote((VECTORS_CORE,), S.sg_rows.at[core], S.sg_rows.at[core], 0, 1)
 
     def vectors_done():
-        arrived(VECTORS_Y, S.sg_y.at[1 - b])
-        everything = S.sg_y[0] + S.sg_y[1]
-        S.sg_rows[...] = everything
+        arrived((VECTORS_CORE,), S.sg_rows.at[1 - core])
+        everything = S.sg_rows[...].reshape(16, D)
         for i in range(4):
             S.smalls[i] = everything[:, HW * i : HW * (i + 1)]
-        finishing.append(local(VECTORS_Y, S.smalls, smalls_out))
-        finishing.append(local(VECTORS_Z, S.sg_rows, rows_out))
+        finishing.append(local((VECTORS_Y,), S.smalls, smalls_out))
+        finishing.append(local((VECTORS_Z,), S.sg_rows, rows_out))
 
     def heads_x():
         for i in range(2):
@@ -1264,85 +1351,175 @@
     def heads_line():
         arrived((HEADS_Y,), S.heads_y)
         S.heads_done[a] = (S.heads_row[b].astype(F32) + S.heads_y[...].astype(F32)).astype(BF)
-        for j in (1, 2, 3):
-            remote((HEADS_LINE, j), S.heads_done.at[a], S.heads_done.at[a], 2 * j, 0)
+        own = S.heads_done.at[a]
+        remote((HEADS_LINE, 1), own, own, 2, 0)
+
+        @only(False)
+        def to_other_middle():
+            remote((HEADS_LINE, 3), own, own, 6, 0, like=lambda: S.heads_done.at[0])
+
+    def pass_heads(key, j, onward, bits):
+        part = S.heads_done.at[bit_xor(a, j)]
+        if key is not None:
+            arrived((key, j), part)
+        remote(onward, part, part, bits, 0, like=lambda: S.heads_done.at[0])
+
+    def heads_near_end():
+        arrived((HEADS_LINE, 1), S.heads_done.at[bit_xor(a, 1)])
+
+        @only(False)
+        def to_other_middle():
+            pass_heads(None, 1, (HEADS_LINE, 2), 6)
+
+    def heads_middle():
+        @only(False)
+        def to_near_end():
+            pass_heads(HEADS_LINE, 3, (HEADS_EDGE, 2), 2)
+
+    def heads_far_end():
+        @only(False)
+        def to_near_end():
+            pass_heads(HEADS_LINE, 2, (HEADS_EDGE, 3), 2)
 
     def heads_pair():
-        for j in (1, 2, 3):
-            arrived((HEADS_LINE, j), S.heads_done.at[bit_xor(a, j)])
+        @only(True)
+        def from_middle():
+            for j in (2, 3):
+                arrived((HEADS_EDGE, j), S.heads_done.at[bit_xor(a, j)])
+
         remote((HEADS_PAIR,), S.heads_done, heads_out.at[b], 1, 0)
         finishing.append(local((HEADS_PAIR,), S.heads_done, heads_out.at[b]))
 
     def input_done():
-        for j in (1, 2, 3):
-            arrived((INPUT_PARTS, j), S.dx.at[bit_xor(a, j)])
-        total = S.keep[...]
-        for i in range(4):
-            total = total + S.dx[i].astype(F32)
-        S.first[...] = total
+        S.first[...] = S.keep[...] + S.dx_send[a].astype(F32)
+
+        @only(True)
+        def at_end():
+            arrived((INPUT_PARTS, 5), S.dx_last)
+            S.first[...] += S.dx_last[...].astype(F32)
+
+        @only(False)
+        def in_middle():
+            S.first[...] += S.dx_end[0].astype(F32) + S.dx_got[0].astype(F32)
+
         finishing.append(local(INPUT_GRAD, S.first, input_grad_out))
 
     for step, *lot in (
+        (pump_x, PART_K),
+        (pump_x, PART_V),
+        (pump_x, PART_Q),
+        (pass_near_end,),
+        (pump_second, PART_K),
+        (small_vectors,),
+        (pump_second, PART_V),
+        (pump_second, PART_Q),
+        (pass_middle,),
+        (head_weights,),
+        (project, 1),
+        (project, 0),
+        (pass_far_end,),
+        (project, 2),
+        (project, 3),
+        (pump_x, O),
+        (pump_x, IN, 0),
+        (attend_line,),
+        (attend_pair, 1),
+        (attend_pair, 2),
+        (attend_pair, 3),
+        (attend_pair, 0),
+        (send_context,),
+        (pump_x, IN, 1),
+        (pump_x, OUT, 0),
+        (pump_second, IN, 0),
+        (pump_second, O),
+        (pump_second, IN, 1),
+        (pump_x, OUT, 1),
+        (pump_x, IN, 2),
+        (pump_x, OUT, 2),
+        (first_norm,),
+        (pump_x, IN, 3),
+        (feed_in, 0),
+        (pump_x, OUT, 3),
+        (pump_second, IN, 2),
+        (pump_second, OUT, 0),
+        (feed_in, 1),
+        (pump_second, OUT, 2),
+        (pass_settled,),
+        (pump_second, OUT, 1),
+        (pump_second, IN, 3),
+        (feed_in, 2),
+        (pump_second, OUT, 3),
+        (feed_in, 3),
+        (result_and_loss,),
+        (feed_back,),
         (inner_again,),
+        (pass_branch_grad,),
+        (first_norm_back,),
         (out_part,),
-        (reduce_end, 3),
-        (reduce_middle, 3),
+        (y_end, 3),
+        (attention_back,),
+        (y_end, 4),
+        (o_part,),
+        (reduce_middle, 6),
+        (y_middle, 4),
+        (y_end, 5),
         (in_part,),
-        (reduce_end, 4),
-        (reduce_end, 5),
-        (reduce_middle, 4),
-        (reduce_end, 6),
-        (reduce_end, 1),
-        (reduce_middle, 6),
-        (reduce_last, 4),
-        (attention_back,),
-        (reduce_last, 6),
-        (reduce_end, 2),
-        (reduce_middle, 5),
-        (reduce_last, 3),
-        (o_part,),
-        (reduce_middle, 1),
-        (spread_end, 4),
-        (reduce_last, 5),
-        (spread_end, 3),
-        (spread_end, 6),
-        (reduce_middle, 2),
-        (reduce_last, 1),
+        (y_last, 4),
+        (y_middle, 3),
+        (y_middle, 5),
         (heads_part,),
-        (give, 3),
         (vectors_group,),
-        (spread_group, 1),
-        (reduce_end, 0),
-        (give, 6),
-        (spread_end, 5),
-        (reduce_last, 2),
+        (y_end, 0),
+        (y_last, 5),
+        (y_last, 3),
+        (y_middle, 0),
+        (y_spread_end, 4),
         (heads_x,),
         (vectors_line,),
-        (spread_end, 1),
-        (spread_group, 2),
-        (reduce_middle, 0),
-        (give, 5),
+        (y_spread_end, 5),
+        (y_last, 0),
+        (y_end, 1),
         (heads_y,),
-        (give, 4),
-        (spread_end, 2),
-        (reduce_last, 0),
+        (y_spread_end, 3),
+        (reduce_pair, 6),
+        (y_give, 4),
+        (y_middle, 1),
+        (y_spread_end, 0),
+        (heads_line,),
+        (reduce_last, 6),
+        (y_give, 5),
+        (y_end, 2),
+        (y_give, 0),
+        (y_give, 3),
+        (y_last, 1),
+        (heads_near_end,),
+        (input_parts,),
+        (heads_middle,),
+        (y_group, 1),
+        (heads_far_end,),
+        (y_middle, 2),
         (vectors_pair,),
-        (heads_line,),
-        (give, 1),
-        (input_parts,),
+        (y_spread_end, 1),
+        (spread_middle, 6),
+        (heads_pair,),
+        (y_last, 2),
+        (spread_end, 6),
+        (y_give, 1),
+        (y_group, 2),
+        (vectors_core,),
+        (y_spread_end, 2),
+        (spread_ends, 6),
+        (y_give, 2),
+        (input_middle,),
+        (input_end,),
+        (input_done,),
         (vectors_done,),
-        (spread_end, 0),
-        (give, 2),
-        (heads_pair,),
-        (give, 0),
-        (input_done,),
-
+        (finish_lot, 6),
     ):
         step(*lot)
 
     arrived((HEADS_PAIR,), heads_out.at[1 - b])
-    for lot in range(len(LOTS)):
-        settle(lot)
+    settle()
     for copy in finishing:
         copy.wait()
     for copy in started:
@@ -1379,9 +1556,9 @@
         w = lax.axis_index("wsh")
         for i in range(8):
             vectors[i][...] = smalls[w, i, :]
-        inner_bias[...] = rows[8 + w, :]
-        error = jnp.sum(rows[12:13, :])
-        count = jnp.max(rows[13:14, :])
+        inner_bias[...] = rows[1, w, :]
+        error = jnp.sum(rows[1, 4:5, :])
+        count = jnp.max(rows[1, 5:6, :])
         loss[0] = error / (count * D)
 
 
@@ -1419,7 +1596,7 @@
             low(4, 2, 2, 48, D),
             low(2, 4, HW // 2, HEAD_COLS),
             full(GROUP, 16, HW),
-            full(16, D),
+            full(2, 8, D),
         ),
         in_specs=[hbm] * 8 + [smem] * 2 + [vmem] * 9,
         out_specs=[hbm] * 9,
@@ -1473,7 +1650,7 @@
             pl.BlockSpec((2, 2, 2, 48, D), lambda i: (i, 0, 0, 0, 0)),
             pl.BlockSpec((1, 4, HW // 2, HEAD_COLS), lambda i: (i, 0, 0, 0)),
             whole(GROUP, 16, HW),
-            whole(16, D),
+            whole(2, 8, D),
             by_row,
             by_row,
         ],

time: 169 us -> 156 us (0.923); the launches traced: 166 us -> 156 us
  Pallas kernels: 164 us -> 155 us
    pallas_call x1, Pallas kernels: 159 us -> 149 us  [fused_body(): pl.pallas_call(fused_kernel, out_shape=(low(ROWS, D), full(ROWS, D), low(...]
where the time goes in v4:
time: 156 us
  Pallas kernels  155 us (99%)
    pallas_call x1, Pallas kernels, fused_body(): pl.pallas_call(fused_kernel, out_shape=(low(ROWS, D), full(ROWS, D), low(...  149 us
    pallas_call x1, Pallas kernels, fused_body(): pl.pallas_call(finish_kernel, grid=(steps,), out_shape=(full(HW, D),) * 4...  5.18 us

profile of v4, /device:TPU:0, one launch (start us, length us, event | category | flops | bytes accessed | tf_op | source)
XLA Modules:
  0.0 156.1 jit_solution(14583085078804722506)
XLA Ops:
  1.3 149.5 %layer.1 = (bf16[128,768]{1,0:T(8,128)(2,1)}, f32[128,768]{1,0:T(8,128)}, bf16[2,2,96,384]{3,2,1,0:T(8,128)(2,1)}, bf16[2,2,4,48,384]{4,3,2,1,0:T(8,128)(2,1)}, ...) custom-call(bf16[1,128,768]{2,1,0:T(8,128)(2,1)} %refs_0_.1, ...), custom_call_target="tpu_custom_call" | custom-call | tf_op jit(solution)/shard_map/layer/pallas_call | solution.py:1588
  150.8 5.2 %finish.1 = (f32[192,768]{1,0:T(8,128)}, f32[192,768]{1,0:T(8,128)}, f32[192,768]{1,0:T(8,128)}, f32[192,768]{1,0:T(8,128)}, f32[192,3072]{1,0:T(8,128)}, /*inde...) custom-call(bf16[2,2,96,384]{3,2,1,0:T(8,128)(2,1)} %get-tuple-eleme, ...), custom_call_target="tpu_custom_call" | custom-call | tf_op jit(solution)/shard_map/finish/pallas_call | solution.py:1639

commit v5 on v4

--- a/solution.py
+++ b/solution.py
@@ -403,9 +403,9 @@
 Q, K, V, O, IN, OUT, PART_Q, PART_K, PART_V = range(9)
 SLICE = 256
 WEIGHT_SHAPES = [(192, 768)] * 4 + [(192, 3072), (768, 768)] + [(192, SLICE)] * 3
-SECOND_WAY = {O: 1, IN: 1, OUT: 2, PART_Q: 1, PART_K: 1, PART_V: 1}
+SECOND_WAY = {O: 1, IN: 2, OUT: 1, PART_Q: 1, PART_K: 1, PART_V: 1}
 LOT_O, LOT_IN, LOT_OUT = (0,), (1, 2), (3, 4, 5, 6)
-LOT_PAIR = LOT_O + LOT_IN + LOT_OUT[:3]
+LOT_PAIR = LOT_O + LOT_IN + LOT_OUT[:2]
 LOTS = [(96, 384)] + [(4, 48, 384)] * 2 + [(48, D)] * 4
 PIECES = {IN: (1, 4), OUT: (4, 1)}
 HEAD_COLS = 640
@@ -1309,14 +1309,32 @@
         for j in (1, 2, 3):
             arrived((VECTORS_W, j), S.sg_w.at[bit_xor(w, j)])
         S.sg_all[...] = (S.sg_w[0] + S.sg_w[1]) + (S.sg_w[2] + S.sg_w[3])
-        S.sg_z[a] = S.sg_all[own_rows, :]
-        for j in (1, 2, 3):
-            remote((VECTORS_Z, j), S.sg_z.at[a], S.sg_z.at[a], 2 * j, 0)
+        S.sg_z[0] = S.sg_all[own_rows, :]
+
+        @only(True)
+        def to_middle():
+            remote((VECTORS_Z, 1), S.sg_z.at[0], S.sg_z.at[1], 2, 0, like=lambda: S.sg_z.at[1])
+
+    def vectors_middle():
+        @only(False)
+        def to_other_middle():
+            arrived((VECTORS_Z, 1), S.sg_z.at[1])
+            S.sg_z[2] = S.sg_z[0] + S.sg_z[1]
+            remote((VECTORS_Z, 2), S.sg_z.at[2], S.sg_z.at[3], 6, 0, like=lambda: S.sg_z.at[2])
+
+    def vectors_end():
+        @only(False)
+        def to_end():
+            arrived((VECTORS_Z, 2), S.sg_z.at[3])
+            S.sg_y[b] = S.sg_z[2] + S.sg_z[3]
+            whole = S.sg_y.at[b]
+            remote((VECTORS_Z, 3), whole, whole, 2, 0, like=lambda: S.sg_y.at[0])
 
     def vectors_pair():
-        for j in (1, 2, 3):
-            arrived((VECTORS_Z, j), S.sg_z.at[bit_xor(a, j)])
-        S.sg_y[b] = (S.sg_z[0] + S.sg_z[1]) + (S.sg_z[2] + S.sg_z[3])
+        @only(True)
+        def from_middle():
+            arrived((VECTORS_Z, 3), S.sg_y.at[b])
+
         remote((VECTORS_Y,), S.sg_y.at[b], S.sg_y.at[b], 1, 0)
 
     def vectors_core():
@@ -1404,113 +1422,130 @@
 
         finishing.append(local(INPUT_GRAD, S.first, input_grad_out))
 
+    marked = []
+
+    def mark():
+        marked.extend(started)
+        started.clear()
+
+    def retire():
+        for copy in marked:
+            copy.wait_send()
+        marked.clear()
+
     for step, *lot in (
+        (pass_near_end,),
         (pump_x, PART_K),
+        (pass_middle,),
+        (pump_x, PART_Q),
         (pump_x, PART_V),
-        (pump_x, PART_Q),
-        (pass_near_end,),
+        (pump_second, PART_Q),
+        (pump_x, O),
+        (small_vectors,),
+        (pass_far_end,),
+        (pump_second, PART_V),
         (pump_second, PART_K),
-        (small_vectors,),
-        (pump_second, PART_V),
-        (pump_second, PART_Q),
-        (pass_middle,),
         (head_weights,),
+        (project, 0),
+        (project, 2),
         (project, 1),
-        (project, 0),
-        (pass_far_end,),
-        (project, 2),
+        (pump_x, IN, 0),
+        (pump_x, IN, 1),
         (project, 3),
-        (pump_x, O),
-        (pump_x, IN, 0),
+        (pump_second, O),
         (attend_line,),
+        (attend_pair, 0),
+        (pump_x, IN, 3),
         (attend_pair, 1),
         (attend_pair, 2),
+        (pump_x, OUT, 0),
+        (pump_second, IN, 1),
         (attend_pair, 3),
-        (attend_pair, 0),
         (send_context,),
-        (pump_x, IN, 1),
-        (pump_x, OUT, 0),
+        (pump_x, IN, 2),
+        (pump_x, OUT, 1),
         (pump_second, IN, 0),
-        (pump_second, O),
-        (pump_second, IN, 1),
-        (pump_x, OUT, 1),
-        (pump_x, IN, 2),
         (pump_x, OUT, 2),
+        (pump_second, OUT, 1),
+        (pump_second, IN, 3),
+        (pump_x, OUT, 3),
         (first_norm,),
-        (pump_x, IN, 3),
         (feed_in, 0),
-        (pump_x, OUT, 3),
-        (pump_second, IN, 2),
         (pump_second, OUT, 0),
         (feed_in, 1),
         (pump_second, OUT, 2),
-        (pass_settled,),
-        (pump_second, OUT, 1),
-        (pump_second, IN, 3),
+        (pump_second, IN, 2),
         (feed_in, 2),
         (pump_second, OUT, 3),
         (feed_in, 3),
         (result_and_loss,),
+        (pass_settled,),
         (feed_back,),
+        (first_norm_back,),
+        (mark,),
         (inner_again,),
         (pass_branch_grad,),
-        (first_norm_back,),
         (out_part,),
+        (attention_back,),
+        (reduce_middle, 5),
+        (reduce_pair, 5),
         (y_end, 3),
-        (attention_back,),
-        (y_end, 4),
         (o_part,),
         (reduce_middle, 6),
+        (y_middle, 3),
+        (reduce_last, 5),
+        (in_part,),
+        (y_last, 3),
+        (y_end, 4),
+        (heads_part,),
         (y_middle, 4),
-        (y_end, 5),
-        (in_part,),
+        (y_end, 0),
+        (vectors_group,),
+        (spread_middle, 5),
+        (y_spread_end, 3),
+        (heads_x,),
         (y_last, 4),
-        (y_middle, 3),
-        (y_middle, 5),
-        (heads_part,),
-        (vectors_group,),
-        (y_end, 0),
-        (y_last, 5),
-        (y_last, 3),
         (y_middle, 0),
+        (vectors_line,),
+        (vectors_middle,),
+        (spread_end, 5),
         (y_spread_end, 4),
-        (heads_x,),
-        (vectors_line,),
-        (y_spread_end, 5),
+        (y_end, 1),
         (y_last, 0),
-        (y_end, 1),
         (heads_y,),
-        (y_spread_end, 3),
+        (y_middle, 1),
         (reduce_pair, 6),
-        (y_give, 4),
-        (y_middle, 1),
+        (spread_ends, 5),
+        (retire,),
+        (vectors_end,),
         (y_spread_end, 0),
         (heads_line,),
+        (y_end, 2),
         (reduce_last, 6),
-        (y_give, 5),
-        (y_end, 2),
+        (y_give, 3),
+        (y_give, 4),
+        (y_last, 1),
+        (vectors_pair,),
         (y_give, 0),
-        (y_give, 3),
-        (y_last, 1),
         (heads_near_end,),
-        (input_parts,),
         (heads_middle,),
         (y_group, 1),
         (heads_far_end,),
         (y_middle, 2),
-        (vectors_pair,),
-        (y_spread_end, 1),
+        (input_parts,),
         (spread_middle, 6),
         (heads_pair,),
         (y_last, 2),
+        (y_spread_end, 1),
         (spread_end, 6),
         (y_give, 1),
         (y_group, 2),
+        (spread_ends, 6),
+        (input_middle,),
+        (y_spread_end, 2),
+        (y_give, 2),
         (vectors_core,),
-        (y_spread_end, 2),
-        (spread_ends, 6),
-        (y_give, 2),
-        (input_middle,),
+        (finish_lot, 5),
         (input_end,),
         (input_done,),
         (vectors_done,),
@@ -1524,42 +1559,83 @@
         copy.wait()
     for copy in started:
         copy.wait_send()
-    for end, like, number in sent_by_role:
+    for end in (True, False):
 
         @only(end)
         def sent():
-            source = like()
-            pltpu.make_async_copy(source, source, send_sems.at[number]).wait()
+            for role, like, number in sent_by_role:
+                if role == end:
+                    source = like()
+                    pltpu.make_async_copy(source, source, send_sems.at[number]).wait()
 
 
 def finish_kernel(*refs):
-    g_o, g_in0, g_in1, g_out, heads, smalls, rows, output, input_grad = refs[:9]
-    r_q, r_k, r_v, r_o, r_in, r_out = refs[9:15]
-    vectors, inner_bias, loss, r_output, r_input = refs[15:23], *refs[23:]
-    step = pl.program_id(0)
-    for i in range(2):
-        r_o[:, 384 * i : 384 * (i + 1)] = g_o[i].reshape(HW // 2, 384).astype(F32)
-        for j in range(4):
-            first = D * j + 384 * i
-            for k, source in enumerate((g_in0, g_in1)):
-                r_in[48 * k : 48 * (k + 1), first : first + 384] = source[i, 0, j].astype(F32)
-    r_out[...] = g_out[...].reshape(D // 2, D).astype(F32)
-    for i, result in ((0, r_k), (1, r_v), (2, r_q)):
-        result[...] = jnp.concatenate(
-            [heads[0, j, :, HW * i : HW * (i + 1)].astype(F32) for j in range(4)], axis=1
-        )
-    r_output[0] = output[...]
-    r_input[0] = input_grad[...]
-
-    @pl.when(step == 0)
-    def once():
-        w = lax.axis_index("wsh")
-        for i in range(8):
-            vectors[i][...] = smalls[w, i, :]
-        inner_bias[...] = rows[1, w, :]
-        error = jnp.sum(rows[1, 4:5, :])
-        count = jnp.max(rows[1, 5:6, :])
-        loss[0] = error / (count * D)
+    g_o, g_in0, g_in1, g_out, heads, output, input_grad, smalls, rows = refs[:9]
+    r_q, r_k, r_v, r_o, r_in, r_out, r_output, r_input = refs[9:17]
+    vectors, inner_bias, loss = refs[17:25], refs[25], refs[26]
+    low_o, low_in0, low_in1, low_out, low_heads, low_output, full_input = refs[27:34]
+    f_q, f_k, f_v, f_o, f_in, f_out, load_sems, store_sems = refs[34:]
+
+    def load(number, source, target):
+        copy = pltpu.make_async_copy(source, target, load_sems.at[number])
+        copy.start()
+        return copy
+
+    stores = []
+
+    def store(source, target):
+        copy = pltpu.make_async_copy(source, target, store_sems.at[len(stores)])
+        copy.start()
+        stores.append(copy)
+
+    out_loads = [load(i, g_out.at[i], low_out.at[i]) for i in range(4)]
+    in_loads = [load(4, g_in0, low_in0), load(5, g_in1, low_in1)]
+    heads_load = load(6, heads, low_heads)
+    o_load = load(7, g_o, low_o)
+    output_load = load(8, output, low_output)
+    input_load = load(9, input_grad, full_input)
+
+    for i in range(4):
+        out_loads[i].wait()
+        rows_here = pl.ds(HW * i, HW)
+        f_out[rows_here, :] = low_out[i].reshape(HW, D).astype(F32)
+        store(f_out.at[rows_here], r_out.at[rows_here])
+    for copy in in_loads:
+        copy.wait()
+    for z in range(2):
+        for k, source in enumerate((low_in0, low_in1)):
+            first_row = 96 * z + 48 * k
+            for y in range(2):
+                for j in range(4):
+                    first = D * j + 384 * y
+                    f_in[first_row : first_row + 48, first : first + 384] = source[y, z, j].astype(F32)
+        store(f_in.at[pl.ds(96 * z, 96)], r_in.at[pl.ds(96 * z, 96)])
+    heads_load.wait()
+    for i, (made, result) in enumerate(((f_k, r_k), (f_v, r_v), (f_q, r_q))):
+        for z in range(2):
+            made[96 * z : 96 * (z + 1), :] = jnp.concatenate(
+                [low_heads[z, j, :, HW * i : HW * (i + 1)].astype(F32) for j in range(4)], axis=1
+            )
+        store(made, result)
+    o_load.wait()
+    for z in range(2):
+        for i in range(2):
+            f_o[96 * z : 96 * (z + 1), 384 * i : 384 * (i + 1)] = low_o[i, z].astype(F32)
+    store(f_o, r_o)
+    output_load.wait()
+    store(low_output, r_output.at[0])
+    input_load.wait()
+    store(full_input, r_input.at[0])
+
+    w = lax.axis_index("wsh")
+    for i in range(8):
+        vectors[i][...] = smalls[w, i, :]
+    inner_bias[...] = rows[1, w, :]
+    error = jnp.sum(rows[1, 4:5, :])
+    count = jnp.max(rows[1, 5:6, :])
+    loss[0] = error / (count * D)
+    for copy in stores:
+        copy.wait()
 
 
 def fused_body(tokens, teacher, doc_lengths, valid_len, *weights):
@@ -1632,45 +1708,37 @@
         in_bias,
     )
 
-    steps = 2
-    square_out = pl.BlockSpec((HW // steps, D), lambda i: (i, 0))
-    whole = lambda *shape: pl.BlockSpec(shape, lambda i: (0,) * len(shape))
-    by_row = pl.BlockSpec((ROWS // steps, D), lambda i: (i, 0))
+    square_low = pltpu.VMEM((2, 2, 96, 384), BF)
+    side_low = pltpu.VMEM((2, 2, 4, 48, 384), BF)
     results = pl.pallas_call(
         finish_kernel,
-        grid=(steps,),
         out_shape=(full(HW, D),) * 4
-        + (full(HW, FF), full(D, D))
+        + (full(HW, FF), full(D, D), low(1, ROWS, D), full(1, ROWS, D))
         + (full(HW),) * 8
-        + (full(D), full(1), low(1, ROWS, D), full(1, ROWS, D)),
-        in_specs=[
-            pl.BlockSpec((2, 1, 96, 384), lambda i: (0, i, 0, 0)),
-            pl.BlockSpec((2, 1, 4, 48, 384), lambda i: (0, i, 0, 0, 0)),
-            pl.BlockSpec((2, 1, 4, 48, 384), lambda i: (0, i, 0, 0, 0)),
-            pl.BlockSpec((2, 2, 2, 48, D), lambda i: (i, 0, 0, 0, 0)),
-            pl.BlockSpec((1, 4, HW // 2, HEAD_COLS), lambda i: (i, 0, 0, 0)),
-            whole(GROUP, 16, HW),
-            whole(2, 8, D),
-            by_row,
-            by_row,
+        + (full(D), full(1)),
+        in_specs=[hbm] * 7 + [vmem] * 2,
+        out_specs=[hbm] * 8 + [vmem] * 9 + [smem],
+        scratch_shapes=[
+            square_low,
+            side_low,
+            side_low,
+            pltpu.VMEM((4, 2, 2, 48, D), BF),
+            pltpu.VMEM((2, 4, HW // 2, HEAD_COLS), BF),
+            pltpu.VMEM((ROWS, D), BF),
+            pltpu.VMEM((ROWS, D), F32),
+        ]
+        + [pltpu.VMEM((HW, D), F32)] * 4
+        + [
+            pltpu.VMEM((HW, FF), F32),
+            pltpu.VMEM((D, D), F32),
+            pltpu.SemaphoreType.DMA((10,)),
+            pltpu.SemaphoreType.DMA((12,)),
         ],
-        out_specs=[square_out] * 4
-        + [
-            pl.BlockSpec((HW // steps, FF), lambda i: (i, 0)),
-            pl.BlockSpec((D // steps, D), lambda i: (i, 0)),
-        ]
-        + [whole(HW)] * 8
-        + [
-            whole(D),
-            pl.BlockSpec(memory_space=pltpu.SMEM),
-            pl.BlockSpec((1, ROWS // steps, D), lambda i: (0, i, 0)),
-            pl.BlockSpec((1, ROWS // steps, D), lambda i: (0, i, 0)),
-        ],
-        compiler_params=pltpu.CompilerParams(dimension_semantics=("arbitrary",)),
         name="finish",
-    )(g_o, g_in0, g_in1, g_out, heads, smalls, rows, output, input_grad)
+    )(g_o, g_in0, g_in1, g_out, heads, output, input_grad, smalls, rows)
+    r_output, r_input = results[6:8]
+    vectors, inner_bias, loss = results[8:16], *results[16:]
     r_q, r_k, r_v, r_o, r_in, r_out = results[:6]
-    vectors, inner_bias, loss, r_output, r_input = results[6:14], *results[14:]
     return (
         r_output,
         loss.reshape(()),

time: 156 us -> 150 us (0.962)
  Pallas kernels: 155 us -> 148 us
    pallas_call x1, Pallas kernels: 149 us -> 142 us  [fused_body(): pl.pallas_call(fused_kernel, out_shape=(low(ROWS, D), full(ROWS, D), low(...]
where the time goes in v5:
time: 150 us
  Pallas kernels  148 us (99%)
    pallas_call x1, Pallas kernels, fused_body(): pl.pallas_call(fused_kernel, out_shape=(low(ROWS, D), full(ROWS, D), low(...  142 us
    pallas_call x1, Pallas kernels, fused_body(): pl.pallas_call(finish_kernel, out_shape=(full(HW, D),) * 4 + (full(HW, FF...  5.74 us

profile of v5, /device:TPU:0, one launch (start us, length us, event | category | flops | bytes accessed | tf_op | source)
XLA Modules:
  0.0 149.6 jit_solution(16859905369750047493)
XLA Ops:
  1.3 142.3 %layer.1 = (bf16[128,768]{1,0:T(8,128)(2,1)}, f32[128,768]{1,0:T(8,128)}, bf16[2,2,96,384]{3,2,1,0:T(8,128)(2,1)}, bf16[2,2,4,48,384]{4,3,2,1,0:T(8,128)(2,1)}, ...) custom-call(bf16[1,128,768]{2,1,0:T(8,128)(2,1)} %refs_0_.1, ...), custom_call_target="tpu_custom_call" | custom-call | tf_op jit(solution)/shard_map/layer/pallas_call | solution.py:1664
  143.7 5.7 %finish.1 = (f32[192,768]{1,0:T(8,128)}, f32[192,768]{1,0:T(8,128)}, f32[192,768]{1,0:T(8,128)}, f32[192,768]{1,0:T(8,128)}, f32[192,3072]{1,0:T(8,128)}, /*inde...) custom-call(bf16[2,2,96,384]{3,2,1,0:T(8,128)(2,1)} %get-tuple-eleme, ...), custom_call_target="tpu_custom_call" | custom-call | tf_op jit(solution)/shard_map/finish/pallas_call | solution.py:1713

commit v6 on v5

--- a/solution.py
+++ b/solution.py
@@ -406,7 +406,7 @@
 SECOND_WAY = {O: 1, IN: 2, OUT: 1, PART_Q: 1, PART_K: 1, PART_V: 1}
 LOT_O, LOT_IN, LOT_OUT = (0,), (1, 2), (3, 4, 5, 6)
 LOT_PAIR = LOT_O + LOT_IN + LOT_OUT[:2]
-LOTS = [(96, 384)] + [(4, 48, 384)] * 2 + [(48, D)] * 4
+LOTS = [(96, 384)] + [(4, 48, 384)] * 2 + [(96, 384)] * 4
 PIECES = {IN: (1, 4), OUT: (4, 1)}
 HEAD_COLS = 640
 
@@ -518,13 +518,13 @@
     s.inverse = pltpu.VMEM((ROWS, 128), F32)
     s.set_low = pltpu.VMEM((ROWS, D), BF)
     s.ag_half = pltpu.VMEM((2, ROWS, 384), BF)
-    s.bg = pltpu.VMEM((ROWS, D), BF)
+    s.bg = pltpu.VMEM((2, ROWS, 384), BF)
     s.set_all = pltpu.VMEM((GROUP, ROWS, D), BF)
     s.ctx_all = pltpu.VMEM((GROUP, 2, HW, ROWS), BF)
     s.ag_all = pltpu.VMEM((GROUP, ROWS, 384), BF)
     s.inner_all = pltpu.VMEM((GROUP * ROWS, D), F32)
     s.act_all = pltpu.VMEM((GROUP * ROWS, D), BF)
-    s.bg_all = pltpu.VMEM((GROUP, ROWS, D), BF)
+    s.bg_all = pltpu.VMEM((2, GROUP, ROWS, 384), BF)
     s.cg_send = pltpu.VMEM((4, HW, ROWS), BF)
     s.cg = pltpu.VMEM((4, HW, ROWS), BF)
     s.wg = pltpu.VMEM((HEADS, HD, 4 * ROWS), BF)
@@ -798,16 +798,16 @@
 
     def to_near(key, source, everywhere):
         for j in (1, 2):
-            remote((key, j), source, everywhere.at[w], 0, j)
+            remote((*key, j), source, everywhere.at[w], 0, j)
 
     def pass_to_core(key, everywhere):
         slot = everywhere.at[bit_xor(w, 2)]
-        arrived((key, 2), slot)
-        remote((key, 3), slot, slot, 0, 1)
+        arrived((*key, 2), slot)
+        remote((*key, 3), slot, slot, 0, 1)
 
     def from_near(key, everywhere):
         for j in (1, 3):
-            arrived((key, j), everywhere.at[bit_xor(w, j)])
+            arrived((*key, j), everywhere.at[bit_xor(w, j)])
 
     def lanes(parts):
         return jnp.concatenate(parts, axis=1)
@@ -920,13 +920,13 @@
         S.inverse[...] = jnp.broadcast_to(inverse_one, (ROWS, 128))
         S.keep[...] = settled
         S.set_low[...] = settled.astype(BF)
-        to_near(SETTLED_ALL, S.set_low, S.set_all)
+        to_near((SETTLED_ALL,), S.set_low, S.set_all)
         S.set_all[w] = S.set_low[...]
         to_group((CONTEXT_ALL,), lambda to: S.ctx.at[pl.ds(2 * (to // 2), 2)], S.ctx_all)
         S.ctx_all[w] = S.ctx[pl.ds(2 * x, 2)]
 
     def pass_settled():
-        pass_to_core(SETTLED_ALL, S.set_all)
+        pass_to_core((SETTLED_ALL,), S.set_all)
 
     def gelu(inner):
         return 0.5 * inner * (1.0 + jnp.tanh(GELU_C * (inner + 0.044715 * inner * inner * inner)))
@@ -962,29 +962,32 @@
         count = vector(12)
         upstream = diff * ((ROWS * CTX * GROUP) / count)
         d_second = norm_back(upstream * vector(6), normal_two, inverse_two)
-        S.bg[...] = d_second.astype(BF)
-        to_near(BRANCH_GRAD_ALL, S.bg, S.bg_all)
-        S.bg_all[w] = S.bg[...]
+        for i in range(2):
+            S.bg[i] = d_second[:, 384 * i : 384 * (i + 1)].astype(BF)
+            to_near((BRANCH_GRAD_ALL, i), S.bg.at[i], S.bg_all.at[i])
+        for i in range(2):
+            S.bg_all[i, w] = S.bg[i]
         S.keep[...] = d_second
         S.sg[...] = jnp.zeros((16, D), F32)
         note(12, diff * diff)
         S.sg[13:14, :] = count * (1.0 / (CTX * GROUP))
         note(6, upstream * normal_two)
         note(7, upstream)
-        note(5, S.bg[...])
+        note(5, d_second.astype(BF))
 
     def feed_back():
         d_settled = S.keep[...]
+        branch_grad = lanes([S.bg[0], S.bg[1]])
         for t in range(4):
-            d_act = right_product(S.bg[...], S.full[OUT][t])
+            d_act = right_product(branch_grad, S.full[OUT][t])
             inner_grad = (d_act * gelu_slope(S.inner[t])).astype(BF)
             note(8 + t, inner_grad)
             w_part = S.full[IN][:, :, D * t : D * (t + 1)].reshape(D, D)
             d_settled = d_settled + right_product(inner_grad, w_part)
         S.keep[...] = d_settled
 
-    def pass_branch_grad():
-        pass_to_core(BRANCH_GRAD_ALL, S.bg_all)
+    def pass_branch_grad(i):
+        pass_to_core((BRANCH_GRAD_ALL, i), S.bg_all.at[i])
 
     def first_norm_back():
         d_settled, normal_one = S.keep[...], S.first[...]
@@ -1063,7 +1066,7 @@
             remote((SPREAD, lot, 1), done, done, 2, 0, like=lambda: S.done[lot].at[0])
 
     def result_of(lot):
-        return grad_in[lot - LOT_IN[0]] if lot in LOT_IN else grad_out.at[lot - LOT_OUT[0]]
+        return grad_in[lot - LOT_IN[0]] if lot in LOT_IN else grad_out.at[(lot - LOT_OUT[0]) // 2, (lot - LOT_OUT[0]) % 2]
 
     def y_give(lot):
         done = S.done[lot].at[b]
@@ -1171,10 +1174,10 @@
         def from_pair():
             arrived((SPREAD, lot, 3), S.done[lot].at[:, 1 - b])
 
-        finishing.append(local((GIVE, lot), S.done[lot], grad_out.at[lot - LOT_OUT[0]]))
+        finishing.append(local((GIVE, lot), S.done[lot], grad_out.at[(lot - LOT_OUT[0]) // 2, (lot - LOT_OUT[0]) % 2]))
 
     def inner_again():
-        from_near(SETTLED_ALL, S.set_all)
+        from_near((SETTLED_ALL,), S.set_all)
         settled_all = S.set_all[...].reshape(GROUP * ROWS, D)
         hidden = pl.ds(pl.multiple_of(D * w, D), D)
         S.inner_all[...] = (
@@ -1183,18 +1186,19 @@
         )
         S.act_all[...] = gelu(S.inner_all[...]).astype(BF)
 
-    def out_part():
-        from_near(BRANCH_GRAD_ALL, S.bg_all)
-        grad = tn(S.act_all[...], S.bg_all[...].reshape(GROUP * ROWS, D)).astype(BF)
-        for i, lot in enumerate(LOT_OUT):
-            S.part[lot][...] = grad[HW * i : HW * (i + 1)].reshape(2, 2, 48, D)
+    def out_part(i):
+        from_near((BRANCH_GRAD_ALL, i), S.bg_all.at[i])
+        grad = tn(S.act_all[...], S.bg_all[i].reshape(GROUP * ROWS, 384)).astype(BF)
+        for k in range(2):
+            lot = LOT_OUT[2 * i + k]
+            S.part[lot][...] = grad[384 * k : 384 * (k + 1)].reshape(2, 2, 96, 384)
             if lot in LOT_PAIR:
                 remote((REDUCE, lot, 0), S.part[lot].at[1 - b], S.got[lot][0], 1, 0)
             else:
                 reduce_start(lot)
 
     def in_part():
-        branch_grad_all = S.bg_all[...].reshape(GROUP * ROWS, D)
+        branch_grad_all = lanes([S.bg_all[i].reshape(GROUP * ROWS, 384) for i in range(2)])
         inner_grad_all = (
             right_product(branch_grad_all, S.full[OUT][w]) * gelu_slope(S.inner_all[...])
         ).astype(BF)
@@ -1432,6 +1436,12 @@
         for copy in marked:
             copy.wait_send()
         marked.clear()
+
+    def mark_late():
+        mark()
+
+    def retire_late():
+        retire()
 
     for step, *lot in (
         (pass_near_end,),
@@ -1484,8 +1494,10 @@
         (first_norm_back,),
         (mark,),
         (inner_again,),
-        (pass_branch_grad,),
-        (out_part,),
+        (pass_branch_grad, 0),
+        (pass_branch_grad, 1),
+        (out_part, 0),
+        (out_part, 1),
         (attention_back,),
         (reduce_middle, 5),
         (reduce_pair, 5),
@@ -1520,6 +1532,7 @@
         (vectors_end,),
         (y_spread_end, 0),
         (heads_line,),
+        (mark_late,),
         (y_end, 2),
         (reduce_last, 6),
         (y_give, 3),
@@ -1548,6 +1561,7 @@
         (finish_lot, 5),
         (input_end,),
         (input_done,),
+        (retire_late,),
         (vectors_done,),
         (finish_lot, 6),
     ):
@@ -1570,72 +1584,34 @@
 
 
 def finish_kernel(*refs):
-    g_o, g_in0, g_in1, g_out, heads, output, input_grad, smalls, rows = refs[:9]
-    r_q, r_k, r_v, r_o, r_in, r_out, r_output, r_input = refs[9:17]
-    vectors, inner_bias, loss = refs[17:25], refs[25], refs[26]
-    low_o, low_in0, low_in1, low_out, low_heads, low_output, full_input = refs[27:34]
-    f_q, f_k, f_v, f_o, f_in, f_out, load_sems, store_sems = refs[34:]
-
-    def load(number, source, target):
-        copy = pltpu.make_async_copy(source, target, load_sems.at[number])
-        copy.start()
-        return copy
-
-    stores = []
-
-    def store(source, target):
-        copy = pltpu.make_async_copy(source, target, store_sems.at[len(stores)])
-        copy.start()
-        stores.append(copy)
-
-    out_loads = [load(i, g_out.at[i], low_out.at[i]) for i in range(4)]
-    in_loads = [load(4, g_in0, low_in0), load(5, g_in1, low_in1)]
-    heads_load = load(6, heads, low_heads)
-    o_load = load(7, g_o, low_o)
-    output_load = load(8, output, low_output)
-    input_load = load(9, input_grad, full_input)
-
-    for i in range(4):
-        out_loads[i].wait()
-        rows_here = pl.ds(HW * i, HW)
-        f_out[rows_here, :] = low_out[i].reshape(HW, D).astype(F32)
-        store(f_out.at[rows_here], r_out.at[rows_here])
-    for copy in in_loads:
-        copy.wait()
-    for z in range(2):
-        for k, source in enumerate((low_in0, low_in1)):
-            first_row = 96 * z + 48 * k
-            for y in range(2):
-                for j in range(4):
-                    first = D * j + 384 * y
-                    f_in[first_row : first_row + 48, first : first + 384] = source[y, z, j].astype(F32)
-        store(f_in.at[pl.ds(96 * z, 96)], r_in.at[pl.ds(96 * z, 96)])
-    heads_load.wait()
-    for i, (made, result) in enumerate(((f_k, r_k), (f_v, r_v), (f_q, r_q))):
-        for z in range(2):
-            made[96 * z : 96 * (z + 1), :] = jnp.concatenate(
-                [low_heads[z, j, :, HW * i : HW * (i + 1)].astype(F32) for j in range(4)], axis=1
-            )
-        store(made, result)
-    o_load.wait()
-    for z in range(2):
-        for i in range(2):
-            f_o[96 * z : 96 * (z + 1), 384 * i : 384 * (i + 1)] = low_o[i, z].astype(F32)
-    store(f_o, r_o)
-    output_load.wait()
-    store(low_output, r_output.at[0])
-    input_load.wait()
-    store(full_input, r_input.at[0])
-
-    w = lax.axis_index("wsh")
-    for i in range(8):
-        vectors[i][...] = smalls[w, i, :]
-    inner_bias[...] = rows[1, w, :]
-    error = jnp.sum(rows[1, 4:5, :])
-    count = jnp.max(rows[1, 5:6, :])
-    loss[0] = error / (count * D)
-    for copy in stores:
-        copy.wait()
+    g_o, g_in0, g_in1, g_out, heads, smalls, rows, output, input_grad = refs[:9]
+    r_q, r_k, r_v, r_o, r_in, r_out = refs[9:15]
+    vectors, inner_bias, loss, r_output, r_input = refs[15:23], *refs[23:]
+    step = pl.program_id(0)
+    for i in range(2):
+        r_o[:, 384 * i : 384 * (i + 1)] = g_o[i].reshape(HW // 2, 384).astype(F32)
+        for j in range(4):
+            first = D * j + 384 * i
+            for k, source in enumerate((g_in0, g_in1)):
+                r_in[48 * k : 48 * (k + 1), first : first + 384] = source[i, 0, j].astype(F32)
+    for i in range(2):
+        r_out[:, 384 * i : 384 * (i + 1)] = g_out[i].reshape(D // 2, 384).astype(F32)
+    for i, result in ((0, r_k), (1, r_v), (2, r_q)):
+        result[...] = jnp.concatenate(
+            [heads[0, j, :, HW * i : HW * (i + 1)].astype(F32) for j in range(4)], axis=1
+        )
+    r_output[0] = output[...]
+    r_input[0] = input_grad[...]
+
+    @pl.when(step == 0)
+    def once():
+        w = lax.axis_index("wsh")
+        for i in range(8):
+            vectors[i][...] = smalls[w, i, :]
+        inner_bias[...] = rows[1, w, :]
+        error = jnp.sum(rows[1, 4:5, :])
+        count = jnp.max(rows[1, 5:6, :])
+        loss[0] = error / (count * D)
 
 
 def fused_body(tokens, teacher, doc_lengths, valid_len, *weights):
@@ -1669,7 +1645,7 @@
             low(2, 2, 96, 384),
             low(2, 2, 4, 48, 384),
             low(2, 2, 4, 48, 384),
-            low(4, 2, 2, 48, D),
+            low(2, 2, 2, 2, 96, 384),
             low(2, 4, HW // 2, HEAD_COLS),
             full(GROUP, 16, HW),
             full(2, 8, D),
@@ -1708,37 +1684,45 @@
         in_bias,
     )
 
-    square_low = pltpu.VMEM((2, 2, 96, 384), BF)
-    side_low = pltpu.VMEM((2, 2, 4, 48, 384), BF)
+    steps = 2
+    square_out = pl.BlockSpec((HW // steps, D), lambda i: (i, 0))
+    whole = lambda *shape: pl.BlockSpec(shape, lambda i: (0,) * len(shape))
+    by_row = pl.BlockSpec((ROWS // steps, D), lambda i: (i, 0))
     results = pl.pallas_call(
         finish_kernel,
+        grid=(steps,),
         out_shape=(full(HW, D),) * 4
-        + (full(HW, FF), full(D, D), low(1, ROWS, D), full(1, ROWS, D))
+        + (full(HW, FF), full(D, D))
         + (full(HW),) * 8
-        + (full(D), full(1)),
-        in_specs=[hbm] * 7 + [vmem] * 2,
-        out_specs=[hbm] * 8 + [vmem] * 9 + [smem],
-        scratch_shapes=[
-            square_low,
-            side_low,
-            side_low,
-            pltpu.VMEM((4, 2, 2, 48, D), BF),
-            pltpu.VMEM((2, 4, HW // 2, HEAD_COLS), BF),
-            pltpu.VMEM((ROWS, D), BF),
-            pltpu.VMEM((ROWS, D), F32),
+        + (full(D), full(1), low(1, ROWS, D), full(1, ROWS, D)),
+        in_specs=[
+            pl.BlockSpec((2, 1, 96, 384), lambda i: (0, i, 0, 0)),
+            pl.BlockSpec((2, 1, 4, 48, 384), lambda i: (0, i, 0, 0, 0)),
+            pl.BlockSpec((2, 1, 4, 48, 384), lambda i: (0, i, 0, 0, 0)),
+            pl.BlockSpec((2, 1, 2, 2, 96, 384), lambda i: (0, i, 0, 0, 0, 0)),
+            pl.BlockSpec((1, 4, HW // 2, HEAD_COLS), lambda i: (i, 0, 0, 0)),
+            whole(GROUP, 16, HW),
+            whole(2, 8, D),
+            by_row,
+            by_row,
+        ],
+        out_specs=[square_out] * 4
+        + [
+            pl.BlockSpec((HW // steps, FF), lambda i: (i, 0)),
+            pl.BlockSpec((D // steps, D), lambda i: (i, 0)),
         ]
-        + [pltpu.VMEM((HW, D), F32)] * 4
+        + [whole(HW)] * 8
         + [
-            pltpu.VMEM((HW, FF), F32),
-            pltpu.VMEM((D, D), F32),
-            pltpu.SemaphoreType.DMA((10,)),
-            pltpu.SemaphoreType.DMA((12,)),
+            whole(D),
+            pl.BlockSpec(memory_space=pltpu.SMEM),
+            pl.BlockSpec((1, ROWS // steps, D), lambda i: (0, i, 0)),
+            pl.BlockSpec((1, ROWS // steps, D), lambda i: (0, i, 0)),
         ],
+        compiler_params=pltpu.CompilerParams(dimension_semantics=("arbitrary",)),
         name="finish",
-    )(g_o, g_in0, g_in1, g_out, heads, output, input_grad, smalls, rows)
-    r_output, r_input = results[6:8]
-    vectors, inner_bias, loss = results[8:16], *results[16:]
+    )(g_o, g_in0, g_in1, g_out, heads, smalls, rows, output, input_grad)
     r_q, r_k, r_v, r_o, r_in, r_out = results[:6]
+    vectors, inner_bias, loss, r_output, r_input = results[6:14], *results[14:]
     return (
         r_output,
         loss.reshape(()),

time: 150 us -> 148 us (0.987)
  Pallas kernels: 148 us -> 146 us
where the time goes in v6:
time: 148 us
  Pallas kernels  146 us (99%)
    pallas_call x1, Pallas kernels, fused_body(): pl.pallas_call(fused_kernel, out_shape=(low(ROWS, D), full(ROWS, D), low(...  141 us
    pallas_call x1, Pallas kernels, fused_body(): pl.pallas_call(finish_kernel, grid=(steps,), out_shape=(full(HW, D),) * 4...  5.17 us

profile of v6, /device:TPU:0, one launch (start us, length us, event | category | flops | bytes accessed | tf_op | source)
XLA Modules:
  0.0 147.7 jit_solution(11822205729846256658)
XLA Ops:
  1.3 141.1 %layer.1 = (bf16[128,768]{1,0:T(8,128)(2,1)}, f32[128,768]{1,0:T(8,128)}, bf16[2,2,96,384]{3,2,1,0:T(8,128)(2,1)}, bf16[2,2,4,48,384]{4,3,2,1,0:T(8,128)(2,1)}, ...) custom-call(bf16[1,128,768]{2,1,0:T(8,128)(2,1)} %refs_0_.1, ...), custom_call_target="tpu_custom_call" | custom-call | tf_op jit(solution)/shard_map/layer/pallas_call | solution.py:1640
  142.4 5.2 %finish.1 = (f32[192,768]{1,0:T(8,128)}, f32[192,768]{1,0:T(8,128)}, f32[192,768]{1,0:T(8,128)}, f32[192,768]{1,0:T(8,128)}, f32[192,3072]{1,0:T(8,128)}, /*inde...) custom-call(bf16[2,2,96,384]{3,2,1,0:T(8,128)(2,1)} %get-tuple-eleme, ...), custom_call_target="tpu_custom_call" | custom-call | tf_op jit(solution)/shard_map/finish/pallas_call | solution.py:1691

commit v7 on v6

--- a/solution.py
+++ b/solution.py
@@ -671,6 +671,39 @@
         pl.semaphore_signal(
             barrier, inc=1, device_id={"ctx": c_to, "wsh": w_to}, device_id_type=MESH
         )
+    pl.semaphore_wait(barrier, len(peers))
+
+    def mine(name):
+        return bit(c, SECOND_WAY[name])
+
+    def pieces(name):
+        tall, across = PIECES.get(name, (1, 1))
+        return range(tall * across)
+
+    def piece(name, which, number):
+        rows, cols = WEIGHT_SHAPES[name]
+        tall, across = PIECES.get(name, (1, 1))
+        high, broad = rows // 2 // tall, cols // across
+        row = which * (rows // 2) + number // across * high
+        return pl.ds(pl.multiple_of(row, 16), high), slice(
+            number % across * broad, (number % across + 1) * broad
+        )
+
+    def send_core(name):
+        remote((WEIGHT_CORE, name), shard(name), S.full[name].at[w], 0, 1)
+
+    def send_x(name):
+        for i in pieces(name):
+            rows, cols = piece(name, mine(name), i)
+            if name < PART_Q:
+                source = shards[name].at[rows, cols]
+            else:
+                source = shards[name - PART_Q].at[rows, pl.ds(first_col, SLICE)]
+            remote((WEIGHT_X, name, i), source, S.full[name].at[w, rows, cols], 0, 2)
+
+    for name in (PART_K, PART_V, PART_Q):
+        send_x(name)
+        send_core(name)
     loads[TOKENS].wait()
     x_low = S.x[...]
     S.xt[c] = x_low.T
@@ -686,39 +719,6 @@
     ).astype(BF)
     S.small[w, 8:16, HW:D] = jnp.concatenate(wide_rows, axis=0)[:, HW:D].astype(BF)
 
-    pl.semaphore_wait(barrier, len(peers))
-
-    def mine(name):
-        return bit(c, SECOND_WAY[name])
-
-    def pieces(name):
-        tall, across = PIECES.get(name, (1, 1))
-        return range(tall * across)
-
-    def piece(name, which, number):
-        rows, cols = WEIGHT_SHAPES[name]
-        tall, across = PIECES.get(name, (1, 1))
-        high, broad = rows // 2 // tall, cols // across
-        row = which * (rows // 2) + number // across * high
-        return pl.ds(pl.multiple_of(row, 16), high), slice(
-            number % across * broad, (number % across + 1) * broad
-        )
-
-    def send_core(name):
-        remote((WEIGHT_CORE, name), shard(name), S.full[name].at[w], 0, 1)
-
-    def send_x(name):
-        for i in pieces(name):
-            rows, cols = piece(name, mine(name), i)
-            if name < PART_Q:
-                source = shards[name].at[rows, cols]
-            else:
-                source = shards[name - PART_Q].at[rows, pl.ds(first_col, SLICE)]
-            remote((WEIGHT_X, name, i), source, S.full[name].at[w, rows, cols], 0, 2)
-
-    for name in (PART_K, PART_V, PART_Q):
-        send_x(name)
-        send_core(name)
     for j in (1, 2, 3):
         remote((SMALL, j), S.small.at[w], S.small.at[w], 0, j)
     remote((X_LINE, 1), S.xt.at[c], S.xt.at[c], 2, 0)

time: 148 us -> 148 us (level)
  no operation moved by 1% of the time
where the time goes in v7:
time: 148 us; the launch traced here: 147 us
  Pallas kernels  146 us (99%)
    pallas_call x1, Pallas kernels, fused_body(): pl.pallas_call(fused_kernel, out_shape=(low(ROWS, D), full(ROWS, D), low(...  141 us
    pallas_call x1, Pallas kernels, fused_body(): pl.pallas_call(finish_kernel, grid=(steps,), out_shape=(full(HW, D),) * 4...  5.17 us

profile of v7, /device:TPU:0, one launch (start us, length us, event | category | flops | bytes accessed | tf_op | source)
XLA Modules:
  0.0 147.4 jit_solution(14789966004981356500)
XLA Ops:
  1.3 140.8 %layer.1 = (bf16[128,768]{1,0:T(8,128)(2,1)}, f32[128,768]{1,0:T(8,128)}, bf16[2,2,96,384]{3,2,1,0:T(8,128)(2,1)}, bf16[2,2,4,48,384]{4,3,2,1,0:T(8,128)(2,1)}, ...) custom-call(bf16[1,128,768]{2,1,0:T(8,128)(2,1)} %refs_0_.1, ...), custom_call_target="tpu_custom_call" | custom-call | tf_op jit(solution)/shard_map/layer/pallas_call | solution.py:1640
  142.1 5.2 %finish.1 = (f32[192,768]{1,0:T(8,128)}, f32[192,768]{1,0:T(8,128)}, f32[192,768]{1,0:T(8,128)}, f32[192,768]{1,0:T(8,128)}, f32[192,3072]{1,0:T(8,128)}, /*inde...) custom-call(bf16[2,2,96,384]{3,2,1,0:T(8,128)(2,1)} %get-tuple-eleme, ...), custom_call_target="tpu_custom_call" | custom-call | tf_op jit(solution)/shard_map/finish/pallas_call | solution.py:1691

commit v8 on v7

--- a/solution.py
+++ b/solution.py
@@ -707,6 +707,12 @@
     loads[TOKENS].wait()
     x_low = S.x[...]
     S.xt[c] = x_low.T
+    remote((X_LINE, 1), S.xt.at[c], S.xt.at[c], 2, 0)
+
+    @only(False)
+    def x_to_middle():
+        remote((X_LINE, 3), S.xt.at[c], S.xt.at[c], 6, 0, like=lambda: S.xt.at[0])
+
     bias_rows = [row[...].astype(F32).reshape(1, HW) for row in biases[:8]]
     tall = jnp.concatenate(bias_rows, axis=0)
     valid_high = (valid[0] // 64).astype(F32)
@@ -721,12 +727,6 @@
 
     for j in (1, 2, 3):
         remote((SMALL, j), S.small.at[w], S.small.at[w], 0, j)
-    remote((X_LINE, 1), S.xt.at[c], S.xt.at[c], 2, 0)
-
-    @only(False)
-    def x_to_middle():
-        remote((X_LINE, 3), S.xt.at[c], S.xt.at[c], 6, 0, like=lambda: S.xt.at[0])
-
     for name in (O, IN, OUT):
         send_x(name)
         send_core(name)

time: 148 us -> 148 us (level)
  no operation moved by 1% of the time
where the time goes in v8:
time: 148 us; the launch traced here: 147 us
  Pallas kernels  146 us (99%)
    pallas_call x1, Pallas kernels, fused_body(): pl.pallas_call(fused_kernel, out_shape=(low(ROWS, D), full(ROWS, D), low(...  141 us
    pallas_call x1, Pallas kernels, fused_body(): pl.pallas_call(finish_kernel, grid=(steps,), out_shape=(full(HW, D),) * 4...  5.17 us

profile of v8, /device:TPU:0, one launch (start us, length us, event | category | flops | bytes accessed | tf_op | source)
XLA Modules:
  0.0 147.4 jit_solution(17868757471353821667)
XLA Ops:
  1.3 140.8 %layer.1 = (bf16[128,768]{1,0:T(8,128)(2,1)}, f32[128,768]{1,0:T(8,128)}, bf16[2,2,96,384]{3,2,1,0:T(8,128)(2,1)}, bf16[2,2,4,48,384]{4,3,2,1,0:T(8,128)(2,1)}, ...) custom-call(bf16[1,128,768]{2,1,0:T(8,128)(2,1)} %refs_0_.1, ...), custom_call_target="tpu_custom_call" | custom-call | tf_op jit(solution)/shard_map/layer/pallas_call | solution.py:1640
  142.1 5.2 %finish.1 = (f32[192,768]{1,0:T(8,128)}, f32[192,768]{1,0:T(8,128)}, f32[192,768]{1,0:T(8,128)}, f32[192,768]{1,0:T(8,128)}, f32[192,3072]{1,0:T(8,128)}, /*inde...) custom-call(bf16[2,2,96,384]{3,2,1,0:T(8,128)(2,1)} %get-tuple-eleme, ...), custom_call_target="tpu_custom_call" | custom-call | tf_op jit(solution)/shard_map/finish/pallas_call | solution.py:1691
